TPU v7x, 32 devices: a whole 2x2x4 slice. The times are simulated.
32 devices in a mesh: rows: 8 (over y, x, core), cols: 4 (over z).
Axes of the slice: x: 2, y: 2, z: 4, core: 2. Of those that a mesh axis runs over, the one named last changes fastest.
Arguments:
- terminal_value: float32 [1024, 2048], P('rows', 'cols'), may hold values from -6 to 6
- density_start: float32 [1024, 2048], P('rows', 'cols'), may hold values from 0.2 to 3
- start_cells: int32 [131072], P(('rows', 'cols')), may hold values from 0 to 65535
- offsets: float32 [2, 131072], P(None, ('rows', 'cols')), may hold values from -4 to 4
- weights: float32 [131072], P(('rows', 'cols')), may hold values from 0.3 to 9
- dest_tiles: int32 [1024], P(('rows', 'cols')), may hold values from 0 to 31, as said below
- end_cells: int32 [131072], P(('rows', 'cols')), may hold values from 0 to 65535
Outputs:
- value: float32 [1024, 2048], P('rows', 'cols')
- density: float32 [1024, 2048], P('rows', 'cols')
Inputs may be any that keep to these rules, and one draw needn't show every extreme that they name: `dest_tiles`: block b's tile lies in the band of the tile where b starts or in a band next to it. At most 8 blocks that start in one tile go to any one tile, and for every starting tile there is one destination tile that receives exactly 8 of its blocks.
All inputs are finite; a program needn't handle non-finite values.
Results may differ from a plain program's by a relative error of at most 0.0003.
Values sent between devices are 32-bit elements; how exact they have to be, the bound alone decides.
No kernel may reach another device: no remote copies, remote signals or barrier semaphores. Data moves between devices by JAX's collectives and lax.ppermute only.
A program may use at most 64 MiB of HBM per device.

v0:
```python
import functools
import jax
import jax.numpy as jnp
from jax import lax
from jax.experimental import pallas as pl
from jax.experimental.pallas import tpu as pltpu
from jax.sharding import PartitionSpec as P

HJB_STEPS = 4
ITERS = 2
F32, BF16, I32 = jnp.float32, jnp.bfloat16, jnp.int32

PAD = 16
EDGE = 8
GROUP = 4
UNROLL = 4
VMEM_LIMIT = 24 * 1024 * 1024


def swap_pairs(count):
    first = [(i, i ^ 1) for i in range(count)]
    second = [(i, ((i + 1) ^ 1) - 1) for i in range(1, count - 1)]
    return first, second


def swap_both(first, second, axis):
    pairs_a, pairs_b = swap_pairs(lax.axis_size(axis))
    return lax.ppermute(first, axis, pairs_a), lax.ppermute(second, axis, pairs_b)


def xor_permute(value, axis, bit):
    return lax.ppermute(value, axis, [(i, i ^ bit) for i in range(lax.axis_size(axis))])


def vmem_call(kernel, out_shape, n_in, scratch=(), hbm_in=(), hbm_out=(), keep=()):
    def spec(in_hbm):
        return pl.BlockSpec(memory_space=pltpu.HBM if in_hbm else pltpu.VMEM)

    results = [
        leaf if i in keep or i in hbm_out else pltpu.VMEM(leaf.shape, leaf.dtype)
        for i, leaf in enumerate(out_shape)
    ]
    call = pl.pallas_call(
        kernel,
        out_shape=results,
        in_specs=[spec(i in hbm_in) for i in range(n_in)],
        out_specs=[spec(i in hbm_out) for i in range(len(results))],
        scratch_shapes=list(scratch),
        compiler_params=pltpu.CompilerParams(vmem_limit_bytes=VMEM_LIMIT),
    )

    def run(*operands):
        return call(
            *[
                pltpu.with_memory_space_constraint(x, pltpu.HBM if i in hbm_in else pltpu.VMEM)
                for i, x in enumerate(operands)
            ]
        )

    return run


def shape(*dims, dtype=F32):
    return jax.ShapeDtypeStruct(dims, dtype)


def flipped(block):
    rows = block.shape[0]
    width = -(-rows // 128) * 128
    if width > rows:
        block = jnp.concatenate([block, jnp.zeros((width - rows, 128), F32)], axis=0)
    parts = [block[i : i + 128].T for i in range(0, width, 128)]
    return jnp.concatenate(parts, axis=1)


def unflipped(block, rows):
    parts = [block[:, i : i + 128].T for i in range(0, block.shape[1], 128)]
    return jnp.concatenate(parts, axis=0)[:rows]


def row_col(cell, cols):
    if cols & (cols - 1) == 0:
        return cell >> (cols.bit_length() - 1), cell & (cols - 1)
    return cell // cols, cell % cols


def pick(flag, one, other):
    return jnp.where(flag, one, other)


def start_kernel(rows, count, *refs):
    sources, copies = refs[:count], refs[count : 2 * count]
    sa_ref, sb_ref, sum_ref, sems = refs[2 * count :]
    moves = [
        pltpu.make_async_copy(src, dst, sems.at[i])
        for i, (src, dst) in enumerate(zip(sources, copies))
    ]
    for move in moves:
        move.start()
    for move in moves:
        move.wait()
    u_ref, m_ref, wts = copies[:3]
    row_even = lax.axis_index("rows") % 2 == 0
    for index, ref in enumerate((u_ref, m_ref)):
        part = slice(index * EDGE, (index + 1) * EDGE)
        south_going, north_going = ref[rows - EDGE : rows, :], ref[0:EDGE, :]
        sa_ref[part, :] = pick(row_even, south_going, north_going)
        sb_ref[part, :] = pick(row_even, north_going, south_going)
    total = jnp.sum(jnp.sum(wts[...], axis=0, keepdims=True), axis=1, keepdims=True)
    sum_ref[...] = jnp.broadcast_to(total, sum_ref.shape)


def start_mid_kernel(
    rows, cols, u_ref, m_ref, a_ref, b_ref, w_ref, v_ref, ue_ref, me_ref, ca_ref, cb_ref, sum_ref
):
    sum_ref[...] = w_ref[...] + v_ref[...]
    row_even = lax.axis_index("rows") % 2 == 0
    col_even = lax.axis_index("cols") % 2 == 0
    for index, (src, dst) in enumerate(((u_ref, ue_ref), (m_ref, me_ref))):
        dst[...] = jnp.zeros(dst.shape, F32)
        dst[PAD : PAD + rows, 0:cols] = src[...]
        part = slice(index * EDGE, (index + 1) * EDGE)
        north = pick(row_even, b_ref[part, :], a_ref[part, :])
        south = pick(row_even, a_ref[part, :], b_ref[part, :])
        dst[PAD - EDGE : PAD, 0:cols] = north
        dst[PAD + rows : PAD + rows + EDGE, 0:cols] = south
        west_going = flipped(dst[:, 0:128])[0:EDGE]
        east_going = flipped(dst[:, cols - 128 : cols])[128 - EDGE : 128]
        ca_ref[part, :] = pick(col_even, east_going, west_going)
        cb_ref[part, :] = pick(col_even, west_going, east_going)


def side_tile(left, right, width):
    return jnp.concatenate([right, jnp.zeros((128 - 2 * EDGE, width), F32), left], axis=0)


def hjb_sweep(rows, cols, ua, ub, m):
    wide = cols + 128
    tiles = wide // 128
    n_rows, n_cols = lax.axis_size("rows"), lax.axis_size("cols")
    sub = lax.broadcasted_iota(I32, (8, 128), 0)
    lane = lax.broadcasted_iota(I32, (8, 128), 1)
    top, bottom, first, last = sub == 0, sub == 7, lane == 0, lane == 127
    row_first = lax.axis_index("rows") * rows
    col = jnp.where(lane < 64, cols + lane, lane - 128) + lax.axis_index("cols") * cols
    side_ok = (col >= 0) & (col < cols * n_cols)
    src, dst = ua, ub

    def strip(i):
        return [src[i : i + 8, t * 128 : (t + 1) * 128] for t in range(tiles)]

    for step in range(HJB_STEPS):
        start, stop = PAD - 8, PAD + rows + 8
        here = strip(start)
        fell = [pltpu.roll(x, 1, 0) for x in here]
        rose = [pltpu.roll(x, 7, 0) for x in here]
        fell_before = fell
        for i in range(start, stop, 8):
            if i + 8 < stop:
                after = strip(i + 8)
                rose_after = [pltpu.roll(x, 7, 0) for x in after]
                fell_after = [pltpu.roll(x, 1, 0) for x in after]
            else:
                after, rose_after, fell_after = here, rose, fell
            row_ok = None
            if i < PAD or i >= PAD + rows:
                row = sub + (row_first + (i - PAD))
                row_ok = (row >= 0) & (row < rows * n_rows)
            went = [pltpu.roll(x, 1, 1) for x in here]
            came = [pltpu.roll(x, 127, 1) for x in here]
            for t in range(tiles):
                value = here[t]
                up = jnp.where(top, fell_before[t], fell[t])
                down = jnp.where(bottom, rose_after[t], rose[t])
                left = jnp.where(first, went[t - 1], went[t])
                right = jnp.where(last, came[(t + 1) % tiles], came[t])
                slope_x = jnp.maximum(value - jnp.minimum(up, down), 0.0)
                slope_y = jnp.maximum(value - jnp.minimum(left, right), 0.0)
                around = (up + down) + (left + right) + m[i : i + 8, t * 128 : (t + 1) * 128]
                new = 0.5 * value + 0.125 * (around - (slope_x * slope_x + slope_y * slope_y))
                ok = row_ok
                if t == tiles - 1:
                    ok = side_ok if ok is None else ok & side_ok
                dst[i : i + 8, t * 128 : (t + 1) * 128] = (
                    new if ok is None else jnp.where(ok, new, 0.0)
                )
            here, fell_before, fell, rose = after, fell, fell_after, rose_after
        src, dst = dst, src
    return src


def split(value):
    high = value.astype(BF16)
    return high, (value - high.astype(F32)).astype(BF16)


def lane_pick(value, index):
    dims = lax.GatherDimensionNumbers(
        offset_dims=(),
        collapsed_slice_dims=(1,),
        start_index_map=(1,),
        operand_batching_dims=(0,),
        start_indices_batching_dims=(0,),
    )
    return lax.gather(
        value, index[..., None], dims, (1, 1), mode=lax.GatherScatterMode.PROMISE_IN_BOUNDS
    )


def table_height(rows):
    return rows + 16


def fill_tables(rows, cols, u, tabs, halo):
    high_rows = table_height(rows)
    lane = lax.broadcasted_iota(I32, (8, 128), 1)
    lower = lane < 64
    for i in range(0, high_rows, 16):
        for parity in range(2):
            index = (2 * lane + parity) & 127
            for t in range(cols // 256):
                halves = []
                for j in range(2):
                    at = PAD + i + 8 * j
                    one = u[at : at + 8, 2 * t * 128 : (2 * t + 1) * 128]
                    two = u[at : at + 8, (2 * t + 1) * 128 : (2 * t + 2) * 128]
                    halves.append(
                        jnp.where(lower, lane_pick(one, index), lane_pick(two, index))
                    )
                high, low = split(jnp.concatenate(halves, axis=0))
                tabs[parity][i : i + 16, t * 128 : (t + 1) * 128] = high
                tabs[parity][high_rows + i : high_rows + i + 16, t * 128 : (t + 1) * 128] = low
        halo[i : i + 16, :] = jnp.broadcast_to(
            u[PAD + i : PAD + i + 16, cols : cols + 1], (16, 128)
        )


def sample_moves(
    rows, cols, blocks, cap, first, tabs, halo, starts, offs, wts, ends, dest, buf, slot_row,
    corner_row, counter
):
    n_cols = lax.axis_size("cols")
    my_row, my_col = lax.axis_index("rows"), lax.axis_index("cols")
    n_rows = lax.axis_size("rows")
    kinds = 4 if first else 2
    part_rows = 3 * kinds * cap + EDGE
    spare_row = n_cols * part_rows
    buf[...] = jnp.zeros(buf.shape, F32)
    for i in range(3 * n_cols):
        counter[i] = 0
    for b in range(blocks):
        tile = dest[b]
        band, column = tile // n_cols, tile % n_cols
        section = jnp.where(band == my_row, 0, jnp.where(band == (my_row ^ 1), 1, 2))
        distance = column ^ my_col
        rank = counter[distance * 3 + section]
        counter[distance * 3 + section] = rank + 1
        slot_row[b] = distance * part_rows + section * (kinds * cap) + rank
        if not first:
            goes = (band < n_rows - 1) & (column < n_cols - 1)
            row = ((column + 1) ^ my_col) * part_rows + 3 * kinds * cap + section
            corner_row[b] = jnp.where(goes, row, spare_row)

    high_rows = table_height(rows)
    pair_iota = lax.broadcasted_iota(I32, (cols // 2, 256), 0)
    row_iota = lax.broadcasted_iota(I32, (high_rows, 256), 0)

    def step(j, carry):
        def pair(ref):
            return jnp.concatenate([ref[pl.ds(2 * j, 1), :], ref[pl.ds(2 * j + 1, 1), :]], axis=1)

        row, col = row_col(pair(starts), cols)
        lanes = pl.ds(pl.multiple_of(j * 256, 256), 256)
        off_x = offs[0:1, lanes]
        off_y = offs[1:2, lanes]
        odd = (col & 1) == 1
        line = []
        for tab, place in ((tabs[0], (col + 1) >> 1), (tabs[1], col >> 1)):
            hot = jnp.where(pair_iota == place, 1.0, 0.0).astype(BF16)
            both = jnp.dot(tab[...], hot, preferred_element_type=F32)
            line.append(both[0:high_rows] + both[high_rows:])
        beyond = jnp.concatenate([halo[...]] * 2, axis=1)
        even_line = line[0] + jnp.where(col == cols - 1, beyond, 0.0)
        step_y = line[1] - even_line
        frac_x = 0.5 + 0.45 * jnp.tanh(off_x)
        frac_y = 0.5 + 0.45 * jnp.tanh(off_y)
        mixed = even_line + jnp.where(odd, 1.0 - frac_y, frac_y) * step_y
        here, below = row_iota == row, row_iota == row + 1
        grad_x = jnp.sum(
            jnp.where(below, mixed, jnp.where(here, -mixed, 0.0)), axis=0, keepdims=True
        )
        grad_y = jnp.sum(
            step_y * jnp.where(here, 1.0 - frac_x, jnp.where(below, frac_x, 0.0)),
            axis=0,
            keepdims=True,
        )
        grad_y = jnp.where(odd, -grad_y, grad_y)
        moved_x = 0.5 + 0.45 * jnp.tanh(off_x - grad_x)
        moved_y = 0.5 + 0.45 * jnp.tanh(off_y - grad_y)
        out = [moved_x, moved_y]
        if first:
            out += [pair(wts), (pair(ends) + 1).astype(F32)]
        else:
            corner = jnp.where(pair(ends) == rows * cols - 1, pair(wts) * moved_x * moved_y, 0.0)
        for half in range(2):
            if not first:
                buf[pl.ds(corner_row[2 * j + half], 1), :] += corner[:, half * 128 : (half + 1) * 128]
            base = slot_row[2 * j + half]
            for q, value in enumerate(out):
                buf[pl.ds(base + q * cap, 1), :] = value[:, half * 128 : (half + 1) * 128]
        return carry

    lax.fori_loop(0, blocks // 2, step, 0, unroll=UNROLL)


def first_kernel(
    rows, cols, blocks, cap, n_cols, *refs
):
    (ue_in, me_in, ra_ref, rb_ref, w_ref, v_ref, starts, offs, wts, ends, dest_hbm) = refs[:11]
    outs = refs[11 : 11 + n_cols]
    ue_ref, me_ref = refs[11 + n_cols : 13 + n_cols]
    ua, ub, tab_even, tab_odd, halo, buf, slot_row, corner_row, counter, dest, sem = refs[13 + n_cols :]
    fetch = pltpu.make_async_copy(dest_hbm, dest, sem)
    fetch.start()
    col_even = lax.axis_index("cols") % 2 == 0
    tall = ue_in.shape[0]
    width = ra_ref.shape[1]
    for index, (src, dst) in enumerate(((ue_in, ue_ref), (me_in, me_ref))):
        part = slice(index * EDGE, (index + 1) * EDGE)
        west = pick(col_even, rb_ref[part, :], ra_ref[part, :])
        east = pick(col_even, ra_ref[part, :], rb_ref[part, :])
        dst[:, 0:cols] = src[:, 0:cols]
        dst[:, cols : cols + 128] = unflipped(side_tile(west, east, width), tall)
    ua[...] = ue_ref[...]
    ub[...] = jnp.zeros(ub.shape, F32)
    u = hjb_sweep(rows, cols, ua, ub, me_ref)
    tabs = (tab_even, tab_odd)
    fill_tables(rows, cols, u, tabs, halo)
    fetch.wait()
    sample_moves(
        rows, cols, blocks, cap, True, tabs, halo, starts, offs, wts, ends, dest, buf, slot_row,
        corner_row, counter,
    )
    part_rows = 12 * cap + EDGE
    for k in range(n_cols):
        outs[k][0 : part_rows - EDGE, :] = buf[k * part_rows : (k + 1) * part_rows - EDGE, :]
        outs[k][part_rows - EDGE :, :] = w_ref[...] + v_ref[...]


def again_kernel(rows, cols, blocks, cap, n_cols, *refs):
    (ue_ref, m_in, d_ref, ra_ref, rb_ref, total_ref) = refs[:6]
    (starts, offs, wts, ends, dest_hbm) = refs[6:11]
    outs = refs[11 : 11 + n_cols]
    value_hbm, density_ref = refs[11 + n_cols : 13 + n_cols]
    (ua, ub, m, tab_even, tab_odd, halo, buf, slot_row, corner_row, counter, dest, sem, value_sem) = (
        refs[13 + n_cols :]
    )
    fetch = pltpu.make_async_copy(dest_hbm, dest, sem)
    fetch.start()
    col_even = lax.axis_index("cols") % 2 == 0
    n_rows = lax.axis_size("rows")
    tall = ue_ref.shape[0]
    width = ra_ref.shape[1]
    half_scale = 0.5 * ((rows * cols * n_rows * n_cols) / total_ref[0:1, 0:1])
    west = pick(col_even, rb_ref[...], ra_ref[...])
    east = pick(col_even, ra_ref[...], rb_ref[...])
    side = unflipped(side_tile(west[0:EDGE], east[0:EDGE], width), tall)
    pushed = unflipped(
        jnp.concatenate([west[EDGE : 2 * EDGE], jnp.zeros((128 - EDGE, width), F32)], axis=0), tall
    )
    m[:, 0:128] = 0.5 * m_in[:, 0:128] + half_scale * (d_ref[:, 0:128] + pushed)
    m[:, 128:cols] = 0.5 * m_in[:, 128:cols] + half_scale * d_ref[:, 128:cols]
    m[:, cols : cols + 128] = 0.5 * m_in[:, cols : cols + 128] + half_scale * (
        d_ref[:, cols : cols + 128] + side
    )
    density_ref[...] = m[PAD : PAD + rows, 0:cols]
    ua[...] = ue_ref[...]
    ub[...] = jnp.zeros(ub.shape, F32)
    u = hjb_sweep(rows, cols, ua, ub, m)
    leave = pltpu.make_async_copy(u.at[PAD : PAD + rows, 0:cols], value_hbm, value_sem)
    leave.start()
    tabs = (tab_even, tab_odd)
    fill_tables(rows, cols, u, tabs, halo)
    fetch.wait()
    sample_moves(
        rows, cols, blocks, cap, False, tabs, halo, starts, offs, wts, ends, dest, buf, slot_row,
        corner_row, counter,
    )
    part_rows = 6 * cap + EDGE
    for k in range(n_cols):
        outs[k][...] = buf[k * part_rows : (k + 1) * part_rows, :]
    leave.wait()


def deposit_blocks(rows, cols, cap, chunks, moves, masses, scratch, slots):
    acc, beside, lhs_a, rhs_a, lhs_b, rhs_b = scratch
    counts = []
    for q in range(chunks):
        cells = masses[(2 * q + 1) * cap : (2 * q + 2) * cap, :]
        counts.append(jnp.sum(jnp.where(cells > 0.5, 1.0, 0.0)).astype(I32) // 128)
    base = jnp.int32(0)
    for q in range(chunks):
        for rank in range(cap):
            slots[base + rank] = 2 * q * cap + rank
        base = base + counts[q]
    for rank in range(2 * GROUP):
        slots[base + rank] = 2 * chunks * cap
    lhs_b[...] = jnp.zeros(lhs_b.shape, BF16)
    rhs_b[...] = jnp.zeros(rhs_b.shape, BF16)
    high_rows = table_height(rows)
    sub16 = lax.broadcasted_iota(I32, (16, 128), 0)
    sub8 = lax.broadcasted_iota(I32, (8, 128), 0)
    one16, zero16 = jnp.ones((16, 128), BF16), jnp.zeros((16, 128), BF16)

    def relative(line, sub):
        return jnp.broadcast_to(line, sub.shape) - sub

    def build(first_slot, lhs, rhs):
        edges = []
        for t in range(GROUP):
            at = slots[first_slot + t]
            move_x = moves[pl.ds(at, 1), :]
            move_y = moves[pl.ds(at + cap, 1), :]
            mass = masses[pl.ds(at, 1), :]
            row, col = row_col(masses[pl.ds(at + cap, 1), :].astype(I32) - 1, cols)
            odd = (col & 1) == 1
            stay, go = mass * (1.0 - move_x), mass * move_x
            row_at = relative(row, sub16).astype(jnp.int16)
            values = []
            for parity in range(2):
                share = jnp.where(odd == (parity == 1), 1.0 - move_y, move_y)
                first, second = stay * share, go * share
                if parity == 0:
                    edge_row = jnp.where(col == cols - 1, row, -2)
                    edges.append((relative(edge_row, sub8), first, second))
                for one, two in zip(split(first), split(second)):
                    values.append(
                        [jnp.broadcast_to(x.astype(F32), (16, 128)).astype(BF16) for x in (one, two)]
                    )
            for i in range(high_rows // 16):
                here, below = row_at == 16 * i, row_at == 16 * i - 1
                for index, (one, two) in enumerate(values):
                    at_row = (index % 2) * high_rows + 16 * i
                    lhs[index // 2, t, at_row : at_row + 16, :] = jnp.where(
                        here, one, jnp.where(below, two, zero16)
                    )
            for parity, place in ((0, (col + 1) >> 1), (1, col >> 1)):
                place_at = relative(place, sub16).astype(jnp.int16)
                for i in range(cols // 32):
                    rhs[parity, t, 16 * i : 16 * i + 16, :] = jnp.where(
                        place_at == 16 * i, one16, zero16
                    )
        for i in range(rows // 8 + 1):
            total = beside[8 * i : 8 * i + 8, :]
            for row_at, first, second in edges:
                total = total + jnp.where(
                    row_at == 8 * i, first, jnp.where(row_at == 8 * i - 1, second, 0.0)
                )
            beside[8 * i : 8 * i + 8, :] = total

    def multiply(lhs, rhs):
        for parity in range(2):
            one, two = [
                jnp.concatenate([ref[parity, t] for t in range(GROUP)], axis=1) for ref in (lhs, rhs)
            ]
            acc[parity] += lax.dot_general(
                one, two, (((1,), (1,)), ((), ())), preferred_element_type=F32
            )

    def step(g, carry):
        multiply(lhs_b, rhs_b)
        build(2 * g * GROUP, lhs_a, rhs_a)
        multiply(lhs_a, rhs_a)
        build((2 * g + 1) * GROUP, lhs_b, rhs_b)
        return carry

    lax.fori_loop(0, (base + 2 * GROUP - 1) // (2 * GROUP), step, 0)
    multiply(lhs_b, rhs_b)


def finish_grid(rows, cols, acc, beside, grid):
    high_rows = table_height(rows)
    wide = cols + 128
    lane = lax.broadcasted_iota(I32, (8, wide), 1)
    lane1 = lax.broadcasted_iota(I32, (8, 128), 1)
    odd_lane = (lane1 & 1) == 1
    half = lane1 >> 1

    def weave(i, even, odd):
        for t in range(cols // 128):
            index = half + 64 * (t % 2)
            at = slice((t // 2) * 128, (t // 2 + 1) * 128)
            grid[i : i + 8, t * 128 : (t + 1) * 128] = jnp.where(
                odd_lane, lane_pick(odd[:, at], index), lane_pick(even[:, at], index)
            )
        right = jnp.sum(beside[i : i + 8, :], axis=1, keepdims=True)
        grid[i : i + 8, cols:wide] = jnp.where(lane1 == 0, right, 0.0)

    for i in range(0, rows + 8, 8):
        weave(
            i,
            *[acc[p, i : i + 8, :] + acc[p, high_rows + i : high_rows + i + 8, :] for p in range(2)],
        )

    @pl.when(lax.axis_index("rows") == lax.axis_size("rows") - 1)
    def _():
        tail = grid[rows - 8 : rows, :]
        sub8 = lax.broadcasted_iota(I32, (8, wide), 0)
        spill_row = jnp.broadcast_to(grid[rows : rows + 1, :], (8, wide))
        grid[rows - 8 : rows, :] = tail + jnp.where(sub8 == 7, spill_row, 0.0)
        grid[rows : rows + 8, :] = jnp.zeros((8, wide), F32)

    @pl.when(lax.axis_index("cols") == lax.axis_size("cols") - 1)
    def _():
        for i in range(0, rows + 8, 8):
            line = grid[i : i + 8, :]
            moved = jnp.where(lane == cols - 1, pltpu.roll(line, wide - 1, 1), 0.0)
            grid[i : i + 8, :] = jnp.where(lane < cols, line + moved, 0.0)


def own_deposit_kernel(rows, cols, cap, n_cols, first, *refs):
    pieces, refs = refs[:n_cols], refs[n_cols:]
    if first:
        acc_out, beside_out, masses, moves, *scratch, slots = refs
    else:
        masses, acc_out, beside_out, moves, *scratch, slots = refs
    size = 2 * cap
    for k in range(n_cols):
        moves[k * size : (k + 1) * size, :] = pieces[k][0:size, :]
        if first:
            masses[k * size : (k + 1) * size, :] = pieces[k][size : 2 * size, :]
    for ref in (moves, masses) if first else (moves,):
        ref[n_cols * size :, :] = jnp.zeros((size, 128), F32)
    acc_out[...] = jnp.zeros(acc_out.shape, F32)
    beside_out[...] = jnp.zeros(beside_out.shape, F32)
    deposit_blocks(
        rows, cols, cap, n_cols, moves, masses, (acc_out, beside_out, *scratch), slots
    )


def other_deposit(rows, cols, cap, n_cols, first, came, acc_in, beside_in, masses, grid, scratch):
    moves, acc, beside, *rest, slots = scratch
    size = 2 * cap
    step = 2 * size if first else size
    for index, ref in enumerate(came):
        for k in range(n_cols):
            at = (index * n_cols + k) * size
            moves[at : at + size, :] = ref[k * step : k * step + size, :]
            if first:
                masses[at : at + size, :] = ref[k * step + size : (k + 1) * step, :]
    for ref in (moves, masses) if first else (moves,):
        ref[2 * n_cols * size :, :] = jnp.zeros((size, 128), F32)
    acc[...] = acc_in[...]
    beside[...] = beside_in[...]
    deposit_blocks(
        rows, cols, cap, 2 * n_cols, moves, masses, (acc, beside, *rest), slots
    )
    finish_grid(rows, cols, acc, beside, grid)


def first_deposit_kernel(rows, cols, cap, n_cols, *refs):
    ra_ref, rb_ref, acc_in, beside_in, total_in = refs[:5]
    grid, sa_ref, sb_ref, masses, total = refs[5:10]
    other_deposit(
        rows, cols, cap, n_cols, True, (ra_ref, rb_ref), acc_in, beside_in, masses, grid, refs[10:]
    )
    total[...] = total_in[...] + ra_ref[4 * cap * n_cols :, :]
    row_even = lax.axis_index("rows") % 2 == 0
    south_going = grid[rows - 7 : rows + 1, :]
    north_going = grid[0:8, :]
    sa_ref[...] = pick(row_even, south_going, north_going)
    sb_ref[...] = pick(row_even, north_going, south_going)


def last_deposit_kernel(rows, cols, cap, n_cols, *refs):
    ra_ref, rb_ref, acc_in, beside_in, masses, corner_ref = refs[:6]
    grid, row_ref, col_ref = refs[6:9]
    other_deposit(
        rows, cols, cap, n_cols, False, (ra_ref, rb_ref), acc_in, beside_in, masses, grid, refs[9:]
    )
    tail = 2 * cap * n_cols
    corner = corner_ref[0:1, :] + ra_ref[tail + 1 : tail + 2, :] + rb_ref[tail + 2 : tail + 3, :]
    corner = jnp.sum(corner, axis=1, keepdims=True)
    place = lax.broadcasted_iota(I32, (8, 128), 0) + lax.broadcasted_iota(I32, (8, 128), 1)
    row_ref[...] = grid[rows : rows + 8, 0:cols]
    row_ref[:, 0:128] = row_ref[:, 0:128] + jnp.where(place == 0, corner, 0.0)
    col_ref[...] = flipped(grid[0:rows, cols : cols + 128])[0:8]


def edge_mid_kernel(rows, cols, g_ref, a_ref, b_ref, d_ref, ca_ref, cb_ref):
    row_even = lax.axis_index("rows") % 2 == 0
    col_even = lax.axis_index("cols") % 2 == 0
    wide = cols + 128
    north = pick(row_even, b_ref[...], a_ref[...])
    south = pick(row_even, a_ref[...], b_ref[...])
    d_ref[0:PAD, :] = jnp.zeros((PAD, wide), F32)
    d_ref[PAD : PAD + rows, :] = g_ref[0:rows, :]
    d_ref[PAD + rows : PAD + rows + 8, :] = south + g_ref[rows : rows + 8, :]
    d_ref[PAD + rows + 8 :, :] = jnp.zeros((d_ref.shape[0] - PAD - rows - 8, wide), F32)
    d_ref[PAD - 7 : PAD + 1, :] = d_ref[PAD - 7 : PAD + 1, :] + north
    west_going = flipped(d_ref[:, 0:128])[0:EDGE]
    east_going = flipped(d_ref[:, cols - 128 : cols])[128 - EDGE : 128]
    spilled = flipped(d_ref[:, cols : cols + 128])[0:EDGE]
    ca_ref[0:EDGE, :] = pick(col_even, east_going, west_going)
    cb_ref[0:EDGE, :] = pick(col_even, west_going, east_going)
    ca_ref[EDGE:, :] = pick(col_even, spilled, 0.0)
    cb_ref[EDGE:, :] = pick(col_even, 0.0, spilled)


def final_kernel(rows, cols, g_ref, m_ref, row_in, col_in, total_ref, out_ref):
    n_rows, n_cols = lax.axis_size("rows"), lax.axis_size("cols")
    half_scale = 0.5 * ((rows * cols * n_rows * n_cols) / total_ref[0:1, 0:1])
    out_ref[...] = 0.5 * m_ref[...] + half_scale * g_ref[0:rows, 0:cols]
    out_ref[0:8, :] = out_ref[0:8, :] + half_scale * row_in[...]
    beside = jnp.concatenate([col_in[...], jnp.zeros((120, col_in.shape[1]), F32)], axis=0)
    out_ref[:, 0:128] = out_ref[:, 0:128] + half_scale * unflipped(beside, rows)


def exchange_columns(outs):
    came = {k: xor_permute(outs[k], "cols", k) for k in range(len(outs) - 1, 0, -1)}
    return [outs[0]] + [came[k] for k in range(1, len(outs))]


def exchange_rows(pieces, kinds, cap, extra_first, extra_second=None):
    step = kinds * cap
    first = [piece[step : 2 * step] for piece in pieces] + [extra_first]
    second = [piece[2 * step : 3 * step] for piece in pieces]
    if extra_second is not None:
        second.append(extra_second)
    return swap_both(jnp.concatenate(first), jnp.concatenate(second), "rows")


def body(terminal_value, density_start, start_cells, offsets, weights, dest_tiles, end_cells):
    rows, cols = terminal_value.shape
    n_rows, n_cols = lax.axis_size("rows"), lax.axis_size("cols")
    blocks = dest_tiles.shape[0]
    cap = blocks // 4
    chunks = 3 * n_cols
    wide, tall = cols + 128, rows + 2 * PAD
    flat = -(-tall // 128) * 128
    starts = start_cells.reshape(blocks, 128)
    wts = weights.reshape(blocks, 128)
    ends = end_cells.reshape(blocks, 128)
    arrays = (terminal_value, density_start, wts, starts, offsets, ends)
    *arrays, sa, sb, total = vmem_call(
        functools.partial(start_kernel, rows, len(arrays)),
        (
            *[shape(*x.shape, dtype=x.dtype) for x in arrays],
            shape(2 * EDGE, cols),
            shape(2 * EDGE, cols),
            shape(EDGE, 128),
        ),
        len(arrays),
        [pltpu.SemaphoreType.DMA((len(arrays),))],
        hbm_in=range(len(arrays)),
    )(*arrays)
    terminal_value, density_start, wts, starts, offsets, ends = arrays
    bits = [1 << i for i in range(1, n_rows.bit_length() - 1)]
    ra, rb = swap_both(sa, sb, "rows")
    more = xor_permute(total, "rows", bits[0])
    ue, me, ca, cb, total = vmem_call(
        functools.partial(start_mid_kernel, rows, cols),
        (
            shape(tall, wide),
            shape(tall, wide),
            shape(2 * EDGE, flat),
            shape(2 * EDGE, flat),
            shape(EDGE, 128),
        ),
        6,
    )(terminal_value, density_start, ra, rb, total, more)
    ca, cb = swap_both(ca, cb, "cols")
    for bit in bits[1:-1]:
        total = total + xor_permute(total, "rows", bit)
    more = xor_permute(total, "rows", bits[-1])
    sweep_scratch = [
        pltpu.VMEM((tall, wide), F32),
        pltpu.VMEM((tall, wide), F32),
    ]

    def sample_scratch(part_rows):
        return [
            pltpu.VMEM((2 * table_height(rows), cols // 2), BF16),
            pltpu.VMEM((2 * table_height(rows), cols // 2), BF16),
            pltpu.VMEM((table_height(rows), 128), F32),
            pltpu.VMEM((n_cols * part_rows + EDGE, 128), F32),
            pltpu.SMEM((blocks,), I32),
            pltpu.SMEM((blocks,), I32),
            pltpu.SMEM((chunks,), I32),
            pltpu.SMEM((blocks,), I32),
            pltpu.SemaphoreType.DMA(()),
        ]

    high_rows = table_height(rows)
    acc_shape = (2, 2 * high_rows, cols // 2)
    beside_shape = (rows + 8, 128)
    product_scratch = [
        pltpu.VMEM((2, GROUP, 2 * high_rows, 128), BF16),
        pltpu.VMEM((2, GROUP, cols // 2, 128), BF16),
    ] * 2

    def part_rows_of(chunk_count):
        return 2 * cap * (chunk_count + 1)

    own_scratch = [
        pltpu.VMEM((part_rows_of(n_cols), 128), F32),
        *product_scratch,
        pltpu.SMEM((n_cols * cap + 2 * GROUP,), I32),
    ]
    other_scratch = [
        pltpu.VMEM((part_rows_of(2 * n_cols), 128), F32),
        pltpu.VMEM(acc_shape, F32),
        pltpu.VMEM(beside_shape, F32),
        *product_scratch,
        pltpu.SMEM((2 * n_cols * cap + 2 * GROUP,), I32),
    ]
    carried = (shape(*acc_shape), shape(*beside_shape))
    part_rows = 12 * cap + EDGE
    *outs, ue, me = vmem_call(
        functools.partial(first_kernel, rows, cols, blocks, cap, n_cols),
        tuple([shape(part_rows, 128)] * n_cols + [shape(tall, wide)] * 2),
        11,
        sweep_scratch + sample_scratch(part_rows),
        hbm_in=(10,),
    )(ue, me, ca, cb, total, more, starts, offsets, wts, ends, dest_tiles)
    pieces = exchange_columns(outs)
    total = sum(piece[part_rows - EDGE :] for piece in pieces)
    ra, rb = exchange_rows(pieces, 4, cap, total)
    acc, beside, own_masses = vmem_call(
        functools.partial(own_deposit_kernel, rows, cols, cap, n_cols, True),
        (*carried, shape(part_rows_of(n_cols), 128)),
        n_cols,
        own_scratch,
    )(*pieces)
    grid, ea, eb, masses, total = vmem_call(
        functools.partial(first_deposit_kernel, rows, cols, cap, n_cols),
        (
            shape(rows + 8, wide),
            shape(8, wide),
            shape(8, wide),
            shape(part_rows_of(2 * n_cols), 128),
            shape(EDGE, 128),
        ),
        5,
        other_scratch,
    )(ra, rb, acc, beside, total)
    ea, eb = swap_both(ea, eb, "rows")
    deposit, ca, cb = vmem_call(
        functools.partial(edge_mid_kernel, rows, cols),
        (shape(tall, wide), shape(2 * EDGE, flat), shape(2 * EDGE, flat)),
        3,
    )(grid, ea, eb)
    ca, cb = swap_both(ca, cb, "cols")
    part_rows = 6 * cap + EDGE
    *outs, value, density = vmem_call(
        functools.partial(again_kernel, rows, cols, blocks, cap, n_cols),
        tuple([shape(part_rows, 128)] * n_cols + [shape(rows, cols)] * 2),
        11,
        sweep_scratch
        + [pltpu.VMEM((tall, wide), F32)]
        + sample_scratch(part_rows)
        + [pltpu.SemaphoreType.DMA(())],
        hbm_in=(10,),
        hbm_out=(n_cols,),
    )(ue, me, deposit, ca, cb, total, starts, offsets, wts, ends, dest_tiles)
    pieces = exchange_columns(outs)
    corner = sum(piece[part_rows - EDGE :] for piece in pieces)
    ra, rb = exchange_rows(pieces, 2, cap, corner, corner)
    acc, beside = vmem_call(
        functools.partial(own_deposit_kernel, rows, cols, cap, n_cols, False),
        carried,
        n_cols + 1,
        own_scratch,
    )(*pieces, own_masses)
    grid, below, beside = vmem_call(
        functools.partial(last_deposit_kernel, rows, cols, cap, n_cols),
        (shape(rows + 8, wide), shape(8, cols), shape(8, rows)),
        6,
        other_scratch,
    )(ra, rb, acc, beside, masses, corner)
    below = lax.ppermute(below, "rows", [(i, i + 1) for i in range(n_rows - 1)])
    beside = lax.ppermute(beside, "cols", [(i, i + 1) for i in range(n_cols - 1)])
    (density,) = vmem_call(
        functools.partial(final_kernel, rows, cols), (shape(rows, cols),), 5, keep=(0,)
    )(grid, density, below, beside, total)
    return (value, density)


def solution(mesh):
    in_specs = (
        P("rows", "cols"),
        P("rows", "cols"),
        P(("rows", "cols")),
        P(None, ("rows", "cols")),
        P(("rows", "cols")),
        P(("rows", "cols")),
        P(("rows", "cols")),
    )
    out_specs = (P("rows", "cols"), P("rows", "cols"))
    return jax.shard_map(body, mesh=mesh, in_specs=in_specs, out_specs=out_specs, check_vma=False)
```

profile of v0, /device:TPU:11, one launch (start us, length us, event | category | flops | bytes accessed | tf_op | source)
XLA Modules:
  0.0 88.2 jit_solution(1755304262622852039)
XLA Ops:
  0.6 1.2 %shard_map.86 = (f32[128,512]{1,0:T(8,128)S(1)}, f32[128,512]{1,0:T(8,128)S(1)}, f32[32,128]{1,0:T(8,128)S(1)}, s32[32,128]{1,0:T(8,128)S(1)}, f32[2,4096]{1,0:T...) custom-call(f32[128,512]{1,0:T(8,128)} %refs_0_.1, ...), custom_call_target="tpu_custom_call" | custom-call | tf_op jit(solution)/shard_map/pallas_call | solution.py:53
  1.8 0.7 collective-permute-start
  2.6 3.0 %collective-permute-start.1 = (f32[16,512]{1,0:T(8,128)S(1)}, f32[16,512]{1,0:T(8,128)S(1)}, u32[]{:S(2)}, u32[]{:S(2)}) collective-permute-start(f32[16,512]{1,0:T(8,128)S(1)} %get-tuple-element.47), channel_id=1, source_target_pairs={{4,8},{8,4},{12,16},{16,12},{20,24},{24,20},{5,9},{9,5},{13,17},{1... | collective-permute-start | bytes 98312 | tf_op jit(solution)/shard_map/ppermute | solution.py:28
  5.6 0.3 collective-permute-start.2
  5.9 2.5 %collective-permute-done.2.v_ref = f32[8,128]{1,0:T(8,128)S(1)} collective-permute-done((f32[8,128]{1,0:T(8,128)S(1)}, f32[8,128]{1,0:T(8,128)S(1)}, u32[]{:S(2)}, u32[]{:S(2)}) %collective-permute-start.2) | collective-permute-done | bytes 4128 | tf_op jit(solution)/shard_map/ppermute | solution.py:32
  8.4 0.0 collective-permute-done.a_ref
  8.4 0.3 collective-permute-done.1.b_ref
  8.7 0.2 shard_map.87
  8.9 0.2 collective-permute-start.3
  9.1 4.3 %collective-permute-start.4 = (f32[16,256]{1,0:T(8,128)S(1)}, f32[16,256]{1,0:T(8,128)S(1)}, u32[]{:S(2)}, u32[]{:S(2)}) collective-permute-start(f32[16,256]{1,0:T(8,128)S(1)} %get-tuple-element.52), channel_id=1, source_target_pairs={{1,2},{2,1},{5,6},{6,5},{9,10},{10,9},{13,14},{14,13},{17,18},{18,... | collective-permute-start | bytes 49160 | tf_op jit(solution)/shard_map/ppermute | solution.py:28
  13.4 0.1 collective-permute-start.5
  13.5 2.4 %collective-permute-done.5.refs_5_ = f32[8,128]{1,0:T(8,128)S(1)} collective-permute-done((f32[8,128]{1,0:T(8,128)S(1)}, f32[8,128]{1,0:T(8,128)S(1)}, u32[]{:S(2)}, u32[]{:S(2)}) %collective-permute-start.5) | collective-permute-done | bytes 4128 | tf_op jit(solution)/shard_map/ppermute | solution.py:32
  15.9 4.5 %shard_map.88 = (f32[104,128]{1,0:T(8,128)S(1)}, f32[104,128]{1,0:T(8,128)S(1)}, f32[104,128]{1,0:T(8,128)S(1)}, f32[104,128]{1,0:T(8,128)S(1)}, f32[160,640]{1,0:T(8,128)S(1)}, /*index=5*/f32[160,640]{1,0:T(8,128)S(1)}) custom-call(f32[160,640]{1,0:T(8,128)S(1)} %get-tuple-element.49.refs_0_, f32[160,640]{1,0:T(8,128)S(1)} %get-tuple-element.50.refs_1_, ...), custom_call_target="tpu_custom_call" | custom-call | tf_op jit(solution)/shard_map/pallas_call | solution.py:53
  20.5 0.1 collective-permute-start.6
  20.5 1.2 %collective-permute-start.7 = (f32[104,128]{1,0:T(8,128)S(1)}, f32[104,128]{1,0:T(8,128)S(1)}, u32[]{:S(2)}, u32[]{:S(2)}) collective-permute-start(f32[104,128]{1,0:T(8,128)S(1)} %get-tuple-element.62), channel_id=1, source_target_pairs={{0,2},{1,3},{2,0},{3,1},{4,6},{5,7},{6,4},{7,5},{8,10},{9,11},{10,... | collective-permute-start | bytes 159752 | tf_op jit(solution)/shard_map/ppermute | solution.py:32
  21.7 1.4 %collective-permute-start.8 = (f32[104,128]{1,0:T(8,128)S(1)}, f32[104,128]{1,0:T(8,128)S(1)}, u32[]{:S(2)}, u32[]{:S(2)}) collective-permute-start(f32[104,128]{1,0:T(8,128)S(1)} %get-tuple-element.63), channel_id=1, source_target_pairs={{0,3},{1,2},{2,1},{3,0},{4,7},{5,6},{6,5},{7,4},{8,11},{9,10},{10,... | collective-permute-start | bytes 159752 | tf_op jit(solution)/shard_map/ppermute | solution.py:32
  23.2 0.3 collective-permute-done.6.refs_1_
  23.5 1.0 %collective-permute-done.7.refs_2_ = f32[104,128]{1,0:T(8,128)S(1)} collective-permute-done((f32[104,128]{1,0:T(8,128)S(1)}, f32[104,128]{1,0:T(8,128)S(1)}, u32[]{:S(2)}, u32[]{:S(2)}) %collective-permute-start.7) | collective-permute-done | bytes 53280 | tf_op jit(solution)/shard_map/ppermute | solution.py:32
  24.5 2.0 %collective-permute-done.8.refs_3_ = f32[104,128]{1,0:T(8,128)S(1)} collective-permute-done((f32[104,128]{1,0:T(8,128)S(1)}, f32[104,128]{1,0:T(8,128)S(1)}, u32[]{:S(2)}, u32[]{:S(2)}) %collective-permute-start.8) | collective-permute-done | bytes 53280 | tf_op jit(solution)/shard_map/ppermute | solution.py:32
  26.5 2.8 %collective-permute-start.9 = (f32[136,128]{1,0:T(8,128)S(1)}, f32[136,128]{1,0:T(8,128)S(1)}, u32[]{:S(2)}, u32[]{:S(2)}) collective-permute-start(f32[136,128]{1,0:T(8,128)S(1)} %get-tuple-element.88), channel_id=1, source_target_pairs={{0,4},{4,0},{8,12},{12,8},{16,20},{20,16},{24,28},{28,24},{1,5},{5... | collective-permute-start | bytes 208904 | tf_op jit(solution)/shard_map/ppermute | solution.py:28
  29.3 3.9 %collective-permute-start.10 = (f32[128,128]{1,0:T(8,128)S(1)}, f32[128,128]{1,0:T(8,128)S(1)}, u32[]{:S(2)}, u32[]{:S(2)}) collective-permute-start(f32[128,128]{1,0:T(8,128)S(1)} %pad_maximum_fusion), channel_id=1, source_target_pairs={{4,8},{8,4},{12,16},{16,12},{20,24},{24,20},{5,9},{9,5},{13,17},{1... | collective-permute-start | bytes 196616 | tf_op jit(solution)/shard_map/ppermute | solution.py:28
  33.2 2.3 %shard_map.89 = (f32[2,288,256]{2,1,0:T(8,128)S(1)}, f32[136,128]{1,0:T(8,128)S(1)}, f32[80,128]{1,0:T(8,128)S(1)}) custom-call(f32[104,128]{1,0:T(8,128)S(1)} %get-tuple-element.60.refs_0_, f32[104,128]{1,0:T(8,128)S(1)} %collective-permute-done.6.refs_1_, f32[104,128]{1,0:T(8,128)S(1)} %collective-permute-done.7.refs_2_, ...), custom_call_target="tpu_custom_call" | custom-call | tf_op jit(solution)/shard_map/pallas_call | solution.py:53
  35.5 0.3 collective-permute-done.10.refs_1_
  35.8 4.4 %shard_map.90 = (f32[136,640]{1,0:T(8,128)S(1)}, f32[8,640]{1,0:T(8,128)S(1)}, f32[8,640]{1,0:T(8,128)S(1)}, f32[144,128]{1,0:T(8,128)S(1)}, f32[8,128]{1,0:T(8,128)S(1)}) custom-call(f32[136,128]{1,0:T(8,128)S(1)} %collective-permute-done.9.refs_0_, f32[128,128]{1,0:T(8,128)S(1)} %collective-permute-done.10.refs_1_, ...), custom_call_target="tpu_custom_call" | custom-call | tf_op jit(solution)/shard_map/pallas_call | solution.py:53
  40.2 0.1 collective-permute-start.11
  40.3 4.9 %collective-permute-start.12 = (f32[8,640]{1,0:T(8,128)S(1)}, f32[8,640]{1,0:T(8,128)S(1)}, u32[]{:S(2)}, u32[]{:S(2)}) collective-permute-start(f32[8,640]{1,0:T(8,128)S(1)} %get-tuple-element.68), channel_id=1, source_target_pairs={{4,8},{8,4},{12,16},{16,12},{20,24},{24,20},{5,9},{9,5},{13,17},{1... | collective-permute-start | bytes 61448 | tf_op jit(solution)/shard_map/ppermute | solution.py:28
  45.2 0.0 collective-permute-done.11.a_ref
  45.2 1.5 %collective-permute-done.12.b_ref = f32[8,640]{1,0:T(8,128)S(1)} collective-permute-done((f32[8,640]{1,0:T(8,128)S(1)}, f32[8,640]{1,0:T(8,128)S(1)}, u32[]{:S(2)}, u32[]{:S(2)}) %collective-permute-start.12) | collective-permute-done | bytes 20512 | tf_op jit(solution)/shard_map/ppermute | solution.py:28
  46.7 0.1 shard_map.91
  46.8 0.6 collective-permute-start.13
  47.5 5.0 %collective-permute-start.14 = (f32[16,256]{1,0:T(8,128)S(1)}, f32[16,256]{1,0:T(8,128)S(1)}, u32[]{:S(2)}, u32[]{:S(2)}) collective-permute-start(f32[16,256]{1,0:T(8,128)S(1)} %get-tuple-element.71), channel_id=1, source_target_pairs={{1,2},{2,1},{5,6},{6,5},{9,10},{10,9},{13,14},{14,13},{17,18},{18,... | collective-permute-start | bytes 49160 | tf_op jit(solution)/shard_map/ppermute | solution.py:28
  52.5 1.1 %collective-permute-done.14.refs_4_ = f32[16,256]{1,0:T(8,128)S(1)} collective-permute-done((f32[16,256]{1,0:T(8,128)S(1)}, f32[16,256]{1,0:T(8,128)S(1)}, u32[]{:S(2)}, u32[]{:S(2)}) %collective-permute-start.14) | collective-permute-done | bytes 16416 | tf_op jit(solution)/shard_map/ppermute | solution.py:28
  53.6 4.7 %shard_map.92 = (f32[56,128]{1,0:T(8,128)S(1)}, f32[56,128]{1,0:T(8,128)S(1)}, f32[56,128]{1,0:T(8,128)S(1)}, f32[56,128]{1,0:T(8,128)S(1)}, f32[128,512]{1,0:T(8,128)}, /*index=5*/f32[128,512]{1,0:T(8,128)S(1)}) custom-call(f32[160,640]{1,0:T(8,128)S(1)} %get-tuple-element.58.refs_0_, f32[160,640]{1,0:T(8,128)S(1)} %get-tuple-element.59.refs_1_, ...), custom_call_target="tpu_custom_call" | custom-call | tf_op jit(solution)/shard_map/pallas_call | solution.py:53
  58.3 0.1 collective-permute-start.15
  58.4 2.6 %collective-permute-start.16 = (f32[56,128]{1,0:T(8,128)S(1)}, f32[56,128]{1,0:T(8,128)S(1)}, u32[]{:S(2)}, u32[]{:S(2)}) collective-permute-start(f32[56,128]{1,0:T(8,128)S(1)} %get-tuple-element.76), channel_id=1, source_target_pairs={{0,2},{1,3},{2,0},{3,1},{4,6},{5,7},{6,4},{7,5},{8,10},{9,11},{10,... | collective-permute-start | bytes 86024 | tf_op jit(solution)/shard_map/ppermute | solution.py:32
  61.0 0.0 collective-permute-start.17
  61.0 0.1 collective-permute-done.15.refs_1_
  61.1 1.5 %collective-permute-done.16.refs_2_ = f32[56,128]{1,0:T(8,128)S(1)} collective-permute-done((f32[56,128]{1,0:T(8,128)S(1)}, f32[56,128]{1,0:T(8,128)S(1)}, u32[]{:S(2)}, u32[]{:S(2)}) %collective-permute-start.16) | collective-permute-done | bytes 28704 | tf_op jit(solution)/shard_map/ppermute | solution.py:32
  62.6 1.5 %collective-permute-done.17.refs_3_ = f32[56,128]{1,0:T(8,128)S(1)} collective-permute-done((f32[56,128]{1,0:T(8,128)S(1)}, f32[56,128]{1,0:T(8,128)S(1)}, u32[]{:S(2)}, u32[]{:S(2)}) %collective-permute-start.17) | collective-permute-done | bytes 28704 | tf_op jit(solution)/shard_map/ppermute | solution.py:32
  64.1 0.2 collective-permute-start.18
  64.2 7.3 %collective-permute-start.19 = (f32[72,128]{1,0:T(8,128)S(1)}, f32[72,128]{1,0:T(8,128)S(1)}, u32[]{:S(2)}, u32[]{:S(2)}) collective-permute-start(f32[72,128]{1,0:T(8,128)S(1)} %get-tuple-element.86), channel_id=1, source_target_pairs={{4,8},{8,4},{12,16},{16,12},{20,24},{24,20},{5,9},{9,5},{13,17},{1... | collective-permute-start | bytes 110600 | tf_op jit(solution)/shard_map/ppermute | solution.py:28
  71.5 2.3 %shard_map.93 = (f32[2,288,256]{2,1,0:T(8,128)S(1)}, f32[136,128]{1,0:T(8,128)S(1)}) custom-call(f32[56,128]{1,0:T(8,128)S(1)} %get-tuple-element.74.refs_0_, f32[56,128]{1,0:T(8,128)S(1)} %collective-permute-done.15.refs_1_, f32[56,128]{1,0:T(8,128)S(1)} %collective-permute-done.16.refs_2_, f32[56,128]{1,0:T(8,128)S(1)} %collective-permute-done.17.refs_3_, ...), custom_call_target="tpu_custom_call" | custom-call | tf_op jit(solution)/shard_map/pallas_call | solution.py:53
  73.9 0.0 collective-permute-done.19.refs_1_
  73.9 4.4 %shard_map.94 = (f32[136,640]{1,0:T(8,128)S(1)}, f32[8,512]{1,0:T(8,128)S(1)}, f32[8,128]{1,0:T(8,128)S(1)}) custom-call(f32[72,128]{1,0:T(8,128)S(1)} %collective-permute-done.18.refs_0_, f32[72,128]{1,0:T(8,128)S(1)} %collective-permute-done.19.refs_1_, f32[2,288,256]{2,1,0:T(8,128)S(1)} %get-tuple-element.79.refs_2_, ...), custom_call_target="tpu_custom_call" | custom-call | tf_op jit(solution)/shard_map/pallas_call | solution.py:53
  78.3 4.7 %collective-permute-start.20 = (f32[8,512]{1,0:T(8,128)S(1)}, f32[8,512]{1,0:T(8,128)S(1)}, u32[]{:S(2)}, u32[]{:S(2)}) collective-permute-start(f32[8,512]{1,0:T(8,128)S(1)} %get-tuple-element.84), channel_id=1, source_target_pairs={{0,4},{4,8},{8,12},{12,16},{16,20},{20,24},{24,28},{1,5},{5,9},{9,... | collective-permute-start | bytes 49160 | tf_op jit(solution)/shard_map/ppermute | solution.py:781
  83.0 1.9 %collective-permute-start.21 = (f32[8,128]{1,0:T(8,128)S(1)}, f32[8,128]{1,0:T(8,128)S(1)}, u32[]{:S(2)}, u32[]{:S(2)}) collective-permute-start(f32[8,128]{1,0:T(8,128)S(1)} %get-tuple-element.85), channel_id=1, source_target_pairs={{0,1},{1,2},{2,3},{4,5},{5,6},{6,7},{8,9},{9,10},{10,11},{12,13},{... | collective-permute-start | bytes 12296 | tf_op jit(solution)/shard_map/ppermute | solution.py:782
  85.0 2.4 %collective-permute-done.21.col_in = f32[8,128]{1,0:T(8,128)S(1)} collective-permute-done((f32[8,128]{1,0:T(8,128)S(1)}, f32[8,128]{1,0:T(8,128)S(1)}, u32[]{:S(2)}, u32[]{:S(2)}) %collective-permute-start.21) | collective-permute-done | bytes 4128 | tf_op jit(solution)/shard_map/ppermute | solution.py:782
  87.4 0.8 shard_map.95
  (18 shorter events, 0.1 us)
Async XLA Ops:
  1.8 6.6 %collective-permute-start = (f32[16,512]{1,0:T(8,128)S(1)}, f32[16,512]{1,0:T(8,128)S(1)}, u32[]{:S(2)}, u32[]{:S(2)}) collective-permute-start(f32[16,512]{1,0:T(8,128)S(1)} %get-tuple-element.46), channel_id=1, source_target_pairs={{0,4},{4,0},{8,12},{12,8},{16,20},{20,16},{24,28},{28,24},{1,5},{5... | collective-permute-start | bytes 98312 | tf_op jit(solution)/shard_map/ppermute | solution.py:28
  2.6 6.1 %collective-permute-start.1 = (f32[16,512]{1,0:T(8,128)S(1)}, f32[16,512]{1,0:T(8,128)S(1)}, u32[]{:S(2)}, u32[]{:S(2)}) collective-permute-start(f32[16,512]{1,0:T(8,128)S(1)} %get-tuple-element.47), channel_id=1, source_target_pairs={{4,8},{8,4},{12,16},{16,12},{20,24},{24,20},{5,9},{9,5},{13,17},{1... | collective-permute-start | bytes 98312 | tf_op jit(solution)/shard_map/ppermute | solution.py:28
  5.6 2.8 %collective-permute-start.2 = (f32[8,128]{1,0:T(8,128)S(1)}, f32[8,128]{1,0:T(8,128)S(1)}, u32[]{:S(2)}, u32[]{:S(2)}) collective-permute-start(f32[8,128]{1,0:T(8,128)S(1)} %get-tuple-element.48.w_ref), channel_id=1, source_target_pairs={{0,8},{4,12},{8,0},{12,4},{16,24},{20,28},{24,16},{28,20},{1,9},{5... | collective-permute-start | bytes 12296 | tf_op jit(solution)/shard_map/ppermute | solution.py:32
  8.9 7.1 %collective-permute-start.3 = (f32[16,256]{1,0:T(8,128)S(1)}, f32[16,256]{1,0:T(8,128)S(1)}, u32[]{:S(2)}, u32[]{:S(2)}) collective-permute-start(f32[16,256]{1,0:T(8,128)S(1)} %get-tuple-element.51), channel_id=1, source_target_pairs={{0,1},{1,0},{2,3},{3,2},{4,5},{5,4},{6,7},{7,6},{8,9},{9,8},{10,11... | collective-permute-start | bytes 49160 | tf_op jit(solution)/shard_map/ppermute | solution.py:28
  9.1 6.9 %collective-permute-start.4 = (f32[16,256]{1,0:T(8,128)S(1)}, f32[16,256]{1,0:T(8,128)S(1)}, u32[]{:S(2)}, u32[]{:S(2)}) collective-permute-start(f32[16,256]{1,0:T(8,128)S(1)} %get-tuple-element.52), channel_id=1, source_target_pairs={{1,2},{2,1},{5,6},{6,5},{9,10},{10,9},{13,14},{14,13},{17,18},{18,... | collective-permute-start | bytes 49160 | tf_op jit(solution)/shard_map/ppermute | solution.py:28
  13.4 2.5 %collective-permute-start.5 = (f32[8,128]{1,0:T(8,128)S(1)}, f32[8,128]{1,0:T(8,128)S(1)}, u32[]{:S(2)}, u32[]{:S(2)}) collective-permute-start(f32[8,128]{1,0:T(8,128)S(1)} %get-tuple-element.53.refs_4_), channel_id=1, source_target_pairs={{0,16},{4,20},{8,24},{12,28},{16,0},{20,4},{24,8},{28,12},{1,17},{... | collective-permute-start | bytes 12296 | tf_op jit(solution)/shard_map/ppermute | solution.py:32
  20.5 3.0 %collective-permute-start.6 = (f32[104,128]{1,0:T(8,128)S(1)}, f32[104,128]{1,0:T(8,128)S(1)}, u32[]{:S(2)}, u32[]{:S(2)}) collective-permute-start(f32[104,128]{1,0:T(8,128)S(1)} %get-tuple-element.61), channel_id=1, source_target_pairs={{0,1},{1,0},{2,3},{3,2},{4,5},{5,4},{6,7},{7,6},{8,9},{9,8},{10,11... | collective-permute-start | bytes 159752 | tf_op jit(solution)/shard_map/ppermute | solution.py:32
  20.5 4.0 %collective-permute-start.7 = (f32[104,128]{1,0:T(8,128)S(1)}, f32[104,128]{1,0:T(8,128)S(1)}, u32[]{:S(2)}, u32[]{:S(2)}) collective-permute-start(f32[104,128]{1,0:T(8,128)S(1)} %get-tuple-element.62), channel_id=1, source_target_pairs={{0,2},{1,3},{2,0},{3,1},{4,6},{5,7},{6,4},{7,5},{8,10},{9,11},{10,... | collective-permute-start | bytes 159752 | tf_op jit(solution)/shard_map/ppermute | solution.py:32
  21.7 4.8 %collective-permute-start.8 = (f32[104,128]{1,0:T(8,128)S(1)}, f32[104,128]{1,0:T(8,128)S(1)}, u32[]{:S(2)}, u32[]{:S(2)}) collective-permute-start(f32[104,128]{1,0:T(8,128)S(1)} %get-tuple-element.63), channel_id=1, source_target_pairs={{0,3},{1,2},{2,1},{3,0},{4,7},{5,6},{6,5},{7,4},{8,11},{9,10},{10,... | collective-permute-start | bytes 159752 | tf_op jit(solution)/shard_map/ppermute | solution.py:32
  26.5 9.3 %collective-permute-start.9 = (f32[136,128]{1,0:T(8,128)S(1)}, f32[136,128]{1,0:T(8,128)S(1)}, u32[]{:S(2)}, u32[]{:S(2)}) collective-permute-start(f32[136,128]{1,0:T(8,128)S(1)} %get-tuple-element.88), channel_id=1, source_target_pairs={{0,4},{4,0},{8,12},{12,8},{16,20},{20,16},{24,28},{28,24},{1,5},{5... | collective-permute-start | bytes 208904 | tf_op jit(solution)/shard_map/ppermute | solution.py:28
  29.3 6.5 %collective-permute-start.10 = (f32[128,128]{1,0:T(8,128)S(1)}, f32[128,128]{1,0:T(8,128)S(1)}, u32[]{:S(2)}, u32[]{:S(2)}) collective-permute-start(f32[128,128]{1,0:T(8,128)S(1)} %pad_maximum_fusion), channel_id=1, source_target_pairs={{4,8},{8,4},{12,16},{16,12},{20,24},{24,20},{5,9},{9,5},{13,17},{1... | collective-permute-start | bytes 196616 | tf_op jit(solution)/shard_map/ppermute | solution.py:28
  40.2 5.0 %collective-permute-start.11 = (f32[8,640]{1,0:T(8,128)S(1)}, f32[8,640]{1,0:T(8,128)S(1)}, u32[]{:S(2)}, u32[]{:S(2)}) collective-permute-start(f32[8,640]{1,0:T(8,128)S(1)} %get-tuple-element.67), channel_id=1, source_target_pairs={{0,4},{4,0},{8,12},{12,8},{16,20},{20,16},{24,28},{28,24},{1,5},{5... | collective-permute-start | bytes 61448 | tf_op jit(solution)/shard_map/ppermute | solution.py:28
  40.3 6.4 %collective-permute-start.12 = (f32[8,640]{1,0:T(8,128)S(1)}, f32[8,640]{1,0:T(8,128)S(1)}, u32[]{:S(2)}, u32[]{:S(2)}) collective-permute-start(f32[8,640]{1,0:T(8,128)S(1)} %get-tuple-element.68), channel_id=1, source_target_pairs={{4,8},{8,4},{12,16},{16,12},{20,24},{24,20},{5,9},{9,5},{13,17},{1... | collective-permute-start | bytes 61448 | tf_op jit(solution)/shard_map/ppermute | solution.py:28
  46.8 5.7 %collective-permute-start.13 = (f32[16,256]{1,0:T(8,128)S(1)}, f32[16,256]{1,0:T(8,128)S(1)}, u32[]{:S(2)}, u32[]{:S(2)}) collective-permute-start(f32[16,256]{1,0:T(8,128)S(1)} %get-tuple-element.70), channel_id=1, source_target_pairs={{0,1},{1,0},{2,3},{3,2},{4,5},{5,4},{6,7},{7,6},{8,9},{9,8},{10,11... | collective-permute-start | bytes 49160 | tf_op jit(solution)/shard_map/ppermute | solution.py:28
  47.5 6.1 %collective-permute-start.14 = (f32[16,256]{1,0:T(8,128)S(1)}, f32[16,256]{1,0:T(8,128)S(1)}, u32[]{:S(2)}, u32[]{:S(2)}) collective-permute-start(f32[16,256]{1,0:T(8,128)S(1)} %get-tuple-element.71), channel_id=1, source_target_pairs={{1,2},{2,1},{5,6},{6,5},{9,10},{10,9},{13,14},{14,13},{17,18},{18,... | collective-permute-start | bytes 49160 | tf_op jit(solution)/shard_map/ppermute | solution.py:28
  58.3 2.8 %collective-permute-start.15 = (f32[56,128]{1,0:T(8,128)S(1)}, f32[56,128]{1,0:T(8,128)S(1)}, u32[]{:S(2)}, u32[]{:S(2)}) collective-permute-start(f32[56,128]{1,0:T(8,128)S(1)} %get-tuple-element.75), channel_id=1, source_target_pairs={{0,1},{1,0},{2,3},{3,2},{4,5},{5,4},{6,7},{7,6},{8,9},{9,8},{10,11... | collective-permute-start | bytes 86024 | tf_op jit(solution)/shard_map/ppermute | solution.py:32
  58.4 4.2 %collective-permute-start.16 = (f32[56,128]{1,0:T(8,128)S(1)}, f32[56,128]{1,0:T(8,128)S(1)}, u32[]{:S(2)}, u32[]{:S(2)}) collective-permute-start(f32[56,128]{1,0:T(8,128)S(1)} %get-tuple-element.76), channel_id=1, source_target_pairs={{0,2},{1,3},{2,0},{3,1},{4,6},{5,7},{6,4},{7,5},{8,10},{9,11},{10,... | collective-permute-start | bytes 86024 | tf_op jit(solution)/shard_map/ppermute | solution.py:32
  61.0 3.0 %collective-permute-start.17 = (f32[56,128]{1,0:T(8,128)S(1)}, f32[56,128]{1,0:T(8,128)S(1)}, u32[]{:S(2)}, u32[]{:S(2)}) collective-permute-start(f32[56,128]{1,0:T(8,128)S(1)} %get-tuple-element.77), channel_id=1, source_target_pairs={{0,3},{1,2},{2,1},{3,0},{4,7},{5,6},{6,5},{7,4},{8,11},{9,10},{10,... | collective-permute-start | bytes 86024 | tf_op jit(solution)/shard_map/ppermute | solution.py:32
  64.1 9.8 %collective-permute-start.18 = (f32[72,128]{1,0:T(8,128)S(1)}, f32[72,128]{1,0:T(8,128)S(1)}, u32[]{:S(2)}, u32[]{:S(2)}) collective-permute-start(f32[72,128]{1,0:T(8,128)S(1)} %constant_dynamic-update-slice_fusion.5), channel_id=1, source_target_pairs={{0,4},{4,0},{8,12},{12,8},{16,20},{20,16},{24,28},{28,24},{1,5},{5... | collective-permute-start | bytes 110600 | tf_op jit(solution)/shard_map/ppermute | solution.py:28
  64.2 9.6 %collective-permute-start.19 = (f32[72,128]{1,0:T(8,128)S(1)}, f32[72,128]{1,0:T(8,128)S(1)}, u32[]{:S(2)}, u32[]{:S(2)}) collective-permute-start(f32[72,128]{1,0:T(8,128)S(1)} %get-tuple-element.86), channel_id=1, source_target_pairs={{4,8},{8,4},{12,16},{16,12},{20,24},{24,20},{5,9},{9,5},{13,17},{1... | collective-permute-start | bytes 110600 | tf_op jit(solution)/shard_map/ppermute | solution.py:28
  78.3 9.1 %collective-permute-start.20 = (f32[8,512]{1,0:T(8,128)S(1)}, f32[8,512]{1,0:T(8,128)S(1)}, u32[]{:S(2)}, u32[]{:S(2)}) collective-permute-start(f32[8,512]{1,0:T(8,128)S(1)} %get-tuple-element.84), channel_id=1, source_target_pairs={{0,4},{4,8},{8,12},{12,16},{16,20},{20,24},{24,28},{1,5},{5,9},{9,... | collective-permute-start | bytes 49160 | tf_op jit(solution)/shard_map/ppermute | solution.py:781
  83.0 4.4 %collective-permute-start.21 = (f32[8,128]{1,0:T(8,128)S(1)}, f32[8,128]{1,0:T(8,128)S(1)}, u32[]{:S(2)}, u32[]{:S(2)}) collective-permute-start(f32[8,128]{1,0:T(8,128)S(1)} %get-tuple-element.85), channel_id=1, source_target_pairs={{0,1},{1,2},{2,3},{4,5},{5,6},{6,7},{8,9},{9,10},{10,11},{12,13},{... | collective-permute-start | bytes 12296 | tf_op jit(solution)/shard_map/ppermute | solution.py:782
where the time goes:
time: 88.2 us
  starting transfers between devices  45.5 us (52%)
  Pallas kernels  24.9 us (28%)
  waiting for transfers between devices  16.8 us (19%)
    ppermute x6, starting transfers between devices, swap_both(): lax.ppermute(second, axis, pairs_b)  28.5 us
    pallas_call x10, Pallas kernels, run(): call(*[pltpu.with_memory_space_constraint(x, pltpu.HBM if i in hbm_in els...  24.9 us
    ppermute x8, waiting for transfers between devices, xor_permute(): lax.ppermute(value, axis, [(i, i ^ bit) for i in range(lax.axis_size(axis...  11.3 us
    ppermute x8, starting transfers between devices, xor_permute(): lax.ppermute(value, axis, [(i, i ^ bit) for i in range(lax.axis_size(axis...  5.8 us
    ppermute x1, starting transfers between devices, body(): below = lax.ppermute(below, 'rows', [(i, i + 1) for i in range(n_rows - 1)])  4.72 us
    ppermute x6, starting transfers between devices, swap_both(): lax.ppermute(first, axis, pairs_a)  4.61 us
    ppermute x6, waiting for transfers between devices, swap_both(): lax.ppermute(second, axis, pairs_b)  3.12 us
    ppermute x1, waiting for transfers between devices, body(): lax.ppermute(beside, 'cols', [(i, i + 1) for i in range(n_cols - 1)])  2.42 us
  transfers between devices with their start and end apart: 22, of which 13 were waited for; matrix products, arithmetic and copies ran while one was open for 0% of the time, Pallas kernels for 5%

commit v1 on v0

--- a/solution.py
+++ b/solution.py
@@ -262,8 +262,9 @@
             corner_row[b] = jnp.where(goes, row, spare_row)
 
     high_rows = table_height(rows)
-    pair_iota = lax.broadcasted_iota(I32, (cols // 2, 256), 0)
-    row_iota = lax.broadcasted_iota(I32, (high_rows, 256), 0)
+    sub16 = lax.broadcasted_iota(I32, (16, 256), 0)
+    sub8 = lax.broadcasted_iota(I32, (8, 256), 0)
+    one16, zero16 = jnp.ones((16, 256), BF16), jnp.zeros((16, 256), BF16)
 
     def step(j, carry):
         def pair(ref):
@@ -276,24 +277,31 @@
         odd = (col & 1) == 1
         line = []
         for tab, place in ((tabs[0], (col + 1) >> 1), (tabs[1], col >> 1)):
-            hot = jnp.where(pair_iota == place, 1.0, 0.0).astype(BF16)
-            both = jnp.dot(tab[...], hot, preferred_element_type=F32)
-            line.append(both[0:high_rows] + both[high_rows:])
-        beyond = jnp.concatenate([halo[...]] * 2, axis=1)
-        even_line = line[0] + jnp.where(col == cols - 1, beyond, 0.0)
-        step_y = line[1] - even_line
+            at = (jnp.broadcast_to(place, (16, 256)) - sub16).astype(jnp.int16)
+            hot = [jnp.where(at == 16 * i, one16, zero16) for i in range(cols // 32)]
+            line.append(
+                jnp.dot(tab[...], jnp.concatenate(hot, axis=0), preferred_element_type=F32)
+            )
         frac_x = 0.5 + 0.45 * jnp.tanh(off_x)
         frac_y = 0.5 + 0.45 * jnp.tanh(off_y)
-        mixed = even_line + jnp.where(odd, 1.0 - frac_y, frac_y) * step_y
-        here, below = row_iota == row, row_iota == row + 1
-        grad_x = jnp.sum(
-            jnp.where(below, mixed, jnp.where(here, -mixed, 0.0)), axis=0, keepdims=True
-        )
-        grad_y = jnp.sum(
-            step_y * jnp.where(here, 1.0 - frac_x, jnp.where(below, frac_x, 0.0)),
-            axis=0,
-            keepdims=True,
-        )
+        blend = jnp.where(odd, 1.0 - frac_y, frac_y)
+        edge = jnp.broadcast_to(col == cols - 1, (8, 256))
+        row_at = jnp.broadcast_to(row, (8, 256)) - sub8
+        near, far = jnp.broadcast_to(1.0 - frac_x, (8, 256)), jnp.broadcast_to(frac_x, (8, 256))
+        sum_x, sum_y = jnp.zeros((8, 256), F32), jnp.zeros((8, 256), F32)
+        for i in range(0, rows + 8, 8):
+            even, odds = [
+                both[i : i + 8] + both[high_rows + i : high_rows + i + 8] for both in line
+            ]
+            beyond = jnp.concatenate([halo[i : i + 8, :]] * 2, axis=1)
+            even = jnp.where(edge, beyond, even)
+            step_y = odds - even
+            mixed = even + blend * step_y
+            here, below = row_at == i, row_at == i - 1
+            sum_x = sum_x + jnp.where(below, mixed, jnp.where(here, -mixed, 0.0))
+            sum_y = sum_y + step_y * jnp.where(here, near, jnp.where(below, far, 0.0))
+        grad_x = jnp.sum(sum_x, axis=0, keepdims=True)
+        grad_y = jnp.sum(sum_y, axis=0, keepdims=True)
         grad_y = jnp.where(odd, -grad_y, grad_y)
         moved_x = 0.5 + 0.45 * jnp.tanh(off_x - grad_x)
         moved_y = 0.5 + 0.45 * jnp.tanh(off_y - grad_y)
@@ -343,8 +351,9 @@
     )
     part_rows = 12 * cap + EDGE
     for k in range(n_cols):
-        outs[k][0 : part_rows - EDGE, :] = buf[k * part_rows : (k + 1) * part_rows - EDGE, :]
-        outs[k][part_rows - EDGE :, :] = w_ref[...] + v_ref[...]
+        out = outs[(n_cols - k) % n_cols]
+        out[0 : part_rows - EDGE, :] = buf[k * part_rows : (k + 1) * part_rows - EDGE, :]
+        out[part_rows - EDGE :, :] = w_ref[...] + v_ref[...]
 
 
 def again_kernel(rows, cols, blocks, cap, n_cols, *refs):
@@ -388,12 +397,12 @@
     )
     part_rows = 6 * cap + EDGE
     for k in range(n_cols):
-        outs[k][...] = buf[k * part_rows : (k + 1) * part_rows, :]
+        outs[(n_cols - k) % n_cols][...] = buf[k * part_rows : (k + 1) * part_rows, :]
     leave.wait()
 
 
 def deposit_blocks(rows, cols, cap, chunks, moves, masses, scratch, slots):
-    acc, beside, lhs_a, rhs_a, lhs_b, rhs_b = scratch
+    acc, beside = scratch
     counts = []
     for q in range(chunks):
         cells = masses[(2 * q + 1) * cap : (2 * q + 2) * cap, :]
@@ -405,8 +414,6 @@
         base = base + counts[q]
     for rank in range(2 * GROUP):
         slots[base + rank] = 2 * chunks * cap
-    lhs_b[...] = jnp.zeros(lhs_b.shape, BF16)
-    rhs_b[...] = jnp.zeros(rhs_b.shape, BF16)
     high_rows = table_height(rows)
     sub16 = lax.broadcasted_iota(I32, (16, 128), 0)
     sub8 = lax.broadcasted_iota(I32, (8, 128), 0)
@@ -415,8 +422,8 @@
     def relative(line, sub):
         return jnp.broadcast_to(line, sub.shape) - sub
 
-    def build(first_slot, lhs, rhs):
-        edges = []
+    def build(first_slot):
+        edges, left, right = [], ([], []), ([], [])
         for t in range(GROUP):
             at = slots[first_slot + t]
             move_x = moves[pl.ds(at, 1), :]
@@ -437,19 +444,19 @@
                     values.append(
                         [jnp.broadcast_to(x.astype(F32), (16, 128)).astype(BF16) for x in (one, two)]
                     )
+            tiles = [[], [], [], []]
             for i in range(high_rows // 16):
                 here, below = row_at == 16 * i, row_at == 16 * i - 1
                 for index, (one, two) in enumerate(values):
-                    at_row = (index % 2) * high_rows + 16 * i
-                    lhs[index // 2, t, at_row : at_row + 16, :] = jnp.where(
-                        here, one, jnp.where(below, two, zero16)
-                    )
+                    tiles[index].append(jnp.where(here, one, jnp.where(below, two, zero16)))
+            for parity in range(2):
+                left[parity].append(
+                    jnp.concatenate(tiles[2 * parity] + tiles[2 * parity + 1], axis=0)
+                )
             for parity, place in ((0, (col + 1) >> 1), (1, col >> 1)):
                 place_at = relative(place, sub16).astype(jnp.int16)
-                for i in range(cols // 32):
-                    rhs[parity, t, 16 * i : 16 * i + 16, :] = jnp.where(
-                        place_at == 16 * i, one16, zero16
-                    )
+                hot = [jnp.where(place_at == 16 * i, one16, zero16) for i in range(cols // 32)]
+                right[parity].append(jnp.concatenate(hot, axis=0))
         for i in range(rows // 8 + 1):
             total = beside[8 * i : 8 * i + 8, :]
             for row_at, first, second in edges:
@@ -457,25 +464,20 @@
                     row_at == 8 * i, first, jnp.where(row_at == 8 * i - 1, second, 0.0)
                 )
             beside[8 * i : 8 * i + 8, :] = total
-
-    def multiply(lhs, rhs):
         for parity in range(2):
-            one, two = [
-                jnp.concatenate([ref[parity, t] for t in range(GROUP)], axis=1) for ref in (lhs, rhs)
-            ]
             acc[parity] += lax.dot_general(
-                one, two, (((1,), (1,)), ((), ())), preferred_element_type=F32
+                jnp.concatenate(left[parity], axis=1),
+                jnp.concatenate(right[parity], axis=1),
+                (((1,), (1,)), ((), ())),
+                preferred_element_type=F32,
             )
 
     def step(g, carry):
-        multiply(lhs_b, rhs_b)
-        build(2 * g * GROUP, lhs_a, rhs_a)
-        multiply(lhs_a, rhs_a)
-        build((2 * g + 1) * GROUP, lhs_b, rhs_b)
+        for part in range(2):
+            build((2 * g + part) * GROUP)
         return carry
 
     lax.fori_loop(0, (base + 2 * GROUP - 1) // (2 * GROUP), step, 0)
-    multiply(lhs_b, rhs_b)
 
 
 def finish_grid(rows, cols, acc, beside, grid):
@@ -617,8 +619,8 @@
 
 
 def exchange_columns(outs):
-    came = {k: xor_permute(outs[k], "cols", k) for k in range(len(outs) - 1, 0, -1)}
-    return [outs[0]] + [came[k] for k in range(1, len(outs))]
+    came = [xor_permute(part, "cols", len(outs) - i) for i, part in enumerate(outs) if i > 0]
+    return [outs[0]] + came
 
 
 def exchange_rows(pieces, kinds, cap, extra_first, extra_second=None):
@@ -694,24 +696,18 @@
     high_rows = table_height(rows)
     acc_shape = (2, 2 * high_rows, cols // 2)
     beside_shape = (rows + 8, 128)
-    product_scratch = [
-        pltpu.VMEM((2, GROUP, 2 * high_rows, 128), BF16),
-        pltpu.VMEM((2, GROUP, cols // 2, 128), BF16),
-    ] * 2
 
     def part_rows_of(chunk_count):
         return 2 * cap * (chunk_count + 1)
 
     own_scratch = [
         pltpu.VMEM((part_rows_of(n_cols), 128), F32),
-        *product_scratch,
         pltpu.SMEM((n_cols * cap + 2 * GROUP,), I32),
     ]
     other_scratch = [
         pltpu.VMEM((part_rows_of(2 * n_cols), 128), F32),
         pltpu.VMEM(acc_shape, F32),
         pltpu.VMEM(beside_shape, F32),
-        *product_scratch,
         pltpu.SMEM((2 * n_cols * cap + 2 * GROUP,), I32),
     ]
     carried = (shape(*acc_shape), shape(*beside_shape))

time: 88.2 us -> 79.8 us (0.905)
  Pallas kernels: 24.9 us -> 13.1 us
  waiting for transfers between devices: 16.8 us -> 20.8 us
  starting transfers between devices: 45.5 us -> 44.5 us
    pallas_call x10, Pallas kernels: 24.9 us -> 13.1 us  [run(): call(*[pltpu.with_memory_space_constraint(x, pltpu.HBM if i in hbm_in els...]
    ppermute x6, waiting for transfers between devices: 3.12 us -> 7.98 us  [swap_both(): lax.ppermute(second, axis, pairs_b)]
    ppermute x6, starting transfers between devices: 28.5 us -> 24.2 us  [swap_both(): lax.ppermute(second, axis, pairs_b)]
    ppermute x6, starting transfers between devices: 4.61 us -> 7.76 us  [swap_both(): lax.ppermute(first, axis, pairs_a)]
    ppermute x8, waiting for transfers between devices: 11.3 us -> 9.17 us  [xor_permute(): lax.ppermute(value, axis, [(i, i ^ bit) for i in range(lax.axis_size(axis...]
    ppermute x1, waiting for transfers between devices: 2.42 us -> 3.61 us  [body(): lax.ppermute(beside, 'cols', [(i, i + 1) for i in range(n_cols - 1)])]
    ppermute x1, starting transfers between devices: 1.92 us -> 2.81 us  [body(): lax.ppermute(beside, 'cols', [(i, i + 1) for i in range(n_cols - 1)])]
    ppermute x1, starting transfers between devices: 4.72 us -> 3.84 us  [body(): below = lax.ppermute(below, 'rows', [(i, i + 1) for i in range(n_rows - 1)])]
  transfers between devices with their start and end apart: 22 -> 22, of which waited for: 13 -> 13; matrix products, arithmetic and copies ran while one was open for 0% -> 0% of each run, Pallas kernels for 5% -> 0%
where the time goes in v1:
time: 79.8 us; the launch traced here: 79.3 us
  starting transfers between devices  44.5 us (56%)
  waiting for transfers between devices  20.8 us (26%)
  Pallas kernels  13.1 us (16%)
  between operations  0.83 us (1%)
    ppermute x6, starting transfers between devices, swap_both(): lax.ppermute(second, axis, pairs_b)  24.2 us
    pallas_call x10, Pallas kernels, run(): call(*[pltpu.with_memory_space_constraint(x, pltpu.HBM if i in hbm_in els...  13.1 us
    ppermute x8, waiting for transfers between devices, xor_permute(): lax.ppermute(value, axis, [(i, i ^ bit) for i in range(lax.axis_size(axis...  9.17 us
    ppermute x6, waiting for transfers between devices, swap_both(): lax.ppermute(second, axis, pairs_b)  7.98 us
    ppermute x6, starting transfers between devices, swap_both(): lax.ppermute(first, axis, pairs_a)  7.76 us
    ppermute x8, starting transfers between devices, xor_permute(): lax.ppermute(value, axis, [(i, i ^ bit) for i in range(lax.axis_size(axis...  5.81 us
    ppermute x1, starting transfers between devices, body(): below = lax.ppermute(below, 'rows', [(i, i + 1) for i in range(n_rows - 1)])  3.84 us
    ppermute x1, waiting for transfers between devices, body(): lax.ppermute(beside, 'cols', [(i, i + 1) for i in range(n_cols - 1)])  3.61 us
  transfers between devices with their start and end apart: 22, of which 13 were waited for; matrix products, arithmetic and copies ran while one was open for 0% of the time, Pallas kernels for 0%

profile of v1, /device:TPU:11, one launch (start us, length us, event | category | flops | bytes accessed | tf_op | source)
XLA Modules:
  0.0 79.3 jit_solution(8236766590061853823)
XLA Ops:
  0.6 1.2 %shard_map.86 = (f32[128,512]{1,0:T(8,128)S(1)}, f32[128,512]{1,0:T(8,128)S(1)}, f32[32,128]{1,0:T(8,128)S(1)}, s32[32,128]{1,0:T(8,128)S(1)}, f32[2,4096]{1,0:T...) custom-call(f32[128,512]{1,0:T(8,128)} %refs_0_.1, ...), custom_call_target="tpu_custom_call" | custom-call | tf_op jit(solution)/shard_map/pallas_call | solution.py:53
  1.8 0.7 collective-permute-start
  2.6 3.0 %collective-permute-start.1 = (f32[16,512]{1,0:T(8,128)S(1)}, f32[16,512]{1,0:T(8,128)S(1)}, u32[]{:S(2)}, u32[]{:S(2)}) collective-permute-start(f32[16,512]{1,0:T(8,128)S(1)} %get-tuple-element.47), channel_id=1, source_target_pairs={{4,8},{8,4},{12,16},{16,12},{20,24},{24,20},{5,9},{9,5},{13,17},{1... | collective-permute-start | bytes 98312 | tf_op jit(solution)/shard_map/ppermute | solution.py:28
  5.6 0.3 collective-permute-start.2
  5.9 2.5 %collective-permute-done.2.v_ref = f32[8,128]{1,0:T(8,128)S(1)} collective-permute-done((f32[8,128]{1,0:T(8,128)S(1)}, f32[8,128]{1,0:T(8,128)S(1)}, u32[]{:S(2)}, u32[]{:S(2)}) %collective-permute-start.2) | collective-permute-done | bytes 4128 | tf_op jit(solution)/shard_map/ppermute | solution.py:32
  8.4 0.0 collective-permute-done.a_ref
  8.4 0.3 collective-permute-done.1.b_ref
  8.7 0.2 shard_map.87
  8.9 0.2 collective-permute-start.3
  9.1 4.3 %collective-permute-start.4 = (f32[16,256]{1,0:T(8,128)S(1)}, f32[16,256]{1,0:T(8,128)S(1)}, u32[]{:S(2)}, u32[]{:S(2)}) collective-permute-start(f32[16,256]{1,0:T(8,128)S(1)} %get-tuple-element.52), channel_id=1, source_target_pairs={{1,2},{2,1},{5,6},{6,5},{9,10},{10,9},{13,14},{14,13},{17,18},{18,... | collective-permute-start | bytes 49160 | tf_op jit(solution)/shard_map/ppermute | solution.py:28
  13.4 0.1 collective-permute-start.5
  13.5 2.4 %collective-permute-done.5.refs_5_ = f32[8,128]{1,0:T(8,128)S(1)} collective-permute-done((f32[8,128]{1,0:T(8,128)S(1)}, f32[8,128]{1,0:T(8,128)S(1)}, u32[]{:S(2)}, u32[]{:S(2)}) %collective-permute-start.5) | collective-permute-done | bytes 4128 | tf_op jit(solution)/shard_map/ppermute | solution.py:32
  15.9 0.0 collective-permute-done.3.refs_2_
  15.9 0.0 collective-permute-done.4.refs_3_
  15.9 4.1 %shard_map.88 = (f32[104,128]{1,0:T(8,128)S(1)}, f32[104,128]{1,0:T(8,128)S(1)}, f32[104,128]{1,0:T(8,128)S(1)}, f32[104,128]{1,0:T(8,128)S(1)}, f32[160,640]{1,0:T(8,128)S(1)}, /*index=5*/f32[160,640]{1,0:T(8,128)S(1)}) custom-call(f32[160,640]{1,0:T(8,128)S(1)} %get-tuple-element.49.refs_0_, f32[160,640]{1,0:T(8,128)S(1)} %get-tuple-element.50.refs_1_, ...), custom_call_target="tpu_custom_call" | custom-call | tf_op jit(solution)/shard_map/pallas_call | solution.py:53
  20.0 0.1 collective-permute-start.6
  20.1 0.0 collective-permute-start.7
  20.2 2.6 %collective-permute-start.8 = (f32[104,128]{1,0:T(8,128)S(1)}, f32[104,128]{1,0:T(8,128)S(1)}, u32[]{:S(2)}, u32[]{:S(2)}) collective-permute-start(f32[104,128]{1,0:T(8,128)S(1)} %get-tuple-element.63), channel_id=1, source_target_pairs={{0,1},{1,0},{2,3},{3,2},{4,5},{5,4},{6,7},{7,6},{8,9},{9,8},{10,11... | collective-permute-start | bytes 159752 | tf_op jit(solution)/shard_map/ppermute | solution.py:32
  22.7 1.5 %collective-permute-done.6.refs_1_ = f32[104,128]{1,0:T(8,128)S(1)} collective-permute-done((f32[104,128]{1,0:T(8,128)S(1)}, f32[104,128]{1,0:T(8,128)S(1)}, u32[]{:S(2)}, u32[]{:S(2)}) %collective-permute-start.6) | collective-permute-done | bytes 53280 | tf_op jit(solution)/shard_map/ppermute | solution.py:32
  24.2 0.9 %collective-permute-done.8.refs_3_ = f32[104,128]{1,0:T(8,128)S(1)} collective-permute-done((f32[104,128]{1,0:T(8,128)S(1)}, f32[104,128]{1,0:T(8,128)S(1)}, u32[]{:S(2)}, u32[]{:S(2)}) %collective-permute-start.8) | collective-permute-done | bytes 53280 | tf_op jit(solution)/shard_map/ppermute | solution.py:32
  25.1 3.0 %collective-permute-start.9 = (f32[136,128]{1,0:T(8,128)S(1)}, f32[136,128]{1,0:T(8,128)S(1)}, u32[]{:S(2)}, u32[]{:S(2)}) collective-permute-start(f32[136,128]{1,0:T(8,128)S(1)} %get-tuple-element.88), channel_id=1, source_target_pairs={{0,4},{4,0},{8,12},{12,8},{16,20},{20,16},{24,28},{28,24},{1,5},{5... | collective-permute-start | bytes 208904 | tf_op jit(solution)/shard_map/ppermute | solution.py:28
  28.2 3.9 %collective-permute-start.10 = (f32[128,128]{1,0:T(8,128)S(1)}, f32[128,128]{1,0:T(8,128)S(1)}, u32[]{:S(2)}, u32[]{:S(2)}) collective-permute-start(f32[128,128]{1,0:T(8,128)S(1)} %pad_maximum_fusion), channel_id=1, source_target_pairs={{4,8},{8,4},{12,16},{16,12},{20,24},{24,20},{5,9},{9,5},{13,17},{1... | collective-permute-start | bytes 196616 | tf_op jit(solution)/shard_map/ppermute | solution.py:28
  32.1 0.2 shard_map.89
  32.3 2.4 %collective-permute-done.10.refs_1_ = f32[128,128]{1,0:T(8,128)S(1)} collective-permute-done((f32[128,128]{1,0:T(8,128)S(1)}, f32[128,128]{1,0:T(8,128)S(1)}, u32[]{:S(2)}, u32[]{:S(2)}) %collective-permute-start.10) | collective-permute-done | bytes 65568 | tf_op jit(solution)/shard_map/ppermute | solution.py:28
  34.7 1.1 %shard_map.90 = (f32[136,640]{1,0:T(8,128)S(1)}, f32[8,640]{1,0:T(8,128)S(1)}, f32[8,640]{1,0:T(8,128)S(1)}, f32[144,128]{1,0:T(8,128)S(1)}, f32[8,128]{1,0:T(8,128)S(1)}) custom-call(f32[136,128]{1,0:T(8,128)S(1)} %collective-permute-done.9.refs_0_, f32[128,128]{1,0:T(8,128)S(1)} %collective-permute-done.10.refs_1_, ...), custom_call_target="tpu_custom_call" | custom-call | tf_op jit(solution)/shard_map/pallas_call | solution.py:53
  35.8 0.1 collective-permute-start.11
  35.9 5.9 %collective-permute-start.12 = (f32[8,640]{1,0:T(8,128)S(1)}, f32[8,640]{1,0:T(8,128)S(1)}, u32[]{:S(2)}, u32[]{:S(2)}) collective-permute-start(f32[8,640]{1,0:T(8,128)S(1)} %get-tuple-element.68), channel_id=1, source_target_pairs={{4,8},{8,4},{12,16},{16,12},{20,24},{24,20},{5,9},{9,5},{13,17},{1... | collective-permute-start | bytes 61448 | tf_op jit(solution)/shard_map/ppermute | solution.py:28
  41.8 1.5 %collective-permute-done.12.b_ref = f32[8,640]{1,0:T(8,128)S(1)} collective-permute-done((f32[8,640]{1,0:T(8,128)S(1)}, f32[8,640]{1,0:T(8,128)S(1)}, u32[]{:S(2)}, u32[]{:S(2)}) %collective-permute-start.12) | collective-permute-done | bytes 20512 | tf_op jit(solution)/shard_map/ppermute | solution.py:28
  43.3 0.1 shard_map.91
  43.5 1.5 %collective-permute-start.13 = (f32[16,256]{1,0:T(8,128)S(1)}, f32[16,256]{1,0:T(8,128)S(1)}, u32[]{:S(2)}, u32[]{:S(2)}) collective-permute-start(f32[16,256]{1,0:T(8,128)S(1)} %get-tuple-element.70), channel_id=1, source_target_pairs={{0,1},{1,0},{2,3},{3,2},{4,5},{5,4},{6,7},{7,6},{8,9},{9,8},{10,11... | collective-permute-start | bytes 49160 | tf_op jit(solution)/shard_map/ppermute | solution.py:28
  44.9 2.3 %collective-permute-start.14 = (f32[16,256]{1,0:T(8,128)S(1)}, f32[16,256]{1,0:T(8,128)S(1)}, u32[]{:S(2)}, u32[]{:S(2)}) collective-permute-start(f32[16,256]{1,0:T(8,128)S(1)} %get-tuple-element.71), channel_id=1, source_target_pairs={{1,2},{2,1},{5,6},{6,5},{9,10},{10,9},{13,14},{14,13},{17,18},{18,... | collective-permute-start | bytes 49160 | tf_op jit(solution)/shard_map/ppermute | solution.py:28
  47.3 2.1 %collective-permute-done.14.refs_4_ = f32[16,256]{1,0:T(8,128)S(1)} collective-permute-done((f32[16,256]{1,0:T(8,128)S(1)}, f32[16,256]{1,0:T(8,128)S(1)}, u32[]{:S(2)}, u32[]{:S(2)}) %collective-permute-start.14) | collective-permute-done | bytes 16416 | tf_op jit(solution)/shard_map/ppermute | solution.py:28
  49.4 4.2 %shard_map.92 = (f32[56,128]{1,0:T(8,128)S(1)}, f32[56,128]{1,0:T(8,128)S(1)}, f32[56,128]{1,0:T(8,128)S(1)}, f32[56,128]{1,0:T(8,128)S(1)}, f32[128,512]{1,0:T(8,128)}, /*index=5*/f32[128,512]{1,0:T(8,128)S(1)}) custom-call(f32[160,640]{1,0:T(8,128)S(1)} %get-tuple-element.58.refs_0_, f32[160,640]{1,0:T(8,128)S(1)} %get-tuple-element.59.refs_1_, ...), custom_call_target="tpu_custom_call" | custom-call | tf_op jit(solution)/shard_map/pallas_call | solution.py:53
  53.6 0.5 collective-permute-start.15
  54.1 0.2 collective-permute-start.16
  54.3 2.0 %collective-permute-start.17 = (f32[56,128]{1,0:T(8,128)S(1)}, f32[56,128]{1,0:T(8,128)S(1)}, u32[]{:S(2)}, u32[]{:S(2)}) collective-permute-start(f32[56,128]{1,0:T(8,128)S(1)} %get-tuple-element.77), channel_id=1, source_target_pairs={{0,1},{1,0},{2,3},{3,2},{4,5},{5,4},{6,7},{7,6},{8,9},{9,8},{10,11... | collective-permute-start | bytes 86024 | tf_op jit(solution)/shard_map/ppermute | solution.py:32
  56.3 0.4 collective-permute-done.15.refs_1_
  56.7 1.0 %collective-permute-done.16.refs_2_ = f32[56,128]{1,0:T(8,128)S(1)} collective-permute-done((f32[56,128]{1,0:T(8,128)S(1)}, f32[56,128]{1,0:T(8,128)S(1)}, u32[]{:S(2)}, u32[]{:S(2)}) %collective-permute-start.16) | collective-permute-done | bytes 28704 | tf_op jit(solution)/shard_map/ppermute | solution.py:32
  57.8 0.4 collective-permute-done.17.refs_3_
  58.2 2.2 %collective-permute-start.18 = (f32[72,128]{1,0:T(8,128)S(1)}, f32[72,128]{1,0:T(8,128)S(1)}, u32[]{:S(2)}, u32[]{:S(2)}) collective-permute-start(f32[72,128]{1,0:T(8,128)S(1)} %constant_dynamic-update-slice_fusion.5), channel_id=1, source_target_pairs={{0,4},{4,0},{8,12},{12,8},{16,20},{20,16},{24,28},{28,24},{1,5},{5... | collective-permute-start | bytes 110600 | tf_op jit(solution)/shard_map/ppermute | solution.py:28
  60.4 4.8 %collective-permute-start.19 = (f32[72,128]{1,0:T(8,128)S(1)}, f32[72,128]{1,0:T(8,128)S(1)}, u32[]{:S(2)}, u32[]{:S(2)}) collective-permute-start(f32[72,128]{1,0:T(8,128)S(1)} %get-tuple-element.86), channel_id=1, source_target_pairs={{4,8},{8,4},{12,16},{16,12},{20,24},{24,20},{5,9},{9,5},{13,17},{1... | collective-permute-start | bytes 110600 | tf_op jit(solution)/shard_map/ppermute | solution.py:28
  65.2 0.2 shard_map.93
  65.4 1.6 %collective-permute-done.19.refs_1_ = f32[72,128]{1,0:T(8,128)S(1)} collective-permute-done((f32[72,128]{1,0:T(8,128)S(1)}, f32[72,128]{1,0:T(8,128)S(1)}, u32[]{:S(2)}, u32[]{:S(2)}) %collective-permute-start.19) | collective-permute-done | bytes 36896 | tf_op jit(solution)/shard_map/ppermute | solution.py:28
  67.1 1.1 %shard_map.94 = (f32[136,640]{1,0:T(8,128)S(1)}, f32[8,512]{1,0:T(8,128)S(1)}, f32[8,128]{1,0:T(8,128)S(1)}) custom-call(f32[72,128]{1,0:T(8,128)S(1)} %collective-permute-done.18.refs_0_, f32[72,128]{1,0:T(8,128)S(1)} %collective-permute-done.19.refs_1_, f32[2,288,256]{2,1,0:T(8,128)S(1)} %get-tuple-element.79.refs_2_, ...), custom_call_target="tpu_custom_call" | custom-call | tf_op jit(solution)/shard_map/pallas_call | solution.py:53
  68.2 3.8 %collective-permute-start.20 = (f32[8,512]{1,0:T(8,128)S(1)}, f32[8,512]{1,0:T(8,128)S(1)}, u32[]{:S(2)}, u32[]{:S(2)}) collective-permute-start(f32[8,512]{1,0:T(8,128)S(1)} %get-tuple-element.84), channel_id=1, source_target_pairs={{0,4},{4,8},{8,12},{12,16},{16,20},{20,24},{24,28},{1,5},{5,9},{9,... | collective-permute-start | bytes 49160 | tf_op jit(solution)/shard_map/ppermute | solution.py:777
  72.0 2.8 %collective-permute-start.21 = (f32[8,128]{1,0:T(8,128)S(1)}, f32[8,128]{1,0:T(8,128)S(1)}, u32[]{:S(2)}, u32[]{:S(2)}) collective-permute-start(f32[8,128]{1,0:T(8,128)S(1)} %get-tuple-element.85), channel_id=1, source_target_pairs={{0,1},{1,2},{2,3},{4,5},{5,6},{6,7},{8,9},{9,10},{10,11},{12,13},{... | collective-permute-start | bytes 12296 | tf_op jit(solution)/shard_map/ppermute | solution.py:778
  74.8 3.6 %collective-permute-done.21.col_in = f32[8,128]{1,0:T(8,128)S(1)} collective-permute-done((f32[8,128]{1,0:T(8,128)S(1)}, f32[8,128]{1,0:T(8,128)S(1)}, u32[]{:S(2)}, u32[]{:S(2)}) %collective-permute-start.21) | collective-permute-done | bytes 4128 | tf_op jit(solution)/shard_map/ppermute | solution.py:778
  78.5 0.8 %shard_map.95 = f32[128,512]{1,0:T(8,128)} custom-call(f32[136,640]{1,0:T(8,128)S(1)} %get-tuple-element.82.g_ref, f32[128,512]{1,0:T(8,128)S(1)} %get-tuple-element.83.m_ref, f32[8,512]{1,0:T(8,128)S(1)} %collective-permute-done.20.row_in, f32[8,128]{1,0:T(8,128)S(1)} %collective-permute-done.21.col_in, f32[8,128]{1,0:T(8,128)S(1)} %get-tuple-element.72.refs_5_.total_ref), custom_call_target="tpu_custom_call" | custom-call | tf_op jit(solution)/shard_map/pallas_call | solution.py:53
  (18 shorter events, 0.1 us)
Async XLA Ops:
  1.8 6.6 %collective-permute-start = (f32[16,512]{1,0:T(8,128)S(1)}, f32[16,512]{1,0:T(8,128)S(1)}, u32[]{:S(2)}, u32[]{:S(2)}) collective-permute-start(f32[16,512]{1,0:T(8,128)S(1)} %get-tuple-element.46), channel_id=1, source_target_pairs={{0,4},{4,0},{8,12},{12,8},{16,20},{20,16},{24,28},{28,24},{1,5},{5... | collective-permute-start | bytes 98312 | tf_op jit(solution)/shard_map/ppermute | solution.py:28
  2.6 6.1 %collective-permute-start.1 = (f32[16,512]{1,0:T(8,128)S(1)}, f32[16,512]{1,0:T(8,128)S(1)}, u32[]{:S(2)}, u32[]{:S(2)}) collective-permute-start(f32[16,512]{1,0:T(8,128)S(1)} %get-tuple-element.47), channel_id=1, source_target_pairs={{4,8},{8,4},{12,16},{16,12},{20,24},{24,20},{5,9},{9,5},{13,17},{1... | collective-permute-start | bytes 98312 | tf_op jit(solution)/shard_map/ppermute | solution.py:28
  5.6 2.8 %collective-permute-start.2 = (f32[8,128]{1,0:T(8,128)S(1)}, f32[8,128]{1,0:T(8,128)S(1)}, u32[]{:S(2)}, u32[]{:S(2)}) collective-permute-start(f32[8,128]{1,0:T(8,128)S(1)} %get-tuple-element.48.w_ref), channel_id=1, source_target_pairs={{0,8},{4,12},{8,0},{12,4},{16,24},{20,28},{24,16},{28,20},{1,9},{5... | collective-permute-start | bytes 12296 | tf_op jit(solution)/shard_map/ppermute | solution.py:32
  8.9 7.1 %collective-permute-start.3 = (f32[16,256]{1,0:T(8,128)S(1)}, f32[16,256]{1,0:T(8,128)S(1)}, u32[]{:S(2)}, u32[]{:S(2)}) collective-permute-start(f32[16,256]{1,0:T(8,128)S(1)} %get-tuple-element.51), channel_id=1, source_target_pairs={{0,1},{1,0},{2,3},{3,2},{4,5},{5,4},{6,7},{7,6},{8,9},{9,8},{10,11... | collective-permute-start | bytes 49160 | tf_op jit(solution)/shard_map/ppermute | solution.py:28
  9.1 6.9 %collective-permute-start.4 = (f32[16,256]{1,0:T(8,128)S(1)}, f32[16,256]{1,0:T(8,128)S(1)}, u32[]{:S(2)}, u32[]{:S(2)}) collective-permute-start(f32[16,256]{1,0:T(8,128)S(1)} %get-tuple-element.52), channel_id=1, source_target_pairs={{1,2},{2,1},{5,6},{6,5},{9,10},{10,9},{13,14},{14,13},{17,18},{18,... | collective-permute-start | bytes 49160 | tf_op jit(solution)/shard_map/ppermute | solution.py:28
  13.4 2.5 %collective-permute-start.5 = (f32[8,128]{1,0:T(8,128)S(1)}, f32[8,128]{1,0:T(8,128)S(1)}, u32[]{:S(2)}, u32[]{:S(2)}) collective-permute-start(f32[8,128]{1,0:T(8,128)S(1)} %get-tuple-element.53.refs_4_), channel_id=1, source_target_pairs={{0,16},{4,20},{8,24},{12,28},{16,0},{20,4},{24,8},{28,12},{1,17},{... | collective-permute-start | bytes 12296 | tf_op jit(solution)/shard_map/ppermute | solution.py:32
  20.0 4.2 %collective-permute-start.6 = (f32[104,128]{1,0:T(8,128)S(1)}, f32[104,128]{1,0:T(8,128)S(1)}, u32[]{:S(2)}, u32[]{:S(2)}) collective-permute-start(f32[104,128]{1,0:T(8,128)S(1)} %get-tuple-element.61), channel_id=1, source_target_pairs={{0,3},{1,2},{2,1},{3,0},{4,7},{5,6},{6,5},{7,4},{8,11},{9,10},{10,... | collective-permute-start | bytes 159752 | tf_op jit(solution)/shard_map/ppermute | solution.py:32
  20.1 4.1 %collective-permute-start.7 = (f32[104,128]{1,0:T(8,128)S(1)}, f32[104,128]{1,0:T(8,128)S(1)}, u32[]{:S(2)}, u32[]{:S(2)}) collective-permute-start(f32[104,128]{1,0:T(8,128)S(1)} %get-tuple-element.62), channel_id=1, source_target_pairs={{0,2},{1,3},{2,0},{3,1},{4,6},{5,7},{6,4},{7,5},{8,10},{9,11},{10,... | collective-permute-start | bytes 159752 | tf_op jit(solution)/shard_map/ppermute | solution.py:32
  20.2 4.9 %collective-permute-start.8 = (f32[104,128]{1,0:T(8,128)S(1)}, f32[104,128]{1,0:T(8,128)S(1)}, u32[]{:S(2)}, u32[]{:S(2)}) collective-permute-start(f32[104,128]{1,0:T(8,128)S(1)} %get-tuple-element.63), channel_id=1, source_target_pairs={{0,1},{1,0},{2,3},{3,2},{4,5},{5,4},{6,7},{7,6},{8,9},{9,8},{10,11... | collective-permute-start | bytes 159752 | tf_op jit(solution)/shard_map/ppermute | solution.py:32
  25.1 9.6 %collective-permute-start.9 = (f32[136,128]{1,0:T(8,128)S(1)}, f32[136,128]{1,0:T(8,128)S(1)}, u32[]{:S(2)}, u32[]{:S(2)}) collective-permute-start(f32[136,128]{1,0:T(8,128)S(1)} %get-tuple-element.88), channel_id=1, source_target_pairs={{0,4},{4,0},{8,12},{12,8},{16,20},{20,16},{24,28},{28,24},{1,5},{5... | collective-permute-start | bytes 208904 | tf_op jit(solution)/shard_map/ppermute | solution.py:28
  28.2 6.5 %collective-permute-start.10 = (f32[128,128]{1,0:T(8,128)S(1)}, f32[128,128]{1,0:T(8,128)S(1)}, u32[]{:S(2)}, u32[]{:S(2)}) collective-permute-start(f32[128,128]{1,0:T(8,128)S(1)} %pad_maximum_fusion), channel_id=1, source_target_pairs={{4,8},{8,4},{12,16},{16,12},{20,24},{24,20},{5,9},{9,5},{13,17},{1... | collective-permute-start | bytes 196616 | tf_op jit(solution)/shard_map/ppermute | solution.py:28
  35.8 5.9 %collective-permute-start.11 = (f32[8,640]{1,0:T(8,128)S(1)}, f32[8,640]{1,0:T(8,128)S(1)}, u32[]{:S(2)}, u32[]{:S(2)}) collective-permute-start(f32[8,640]{1,0:T(8,128)S(1)} %get-tuple-element.67), channel_id=1, source_target_pairs={{0,4},{4,0},{8,12},{12,8},{16,20},{20,16},{24,28},{28,24},{1,5},{5... | collective-permute-start | bytes 61448 | tf_op jit(solution)/shard_map/ppermute | solution.py:28
  35.9 7.4 %collective-permute-start.12 = (f32[8,640]{1,0:T(8,128)S(1)}, f32[8,640]{1,0:T(8,128)S(1)}, u32[]{:S(2)}, u32[]{:S(2)}) collective-permute-start(f32[8,640]{1,0:T(8,128)S(1)} %get-tuple-element.68), channel_id=1, source_target_pairs={{4,8},{8,4},{12,16},{16,12},{20,24},{24,20},{5,9},{9,5},{13,17},{1... | collective-permute-start | bytes 61448 | tf_op jit(solution)/shard_map/ppermute | solution.py:28
  43.5 3.8 %collective-permute-start.13 = (f32[16,256]{1,0:T(8,128)S(1)}, f32[16,256]{1,0:T(8,128)S(1)}, u32[]{:S(2)}, u32[]{:S(2)}) collective-permute-start(f32[16,256]{1,0:T(8,128)S(1)} %get-tuple-element.70), channel_id=1, source_target_pairs={{0,1},{1,0},{2,3},{3,2},{4,5},{5,4},{6,7},{7,6},{8,9},{9,8},{10,11... | collective-permute-start | bytes 49160 | tf_op jit(solution)/shard_map/ppermute | solution.py:28
  44.9 4.5 %collective-permute-start.14 = (f32[16,256]{1,0:T(8,128)S(1)}, f32[16,256]{1,0:T(8,128)S(1)}, u32[]{:S(2)}, u32[]{:S(2)}) collective-permute-start(f32[16,256]{1,0:T(8,128)S(1)} %get-tuple-element.71), channel_id=1, source_target_pairs={{1,2},{2,1},{5,6},{6,5},{9,10},{10,9},{13,14},{14,13},{17,18},{18,... | collective-permute-start | bytes 49160 | tf_op jit(solution)/shard_map/ppermute | solution.py:28
  53.6 3.1 %collective-permute-start.15 = (f32[56,128]{1,0:T(8,128)S(1)}, f32[56,128]{1,0:T(8,128)S(1)}, u32[]{:S(2)}, u32[]{:S(2)}) collective-permute-start(f32[56,128]{1,0:T(8,128)S(1)} %get-tuple-element.75), channel_id=1, source_target_pairs={{0,3},{1,2},{2,1},{3,0},{4,7},{5,6},{6,5},{7,4},{8,11},{9,10},{10,... | collective-permute-start | bytes 86024 | tf_op jit(solution)/shard_map/ppermute | solution.py:32
  54.1 3.6 %collective-permute-start.16 = (f32[56,128]{1,0:T(8,128)S(1)}, f32[56,128]{1,0:T(8,128)S(1)}, u32[]{:S(2)}, u32[]{:S(2)}) collective-permute-start(f32[56,128]{1,0:T(8,128)S(1)} %get-tuple-element.76), channel_id=1, source_target_pairs={{0,2},{1,3},{2,0},{3,1},{4,6},{5,7},{6,4},{7,5},{8,10},{9,11},{10,... | collective-permute-start | bytes 86024 | tf_op jit(solution)/shard_map/ppermute | solution.py:32
  54.3 3.9 %collective-permute-start.17 = (f32[56,128]{1,0:T(8,128)S(1)}, f32[56,128]{1,0:T(8,128)S(1)}, u32[]{:S(2)}, u32[]{:S(2)}) collective-permute-start(f32[56,128]{1,0:T(8,128)S(1)} %get-tuple-element.77), channel_id=1, source_target_pairs={{0,1},{1,0},{2,3},{3,2},{4,5},{5,4},{6,7},{7,6},{8,9},{9,8},{10,11... | collective-permute-start | bytes 86024 | tf_op jit(solution)/shard_map/ppermute | solution.py:32
  58.2 7.2 %collective-permute-start.18 = (f32[72,128]{1,0:T(8,128)S(1)}, f32[72,128]{1,0:T(8,128)S(1)}, u32[]{:S(2)}, u32[]{:S(2)}) collective-permute-start(f32[72,128]{1,0:T(8,128)S(1)} %constant_dynamic-update-slice_fusion.5), channel_id=1, source_target_pairs={{0,4},{4,0},{8,12},{12,8},{16,20},{20,16},{24,28},{28,24},{1,5},{5... | collective-permute-start | bytes 110600 | tf_op jit(solution)/shard_map/ppermute | solution.py:28
  60.4 6.6 %collective-permute-start.19 = (f32[72,128]{1,0:T(8,128)S(1)}, f32[72,128]{1,0:T(8,128)S(1)}, u32[]{:S(2)}, u32[]{:S(2)}) collective-permute-start(f32[72,128]{1,0:T(8,128)S(1)} %get-tuple-element.86), channel_id=1, source_target_pairs={{4,8},{8,4},{12,16},{16,12},{20,24},{24,20},{5,9},{9,5},{13,17},{1... | collective-permute-start | bytes 110600 | tf_op jit(solution)/shard_map/ppermute | solution.py:28
  68.2 10.3 %collective-permute-start.20 = (f32[8,512]{1,0:T(8,128)S(1)}, f32[8,512]{1,0:T(8,128)S(1)}, u32[]{:S(2)}, u32[]{:S(2)}) collective-permute-start(f32[8,512]{1,0:T(8,128)S(1)} %get-tuple-element.84), channel_id=1, source_target_pairs={{0,4},{4,8},{8,12},{12,16},{16,20},{20,24},{24,28},{1,5},{5,9},{9,... | collective-permute-start | bytes 49160 | tf_op jit(solution)/shard_map/ppermute | solution.py:777
  72.0 6.4 %collective-permute-start.21 = (f32[8,128]{1,0:T(8,128)S(1)}, f32[8,128]{1,0:T(8,128)S(1)}, u32[]{:S(2)}, u32[]{:S(2)}) collective-permute-start(f32[8,128]{1,0:T(8,128)S(1)} %get-tuple-element.85), channel_id=1, source_target_pairs={{0,1},{1,2},{2,3},{4,5},{5,6},{6,7},{8,9},{9,10},{10,11},{12,13},{... | collective-permute-start | bytes 12296 | tf_op jit(solution)/shard_map/ppermute | solution.py:778

commit v2 on v1

--- a/solution.py
+++ b/solution.py
@@ -90,7 +90,7 @@
 
 def start_kernel(rows, count, *refs):
     sources, copies = refs[:count], refs[count : 2 * count]
-    sa_ref, sb_ref, sum_ref, sems = refs[2 * count :]
+    sa_ref, sb_ref, sems = refs[2 * count :]
     moves = [
         pltpu.make_async_copy(src, dst, sems.at[i])
         for i, (src, dst) in enumerate(zip(sources, copies))
@@ -107,13 +107,13 @@
         sa_ref[part, :] = pick(row_even, south_going, north_going)
         sb_ref[part, :] = pick(row_even, north_going, south_going)
     total = jnp.sum(jnp.sum(wts[...], axis=0, keepdims=True), axis=1, keepdims=True)
-    sum_ref[...] = jnp.broadcast_to(total, sum_ref.shape)
+    sa_ref[2 * EDGE :, :] = jnp.broadcast_to(total, (EDGE, sa_ref.shape[1]))
 
 
 def start_mid_kernel(
-    rows, cols, u_ref, m_ref, a_ref, b_ref, w_ref, v_ref, ue_ref, me_ref, ca_ref, cb_ref, sum_ref
+    rows, cols, u_ref, m_ref, a_ref, b_ref, s_ref, ue_ref, me_ref, ca_ref, cb_ref, sum_ref
 ):
-    sum_ref[...] = w_ref[...] + v_ref[...]
+    sum_ref[...] = s_ref[2 * EDGE :, 0:128] + a_ref[2 * EDGE :, 0:128]
     row_even = lax.axis_index("rows") % 2 == 0
     col_even = lax.axis_index("cols") % 2 == 0
     for index, (src, dst) in enumerate(((u_ref, ue_ref), (m_ref, me_ref))):
@@ -134,7 +134,7 @@
     return jnp.concatenate([right, jnp.zeros((128 - 2 * EDGE, width), F32), left], axis=0)
 
 
-def hjb_sweep(rows, cols, ua, ub, m):
+def hjb_sweep(rows, cols, ua, ub, m, between):
     wide = cols + 128
     tiles = wide // 128
     n_rows, n_cols = lax.axis_size("rows"), lax.axis_size("cols")
@@ -150,6 +150,8 @@
         return [src[i : i + 8, t * 128 : (t + 1) * 128] for t in range(tiles)]
 
     for step in range(HJB_STEPS):
+        if step == HJB_STEPS // 2:
+            between()
         start, stop = PAD - 8, PAD + rows + 8
         here = strip(start)
         fell = [pltpu.roll(x, 1, 0) for x in here]
@@ -235,17 +237,13 @@
         )
 
 
-def sample_moves(
-    rows, cols, blocks, cap, first, tabs, halo, starts, offs, wts, ends, dest, buf, slot_row,
-    corner_row, counter
-):
+def fill_slots(rows, blocks, cap, first, dest, slot_row, corner_row, counter):
     n_cols = lax.axis_size("cols")
     my_row, my_col = lax.axis_index("rows"), lax.axis_index("cols")
     n_rows = lax.axis_size("rows")
     kinds = 4 if first else 2
     part_rows = 3 * kinds * cap + EDGE
     spare_row = n_cols * part_rows
-    buf[...] = jnp.zeros(buf.shape, F32)
     for i in range(3 * n_cols):
         counter[i] = 0
     for b in range(blocks):
@@ -261,6 +259,11 @@
             row = ((column + 1) ^ my_col) * part_rows + 3 * kinds * cap + section
             corner_row[b] = jnp.where(goes, row, spare_row)
 
+
+def sample_moves(
+    rows, cols, blocks, cap, first, tabs, halo, starts, offs, wts, ends, buf, slot_row, corner_row
+):
+    buf[...] = jnp.zeros(buf.shape, F32)
     high_rows = table_height(rows)
     sub16 = lax.broadcasted_iota(I32, (16, 256), 0)
     sub8 = lax.broadcasted_iota(I32, (8, 256), 0)
@@ -324,10 +327,10 @@
 def first_kernel(
     rows, cols, blocks, cap, n_cols, *refs
 ):
-    (ue_in, me_in, ra_ref, rb_ref, w_ref, v_ref, starts, offs, wts, ends, dest_hbm) = refs[:11]
-    outs = refs[11 : 11 + n_cols]
-    ue_ref, me_ref = refs[11 + n_cols : 13 + n_cols]
-    ua, ub, tab_even, tab_odd, halo, buf, slot_row, corner_row, counter, dest, sem = refs[13 + n_cols :]
+    (ue_in, me_in, ra_ref, rb_ref, w_ref, starts, offs, wts, ends, dest_hbm) = refs[:10]
+    outs = refs[10 : 10 + n_cols]
+    ue_ref, me_ref = refs[10 + n_cols : 12 + n_cols]
+    ua, ub, tab_even, tab_odd, halo, buf, slot_row, corner_row, counter, dest, sem = refs[12 + n_cols :]
     fetch = pltpu.make_async_copy(dest_hbm, dest, sem)
     fetch.start()
     col_even = lax.axis_index("cols") % 2 == 0
@@ -341,29 +344,33 @@
         dst[:, cols : cols + 128] = unflipped(side_tile(west, east, width), tall)
     ua[...] = ue_ref[...]
     ub[...] = jnp.zeros(ub.shape, F32)
-    u = hjb_sweep(rows, cols, ua, ub, me_ref)
+
+    def place_blocks():
+        fetch.wait()
+        fill_slots(rows, blocks, cap, True, dest, slot_row, corner_row, counter)
+
+    u = hjb_sweep(rows, cols, ua, ub, me_ref, place_blocks)
     tabs = (tab_even, tab_odd)
     fill_tables(rows, cols, u, tabs, halo)
-    fetch.wait()
     sample_moves(
-        rows, cols, blocks, cap, True, tabs, halo, starts, offs, wts, ends, dest, buf, slot_row,
-        corner_row, counter,
+        rows, cols, blocks, cap, True, tabs, halo, starts, offs, wts, ends, buf, slot_row, corner_row
     )
     part_rows = 12 * cap + EDGE
     for k in range(n_cols):
         out = outs[(n_cols - k) % n_cols]
         out[0 : part_rows - EDGE, :] = buf[k * part_rows : (k + 1) * part_rows - EDGE, :]
-        out[part_rows - EDGE :, :] = w_ref[...] + v_ref[...]
+        out[part_rows - EDGE :, :] = w_ref[...]
 
 
 def again_kernel(rows, cols, blocks, cap, n_cols, *refs):
-    (ue_ref, m_in, d_ref, ra_ref, rb_ref, total_ref) = refs[:6]
-    (starts, offs, wts, ends, dest_hbm) = refs[6:11]
-    outs = refs[11 : 11 + n_cols]
-    value_hbm, density_ref = refs[11 + n_cols : 13 + n_cols]
+    (ue_ref, m_in, d_ref, ra_ref, rb_ref, total_in, more_in) = refs[:7]
+    (starts, offs, wts, ends, dest_hbm) = refs[7:12]
+    outs = refs[12 : 12 + n_cols]
+    value_hbm, density_ref, total_ref = refs[12 + n_cols : 15 + n_cols]
     (ua, ub, m, tab_even, tab_odd, halo, buf, slot_row, corner_row, counter, dest, sem, value_sem) = (
-        refs[13 + n_cols :]
-    )
+        refs[15 + n_cols :]
+    )
+    total_ref[...] = total_in[...] + more_in[...]
     fetch = pltpu.make_async_copy(dest_hbm, dest, sem)
     fetch.start()
     col_even = lax.axis_index("cols") % 2 == 0
@@ -385,15 +392,18 @@
     density_ref[...] = m[PAD : PAD + rows, 0:cols]
     ua[...] = ue_ref[...]
     ub[...] = jnp.zeros(ub.shape, F32)
-    u = hjb_sweep(rows, cols, ua, ub, m)
+
+    def place_blocks():
+        fetch.wait()
+        fill_slots(rows, blocks, cap, False, dest, slot_row, corner_row, counter)
+
+    u = hjb_sweep(rows, cols, ua, ub, m, place_blocks)
     leave = pltpu.make_async_copy(u.at[PAD : PAD + rows, 0:cols], value_hbm, value_sem)
     leave.start()
     tabs = (tab_even, tab_odd)
     fill_tables(rows, cols, u, tabs, halo)
-    fetch.wait()
     sample_moves(
-        rows, cols, blocks, cap, False, tabs, halo, starts, offs, wts, ends, dest, buf, slot_row,
-        corner_row, counter,
+        rows, cols, blocks, cap, False, tabs, halo, starts, offs, wts, ends, buf, slot_row, corner_row
     )
     part_rows = 6 * cap + EDGE
     for k in range(n_cols):
@@ -561,12 +571,11 @@
 
 
 def first_deposit_kernel(rows, cols, cap, n_cols, *refs):
-    ra_ref, rb_ref, acc_in, beside_in, total_in = refs[:5]
-    grid, sa_ref, sb_ref, masses, total = refs[5:10]
+    ra_ref, rb_ref, acc_in, beside_in = refs[:4]
+    grid, sa_ref, sb_ref, masses = refs[4:8]
     other_deposit(
-        rows, cols, cap, n_cols, True, (ra_ref, rb_ref), acc_in, beside_in, masses, grid, refs[10:]
-    )
-    total[...] = total_in[...] + ra_ref[4 * cap * n_cols :, :]
+        rows, cols, cap, n_cols, True, (ra_ref, rb_ref), acc_in, beside_in, masses, grid, refs[8:]
+    )
     row_even = lax.axis_index("rows") % 2 == 0
     south_going = grid[rows - 7 : rows + 1, :]
     north_going = grid[0:8, :]
@@ -623,12 +632,12 @@
     return [outs[0]] + came
 
 
-def exchange_rows(pieces, kinds, cap, extra_first, extra_second=None):
+def exchange_rows(pieces, kinds, cap, extra=None):
     step = kinds * cap
-    first = [piece[step : 2 * step] for piece in pieces] + [extra_first]
+    first = [piece[step : 2 * step] for piece in pieces]
     second = [piece[2 * step : 3 * step] for piece in pieces]
-    if extra_second is not None:
-        second.append(extra_second)
+    if extra is not None:
+        first, second = first + [extra], second + [extra]
     return swap_both(jnp.concatenate(first), jnp.concatenate(second), "rows")
 
 
@@ -644,22 +653,19 @@
     wts = weights.reshape(blocks, 128)
     ends = end_cells.reshape(blocks, 128)
     arrays = (terminal_value, density_start, wts, starts, offsets, ends)
-    *arrays, sa, sb, total = vmem_call(
+    *arrays, sa, sb = vmem_call(
         functools.partial(start_kernel, rows, len(arrays)),
         (
             *[shape(*x.shape, dtype=x.dtype) for x in arrays],
+            shape(3 * EDGE, cols),
             shape(2 * EDGE, cols),
-            shape(2 * EDGE, cols),
-            shape(EDGE, 128),
         ),
         len(arrays),
         [pltpu.SemaphoreType.DMA((len(arrays),))],
         hbm_in=range(len(arrays)),
     )(*arrays)
     terminal_value, density_start, wts, starts, offsets, ends = arrays
-    bits = [1 << i for i in range(1, n_rows.bit_length() - 1)]
     ra, rb = swap_both(sa, sb, "rows")
-    more = xor_permute(total, "rows", bits[0])
     ue, me, ca, cb, total = vmem_call(
         functools.partial(start_mid_kernel, rows, cols),
         (
@@ -669,12 +675,9 @@
             shape(2 * EDGE, flat),
             shape(EDGE, 128),
         ),
-        6,
-    )(terminal_value, density_start, ra, rb, total, more)
+        5,
+    )(terminal_value, density_start, ra, rb, sa)
     ca, cb = swap_both(ca, cb, "cols")
-    for bit in bits[1:-1]:
-        total = total + xor_permute(total, "rows", bit)
-    more = xor_permute(total, "rows", bits[-1])
     sweep_scratch = [
         pltpu.VMEM((tall, wide), F32),
         pltpu.VMEM((tall, wide), F32),
@@ -715,32 +718,37 @@
     *outs, ue, me = vmem_call(
         functools.partial(first_kernel, rows, cols, blocks, cap, n_cols),
         tuple([shape(part_rows, 128)] * n_cols + [shape(tall, wide)] * 2),
-        11,
+        10,
         sweep_scratch + sample_scratch(part_rows),
-        hbm_in=(10,),
-    )(ue, me, ca, cb, total, more, starts, offsets, wts, ends, dest_tiles)
+        hbm_in=(9,),
+    )(ue, me, ca, cb, total, starts, offsets, wts, ends, dest_tiles)
     pieces = exchange_columns(outs)
     total = sum(piece[part_rows - EDGE :] for piece in pieces)
-    ra, rb = exchange_rows(pieces, 4, cap, total)
+    ra, rb = exchange_rows(pieces, 4, cap)
+    bits = [1 << i for i in range(1, n_rows.bit_length() - 1)]
+    more = xor_permute(total, "rows", bits[0])
     acc, beside, own_masses = vmem_call(
         functools.partial(own_deposit_kernel, rows, cols, cap, n_cols, True),
         (*carried, shape(part_rows_of(n_cols), 128)),
         n_cols,
         own_scratch,
     )(*pieces)
-    grid, ea, eb, masses, total = vmem_call(
+    grid, ea, eb, masses = vmem_call(
         functools.partial(first_deposit_kernel, rows, cols, cap, n_cols),
         (
             shape(rows + 8, wide),
             shape(8, wide),
             shape(8, wide),
             shape(part_rows_of(2 * n_cols), 128),
-            shape(EDGE, 128),
         ),
-        5,
+        4,
         other_scratch,
-    )(ra, rb, acc, beside, total)
+    )(ra, rb, acc, beside)
+    ea, eb, more = lax.optimization_barrier((ea, eb, more))
     ea, eb = swap_both(ea, eb, "rows")
+    for bit in bits[1:]:
+        total = total + more
+        more = xor_permute(total, "rows", bit)
     deposit, ca, cb = vmem_call(
         functools.partial(edge_mid_kernel, rows, cols),
         (shape(tall, wide), shape(2 * EDGE, flat), shape(2 * EDGE, flat)),
@@ -748,20 +756,20 @@
     )(grid, ea, eb)
     ca, cb = swap_both(ca, cb, "cols")
     part_rows = 6 * cap + EDGE
-    *outs, value, density = vmem_call(
+    *outs, value, density, total = vmem_call(
         functools.partial(again_kernel, rows, cols, blocks, cap, n_cols),
-        tuple([shape(part_rows, 128)] * n_cols + [shape(rows, cols)] * 2),
-        11,
+        tuple([shape(part_rows, 128)] * n_cols + [shape(rows, cols)] * 2 + [shape(EDGE, 128)]),
+        12,
         sweep_scratch
         + [pltpu.VMEM((tall, wide), F32)]
         + sample_scratch(part_rows)
         + [pltpu.SemaphoreType.DMA(())],
-        hbm_in=(10,),
+        hbm_in=(11,),
         hbm_out=(n_cols,),
-    )(ue, me, deposit, ca, cb, total, starts, offsets, wts, ends, dest_tiles)
+    )(ue, me, deposit, ca, cb, total, more, starts, offsets, wts, ends, dest_tiles)
     pieces = exchange_columns(outs)
     corner = sum(piece[part_rows - EDGE :] for piece in pieces)
-    ra, rb = exchange_rows(pieces, 2, cap, corner, corner)
+    ra, rb = exchange_rows(pieces, 2, cap, corner)
     acc, beside = vmem_call(
         functools.partial(own_deposit_kernel, rows, cols, cap, n_cols, False),
         carried,

time: 79.8 us -> 79.2 us (level)
  Pallas kernels: 13.1 us -> 16.3 us
  waiting for transfers between devices: 20.8 us -> 17.9 us
  starting transfers between devices: 44.5 us -> 42.7 us
    pallas_call x10, Pallas kernels: 13.1 us -> 16.3 us  [run(): call(*[pltpu.with_memory_space_constraint(x, pltpu.HBM if i in hbm_in els...]
    ppermute x6, starting transfers between devices: 24.2 us -> 21.4 us  [swap_both(): lax.ppermute(second, axis, pairs_b)]
    ppermute x8, waiting for transfers between devices: 9.17 us -> 7.41 us  [xor_permute(): lax.ppermute(value, axis, [(i, i ^ bit) for i in range(lax.axis_size(axis...]
    ppermute x1, starting transfers between devices: 3.84 us -> 5.07 us  [body(): below = lax.ppermute(below, 'rows', [(i, i + 1) for i in range(n_rows - 1)])]
    ppermute x1, waiting for transfers between devices: 3.61 us -> 2.42 us  [body(): lax.ppermute(beside, 'cols', [(i, i + 1) for i in range(n_cols - 1)])]
    ppermute x1, starting transfers between devices: 2.81 us -> 1.92 us  [body(): lax.ppermute(beside, 'cols', [(i, i + 1) for i in range(n_cols - 1)])]
  transfers between devices with their start and end apart: 22 -> 22, of which waited for: 13 -> 10; matrix products, arithmetic and copies ran while one was open for 0% -> 0% of each run, Pallas kernels for 0% -> 5%
where the time goes in v2:
time: 79.2 us; the launch traced here: 77.9 us
  starting transfers between devices  42.7 us (54%)
  waiting for transfers between devices  17.9 us (23%)
  Pallas kernels  16.3 us (21%)
  between operations  0.87 us (1%)
    ppermute x6, starting transfers between devices, swap_both(): lax.ppermute(second, axis, pairs_b)  21.4 us
    pallas_call x10, Pallas kernels, run(): call(*[pltpu.with_memory_space_constraint(x, pltpu.HBM if i in hbm_in els...  16.3 us
    ppermute x6, starting transfers between devices, swap_both(): lax.ppermute(first, axis, pairs_a)  8.43 us
    ppermute x6, waiting for transfers between devices, swap_both(): lax.ppermute(second, axis, pairs_b)  8.08 us
    ppermute x8, waiting for transfers between devices, xor_permute(): lax.ppermute(value, axis, [(i, i ^ bit) for i in range(lax.axis_size(axis...  7.41 us
    ppermute x8, starting transfers between devices, xor_permute(): lax.ppermute(value, axis, [(i, i ^ bit) for i in range(lax.axis_size(axis...  5.9 us
    ppermute x1, starting transfers between devices, body(): below = lax.ppermute(below, 'rows', [(i, i + 1) for i in range(n_rows - 1)])  5.07 us
    ppermute x1, waiting for transfers between devices, body(): lax.ppermute(beside, 'cols', [(i, i + 1) for i in range(n_cols - 1)])  2.42 us
  transfers between devices with their start and end apart: 22, of which 10 were waited for; matrix products, arithmetic and copies ran while one was open for 0% of the time, Pallas kernels for 5%

profile of v2, /device:TPU:11, one launch (start us, length us, event | category | flops | bytes accessed | tf_op | source)
XLA Modules:
  0.0 77.9 jit_solution(4851005363752804249)
XLA Ops:
  0.6 1.2 %shard_map.86 = (f32[128,512]{1,0:T(8,128)S(1)}, f32[128,512]{1,0:T(8,128)S(1)}, f32[32,128]{1,0:T(8,128)S(1)}, s32[32,128]{1,0:T(8,128)S(1)}, f32[2,4096]{1,0:T...) custom-call(f32[128,512]{1,0:T(8,128)} %refs_0_.1, f32[128,512]{1,0:T(8,128)} %refs_1_.1, ...), custom_call_target="tpu_custom_call" | custom-call | tf_op jit(solution)/shard_map/pallas_call | solution.py:53
  1.8 0.7 collective-permute-start
  2.6 3.0 %collective-permute-start.1 = (f32[16,512]{1,0:T(8,128)S(1)}, f32[16,512]{1,0:T(8,128)S(1)}, u32[]{:S(2)}, u32[]{:S(2)}) collective-permute-start(f32[16,512]{1,0:T(8,128)S(1)} %get-tuple-element.49), channel_id=1, source_target_pairs={{4,8},{8,4},{12,16},{16,12},{20,24},{24,20},{5,9},{9,5},{13,17},{1... | collective-permute-start | bytes 98312 | tf_op jit(solution)/shard_map/ppermute | solution.py:28
  5.6 3.1 %collective-permute-done.1.b_ref = f32[16,512]{1,0:T(8,128)S(1)} collective-permute-done((f32[16,512]{1,0:T(8,128)S(1)}, f32[16,512]{1,0:T(8,128)S(1)}, u32[]{:S(2)}, u32[]{:S(2)}) %collective-permute-start.1) | collective-permute-done | bytes 32800 | tf_op jit(solution)/shard_map/ppermute | solution.py:28
  8.7 0.0 collective-permute-done.a_ref
  8.7 0.2 shard_map.87
  8.9 0.2 collective-permute-start.2
  9.1 4.3 %collective-permute-start.3 = (f32[16,256]{1,0:T(8,128)S(1)}, f32[16,256]{1,0:T(8,128)S(1)}, u32[]{:S(2)}, u32[]{:S(2)}) collective-permute-start(f32[16,256]{1,0:T(8,128)S(1)} %get-tuple-element.53), channel_id=1, source_target_pairs={{1,2},{2,1},{5,6},{6,5},{9,10},{10,9},{13,14},{14,13},{17,18},{18,... | collective-permute-start | bytes 49160 | tf_op jit(solution)/shard_map/ppermute | solution.py:28
  13.4 1.1 %collective-permute-done.3.refs_3_ = f32[16,256]{1,0:T(8,128)S(1)} collective-permute-done((f32[16,256]{1,0:T(8,128)S(1)}, f32[16,256]{1,0:T(8,128)S(1)}, u32[]{:S(2)}, u32[]{:S(2)}) %collective-permute-start.3) | collective-permute-done | bytes 16416 | tf_op jit(solution)/shard_map/ppermute | solution.py:28
  14.5 4.0 %shard_map.88 = (f32[104,128]{1,0:T(8,128)S(1)}, f32[104,128]{1,0:T(8,128)S(1)}, f32[104,128]{1,0:T(8,128)S(1)}, f32[104,128]{1,0:T(8,128)S(1)}, f32[160,640]{1,0:T(8,128)S(1)}, /*index=5*/f32[160,640]{1,0:T(8,128)S(1)}) custom-call(f32[160,640]{1,0:T(8,128)S(1)} %get-tuple-element.50.refs_0_, f32[160,640]{1,0:T(8,128)S(1)} %get-tuple-element.51.refs_1_, ...), custom_call_target="tpu_custom_call" | custom-call | tf_op jit(solution)/shard_map/pallas_call | solution.py:53
  18.5 1.7 %collective-permute-start.4 = (f32[104,128]{1,0:T(8,128)S(1)}, f32[104,128]{1,0:T(8,128)S(1)}, u32[]{:S(2)}, u32[]{:S(2)}) collective-permute-start(f32[104,128]{1,0:T(8,128)S(1)} %get-tuple-element.62), channel_id=1, source_target_pairs={{0,3},{1,2},{2,1},{3,0},{4,7},{5,6},{6,5},{7,4},{8,11},{9,10},{10,... | collective-permute-start | bytes 159752 | tf_op jit(solution)/shard_map/ppermute | solution.py:32
  20.2 1.3 %collective-permute-start.6 = (f32[104,128]{1,0:T(8,128)S(1)}, f32[104,128]{1,0:T(8,128)S(1)}, u32[]{:S(2)}, u32[]{:S(2)}) collective-permute-start(f32[104,128]{1,0:T(8,128)S(1)} %get-tuple-element.64), channel_id=1, source_target_pairs={{0,1},{1,0},{2,3},{3,2},{4,5},{5,4},{6,7},{7,6},{8,9},{9,8},{10,11... | collective-permute-start | bytes 159752 | tf_op jit(solution)/shard_map/ppermute | solution.py:32
  21.5 0.2 collective-permute-done.4.refs_1_
  21.7 2.4 %collective-permute-done.5.refs_2_ = f32[104,128]{1,0:T(8,128)S(1)} collective-permute-done((f32[104,128]{1,0:T(8,128)S(1)}, f32[104,128]{1,0:T(8,128)S(1)}, u32[]{:S(2)}, u32[]{:S(2)}) %collective-permute-start.5) | collective-permute-done | bytes 53280 | tf_op jit(solution)/shard_map/ppermute | solution.py:32
  24.1 1.9 %collective-permute-start.7 = (f32[128,128]{1,0:T(8,128)S(1)}, f32[128,128]{1,0:T(8,128)S(1)}, u32[]{:S(2)}, u32[]{:S(2)}) collective-permute-start(f32[128,128]{1,0:T(8,128)S(1)} %pad_maximum_fusion), channel_id=1, source_target_pairs={{0,4},{4,0},{8,12},{12,8},{16,20},{20,16},{24,28},{28,24},{1,5},{5... | collective-permute-start | bytes 196616 | tf_op jit(solution)/shard_map/ppermute | solution.py:28
  26.0 3.9 %collective-permute-start.8 = (f32[128,128]{1,0:T(8,128)S(1)}, f32[128,128]{1,0:T(8,128)S(1)}, u32[]{:S(2)}, u32[]{:S(2)}) collective-permute-start(f32[128,128]{1,0:T(8,128)S(1)} %pad_maximum_fusion.1), channel_id=1, source_target_pairs={{4,8},{8,4},{12,16},{16,12},{20,24},{24,20},{5,9},{9,5},{13,17},{1... | collective-permute-start | bytes 196616 | tf_op jit(solution)/shard_map/ppermute | solution.py:28
  30.0 0.1 collective-permute-start.9
  30.1 1.3 %shard_map.89 = (f32[2,288,256]{2,1,0:T(8,128)S(1)}, f32[136,128]{1,0:T(8,128)S(1)}, f32[80,128]{1,0:T(8,128)S(1)}) custom-call(f32[104,128]{1,0:T(8,128)S(1)} %get-tuple-element.61.refs_0_, f32[104,128]{1,0:T(8,128)S(1)} %collective-permute-done.4.refs_1_, f32[104,128]{1,0:T(8,128)S(1)} %collective-permute-done.5.refs_2_, ...), custom_call_target="tpu_custom_call" | custom-call | tf_op jit(solution)/shard_map/pallas_call | solution.py:53
  31.3 0.0 collective-permute-done.7.refs_0_
  31.4 1.3 %collective-permute-done.8.refs_1_ = f32[128,128]{1,0:T(8,128)S(1)} collective-permute-done((f32[128,128]{1,0:T(8,128)S(1)}, f32[128,128]{1,0:T(8,128)S(1)}, u32[]{:S(2)}, u32[]{:S(2)}) %collective-permute-start.8) | collective-permute-done | bytes 65568 | tf_op jit(solution)/shard_map/ppermute | solution.py:28
  32.6 1.6 %shard_map.90 = (f32[136,640]{1,0:T(8,128)S(1)}, f32[8,640]{1,0:T(8,128)S(1)}, f32[8,640]{1,0:T(8,128)S(1)}, f32[144,128]{1,0:T(8,128)S(1)}) custom-call(f32[128,128]{1,0:T(8,128)S(1)} %collective-permute-done.7.refs_0_, f32[128,128]{1,0:T(8,128)S(1)} %collective-permute-done.8.refs_1_, f32[2,288,256]{2,1,0:T(8,128)S(1)} %get-tuple-element.65.refs_2_, ...), custom_call_target="tpu_custom_call" | custom-call | tf_op jit(solution)/shard_map/pallas_call | solution.py:53
  34.2 0.0 collective-permute-done.9
  34.2 0.7 collective-permute-start.10
  35.0 4.3 %collective-permute-start.11 = (f32[8,640]{1,0:T(8,128)S(1)}, f32[8,640]{1,0:T(8,128)S(1)}, u32[]{:S(2)}, u32[]{:S(2)}) collective-permute-start(f32[8,640]{1,0:T(8,128)S(1)} %get-tuple-element.71), channel_id=1, source_target_pairs={{4,8},{8,4},{12,16},{16,12},{20,24},{24,20},{5,9},{9,5},{13,17},{1... | collective-permute-start | bytes 61448 | tf_op jit(solution)/shard_map/ppermute | solution.py:28
  39.3 0.0 collective-permute-done.10.a_ref
  39.3 1.7 %collective-permute-done.11.b_ref = f32[8,640]{1,0:T(8,128)S(1)} collective-permute-done((f32[8,640]{1,0:T(8,128)S(1)}, f32[8,640]{1,0:T(8,128)S(1)}, u32[]{:S(2)}, u32[]{:S(2)}) %collective-permute-start.11) | collective-permute-done | bytes 20512 | tf_op jit(solution)/shard_map/ppermute | solution.py:28
  41.0 0.1 shard_map.91
  41.1 2.1 %collective-permute-start.12 = (f32[16,256]{1,0:T(8,128)S(1)}, f32[16,256]{1,0:T(8,128)S(1)}, u32[]{:S(2)}, u32[]{:S(2)}) collective-permute-start(f32[16,256]{1,0:T(8,128)S(1)} %get-tuple-element.73), channel_id=1, source_target_pairs={{0,1},{1,0},{2,3},{3,2},{4,5},{5,4},{6,7},{7,6},{8,9},{9,8},{10,11... | collective-permute-start | bytes 49160 | tf_op jit(solution)/shard_map/ppermute | solution.py:28
  43.2 1.9 %collective-permute-start.13 = (f32[16,256]{1,0:T(8,128)S(1)}, f32[16,256]{1,0:T(8,128)S(1)}, u32[]{:S(2)}, u32[]{:S(2)}) collective-permute-start(f32[16,256]{1,0:T(8,128)S(1)} %get-tuple-element.74), channel_id=1, source_target_pairs={{1,2},{2,1},{5,6},{6,5},{9,10},{10,9},{13,14},{14,13},{17,18},{18,... | collective-permute-start | bytes 49160 | tf_op jit(solution)/shard_map/ppermute | solution.py:28
  45.1 0.1 collective-permute-start.14
  45.2 2.4 %collective-permute-done.14.refs_6_ = f32[8,128]{1,0:T(8,128)S(1)} collective-permute-done((f32[8,128]{1,0:T(8,128)S(1)}, f32[8,128]{1,0:T(8,128)S(1)}, u32[]{:S(2)}, u32[]{:S(2)}) %collective-permute-start.14) | collective-permute-done | bytes 4128 | tf_op jit(solution)/shard_map/ppermute | solution.py:32
  47.6 0.0 collective-permute-done.12.refs_3_
  47.6 0.0 collective-permute-done.13.refs_4_
  47.6 4.2 %shard_map.92 = (f32[56,128]{1,0:T(8,128)S(1)}, f32[56,128]{1,0:T(8,128)S(1)}, f32[56,128]{1,0:T(8,128)S(1)}, f32[56,128]{1,0:T(8,128)S(1)}, f32[128,512]{1,0:T(...) custom-call(f32[160,640]{1,0:T(8,128)S(1)} %get-tuple-element.59.refs_0_, ...), custom_call_target="tpu_custom_call" | custom-call | tf_op jit(solution)/shard_map/pallas_call | solution.py:53
  51.9 1.5 %collective-permute-start.15 = (f32[56,128]{1,0:T(8,128)S(1)}, f32[56,128]{1,0:T(8,128)S(1)}, u32[]{:S(2)}, u32[]{:S(2)}) collective-permute-start(f32[56,128]{1,0:T(8,128)S(1)} %get-tuple-element.78), channel_id=1, source_target_pairs={{0,3},{1,2},{2,1},{3,0},{4,7},{5,6},{6,5},{7,4},{8,11},{9,10},{10,... | collective-permute-start | bytes 86024 | tf_op jit(solution)/shard_map/ppermute | solution.py:32
  53.4 1.3 %collective-permute-start.17 = (f32[56,128]{1,0:T(8,128)S(1)}, f32[56,128]{1,0:T(8,128)S(1)}, u32[]{:S(2)}, u32[]{:S(2)}) collective-permute-start(f32[56,128]{1,0:T(8,128)S(1)} %get-tuple-element.80), channel_id=1, source_target_pairs={{0,1},{1,0},{2,3},{3,2},{4,5},{5,4},{6,7},{7,6},{8,9},{9,8},{10,11... | collective-permute-start | bytes 86024 | tf_op jit(solution)/shard_map/ppermute | solution.py:32
  54.6 0.0 collective-permute-done.15.refs_1_
  54.7 2.3 %collective-permute-done.16.refs_2_ = f32[56,128]{1,0:T(8,128)S(1)} collective-permute-done((f32[56,128]{1,0:T(8,128)S(1)}, f32[56,128]{1,0:T(8,128)S(1)}, u32[]{:S(2)}, u32[]{:S(2)}) %collective-permute-start.16) | collective-permute-done | bytes 28704 | tf_op jit(solution)/shard_map/ppermute | solution.py:32
  57.0 2.8 %collective-permute-start.18 = (f32[72,128]{1,0:T(8,128)S(1)}, f32[72,128]{1,0:T(8,128)S(1)}, u32[]{:S(2)}, u32[]{:S(2)}) collective-permute-start(f32[72,128]{1,0:T(8,128)S(1)} %constant_dynamic-update-slice_fusion), channel_id=1, source_target_pairs={{0,4},{4,0},{8,12},{12,8},{16,20},{20,16},{24,28},{28,24},{1,5},{5... | collective-permute-start | bytes 110600 | tf_op jit(solution)/shard_map/ppermute | solution.py:28
  59.8 4.0 %collective-permute-start.19 = (f32[72,128]{1,0:T(8,128)S(1)}, f32[72,128]{1,0:T(8,128)S(1)}, u32[]{:S(2)}, u32[]{:S(2)}) collective-permute-start(f32[72,128]{1,0:T(8,128)S(1)} %get-tuple-element.90), channel_id=1, source_target_pairs={{4,8},{8,4},{12,16},{16,12},{20,24},{24,20},{5,9},{9,5},{13,17},{1... | collective-permute-start | bytes 110600 | tf_op jit(solution)/shard_map/ppermute | solution.py:28
  63.8 1.3 %shard_map.93 = (f32[2,288,256]{2,1,0:T(8,128)S(1)}, f32[136,128]{1,0:T(8,128)S(1)}) custom-call(f32[56,128]{1,0:T(8,128)S(1)} %get-tuple-element.77.refs_0_, f32[56,128]{1,0:T(8,128)S(1)} %collective-permute-done.15.refs_1_, f32[56,128]{1,0:T(8,128)S(1)} %collective-permute-done.16.refs_2_, f32[56,128]{1,0:T(8,128)S(1)} %collective-permute-done.17.refs_3_, ...), custom_call_target="tpu_custom_call" | custom-call | tf_op jit(solution)/shard_map/pallas_call | solution.py:53
  65.0 0.9 %collective-permute-done.19.refs_1_ = f32[72,128]{1,0:T(8,128)S(1)} collective-permute-done((f32[72,128]{1,0:T(8,128)S(1)}, f32[72,128]{1,0:T(8,128)S(1)}, u32[]{:S(2)}, u32[]{:S(2)}) %collective-permute-start.19) | collective-permute-done | bytes 36896 | tf_op jit(solution)/shard_map/ppermute | solution.py:28
  66.0 1.7 %shard_map.94 = (f32[136,640]{1,0:T(8,128)S(1)}, f32[8,512]{1,0:T(8,128)S(1)}, f32[8,128]{1,0:T(8,128)S(1)}) custom-call(f32[72,128]{1,0:T(8,128)S(1)} %collective-permute-done.18.refs_0_, f32[72,128]{1,0:T(8,128)S(1)} %collective-permute-done.19.refs_1_, f32[2,288,256]{2,1,0:T(8,128)S(1)} %get-tuple-element.82.refs_2_, ...), custom_call_target="tpu_custom_call" | custom-call | tf_op jit(solution)/shard_map/pallas_call | solution.py:53
  67.6 5.1 %collective-permute-start.20 = (f32[8,512]{1,0:T(8,128)S(1)}, f32[8,512]{1,0:T(8,128)S(1)}, u32[]{:S(2)}, u32[]{:S(2)}) collective-permute-start(f32[8,512]{1,0:T(8,128)S(1)} %get-tuple-element.87), channel_id=1, source_target_pairs={{0,4},{4,8},{8,12},{12,16},{16,20},{20,24},{24,28},{1,5},{5,9},{9,... | collective-permute-start | bytes 49160 | tf_op jit(solution)/shard_map/ppermute | solution.py:785
  72.7 1.9 %collective-permute-start.21 = (f32[8,128]{1,0:T(8,128)S(1)}, f32[8,128]{1,0:T(8,128)S(1)}, u32[]{:S(2)}, u32[]{:S(2)}) collective-permute-start(f32[8,128]{1,0:T(8,128)S(1)} %get-tuple-element.88), channel_id=1, source_target_pairs={{0,1},{1,2},{2,3},{4,5},{5,6},{6,7},{8,9},{9,10},{10,11},{12,13},{... | collective-permute-start | bytes 12296 | tf_op jit(solution)/shard_map/ppermute | solution.py:786
  74.6 2.4 %collective-permute-done.21.col_in = f32[8,128]{1,0:T(8,128)S(1)} collective-permute-done((f32[8,128]{1,0:T(8,128)S(1)}, f32[8,128]{1,0:T(8,128)S(1)}, u32[]{:S(2)}, u32[]{:S(2)}) %collective-permute-start.21) | collective-permute-done | bytes 4128 | tf_op jit(solution)/shard_map/ppermute | solution.py:786
  77.1 0.0 collective-permute-done.20.row_in
  77.1 0.8 %shard_map.95 = f32[128,512]{1,0:T(8,128)} custom-call(f32[136,640]{1,0:T(8,128)S(1)} %get-tuple-element.85.g_ref, f32[128,512]{1,0:T(8,128)S(1)} %get-tuple-element.86.m_ref, f32[8,512]{1,0:T(8,128)S(1)} %collective-permute-done.20.row_in, f32[8,128]{1,0:T(8,128)S(1)} %collective-permute-done.21.col_in, f32[8,128]{1,0:T(8,128)S(1)} %get-tuple-element.89.total_ref), custom_call_target="tpu_custom_call" | custom-call | tf_op jit(solution)/shard_map/pallas_call | solution.py:53
  (20 shorter events, 0.1 us)
Async XLA Ops:
  1.8 6.9 %collective-permute-start = (f32[24,512]{1,0:T(8,128)S(1)}, f32[24,512]{1,0:T(8,128)S(1)}, u32[]{:S(2)}, u32[]{:S(2)}) collective-permute-start(f32[24,512]{1,0:T(8,128)S(1)} %get-tuple-element.48.s_ref), channel_id=1, source_target_pairs={{0,4},{4,0},{8,12},{12,8},{16,20},{20,16},{24,28},{28,24},{1,5},{5... | collective-permute-start | bytes 147464 | tf_op jit(solution)/shard_map/ppermute | solution.py:28
  2.6 6.1 %collective-permute-start.1 = (f32[16,512]{1,0:T(8,128)S(1)}, f32[16,512]{1,0:T(8,128)S(1)}, u32[]{:S(2)}, u32[]{:S(2)}) collective-permute-start(f32[16,512]{1,0:T(8,128)S(1)} %get-tuple-element.49), channel_id=1, source_target_pairs={{4,8},{8,4},{12,16},{16,12},{20,24},{24,20},{5,9},{9,5},{13,17},{1... | collective-permute-start | bytes 98312 | tf_op jit(solution)/shard_map/ppermute | solution.py:28
  8.9 4.6 %collective-permute-start.2 = (f32[16,256]{1,0:T(8,128)S(1)}, f32[16,256]{1,0:T(8,128)S(1)}, u32[]{:S(2)}, u32[]{:S(2)}) collective-permute-start(f32[16,256]{1,0:T(8,128)S(1)} %get-tuple-element.52), channel_id=1, source_target_pairs={{0,1},{1,0},{2,3},{3,2},{4,5},{5,4},{6,7},{7,6},{8,9},{9,8},{10,11... | collective-permute-start | bytes 49160 | tf_op jit(solution)/shard_map/ppermute | solution.py:28
  9.1 5.4 %collective-permute-start.3 = (f32[16,256]{1,0:T(8,128)S(1)}, f32[16,256]{1,0:T(8,128)S(1)}, u32[]{:S(2)}, u32[]{:S(2)}) collective-permute-start(f32[16,256]{1,0:T(8,128)S(1)} %get-tuple-element.53), channel_id=1, source_target_pairs={{1,2},{2,1},{5,6},{6,5},{9,10},{10,9},{13,14},{14,13},{17,18},{18,... | collective-permute-start | bytes 49160 | tf_op jit(solution)/shard_map/ppermute | solution.py:28
  18.5 3.2 %collective-permute-start.4 = (f32[104,128]{1,0:T(8,128)S(1)}, f32[104,128]{1,0:T(8,128)S(1)}, u32[]{:S(2)}, u32[]{:S(2)}) collective-permute-start(f32[104,128]{1,0:T(8,128)S(1)} %get-tuple-element.62), channel_id=1, source_target_pairs={{0,3},{1,2},{2,1},{3,0},{4,7},{5,6},{6,5},{7,4},{8,11},{9,10},{10,... | collective-permute-start | bytes 159752 | tf_op jit(solution)/shard_map/ppermute | solution.py:32
  20.2 3.9 %collective-permute-start.5 = (f32[104,128]{1,0:T(8,128)S(1)}, f32[104,128]{1,0:T(8,128)S(1)}, u32[]{:S(2)}, u32[]{:S(2)}) collective-permute-start(f32[104,128]{1,0:T(8,128)S(1)} %get-tuple-element.63), channel_id=1, source_target_pairs={{0,2},{1,3},{2,0},{3,1},{4,6},{5,7},{6,4},{7,5},{8,10},{9,11},{10,... | collective-permute-start | bytes 159752 | tf_op jit(solution)/shard_map/ppermute | solution.py:32
  20.2 3.9 %collective-permute-start.6 = (f32[104,128]{1,0:T(8,128)S(1)}, f32[104,128]{1,0:T(8,128)S(1)}, u32[]{:S(2)}, u32[]{:S(2)}) collective-permute-start(f32[104,128]{1,0:T(8,128)S(1)} %get-tuple-element.64), channel_id=1, source_target_pairs={{0,1},{1,0},{2,3},{3,2},{4,5},{5,4},{6,7},{7,6},{8,9},{9,8},{10,11... | collective-permute-start | bytes 159752 | tf_op jit(solution)/shard_map/ppermute | solution.py:32
  24.1 7.2 %collective-permute-start.7 = (f32[128,128]{1,0:T(8,128)S(1)}, f32[128,128]{1,0:T(8,128)S(1)}, u32[]{:S(2)}, u32[]{:S(2)}) collective-permute-start(f32[128,128]{1,0:T(8,128)S(1)} %pad_maximum_fusion), channel_id=1, source_target_pairs={{0,4},{4,0},{8,12},{12,8},{16,20},{20,16},{24,28},{28,24},{1,5},{5... | collective-permute-start | bytes 196616 | tf_op jit(solution)/shard_map/ppermute | solution.py:28
  26.0 6.6 %collective-permute-start.8 = (f32[128,128]{1,0:T(8,128)S(1)}, f32[128,128]{1,0:T(8,128)S(1)}, u32[]{:S(2)}, u32[]{:S(2)}) collective-permute-start(f32[128,128]{1,0:T(8,128)S(1)} %pad_maximum_fusion.1), channel_id=1, source_target_pairs={{4,8},{8,4},{12,16},{16,12},{20,24},{24,20},{5,9},{9,5},{13,17},{1... | collective-permute-start | bytes 196616 | tf_op jit(solution)/shard_map/ppermute | solution.py:28
  30.0 4.2 %collective-permute-start.9 = (f32[8,128]{1,0:T(8,128)S(1)}, f32[8,128]{1,0:T(8,128)S(1)}, u32[]{:S(2)}, u32[]{:S(2)}) collective-permute-start(f32[8,128]{1,0:T(8,128)S(1)} %slice_add_fusion.3), channel_id=1, source_target_pairs={{0,8},{4,12},{8,0},{12,4},{16,24},{20,28},{24,16},{28,20},{1,9},{5... | collective-permute-start | bytes 12296 | tf_op jit(solution)/shard_map/ppermute | solution.py:32
  34.2 5.0 %collective-permute-start.10 = (f32[8,640]{1,0:T(8,128)S(1)}, f32[8,640]{1,0:T(8,128)S(1)}, u32[]{:S(2)}, u32[]{:S(2)}) collective-permute-start(f32[8,640]{1,0:T(8,128)S(1)} %get-tuple-element.70), channel_id=1, source_target_pairs={{0,4},{4,0},{8,12},{12,8},{16,20},{20,16},{24,28},{28,24},{1,5},{5... | collective-permute-start | bytes 61448 | tf_op jit(solution)/shard_map/ppermute | solution.py:28
  35.0 6.0 %collective-permute-start.11 = (f32[8,640]{1,0:T(8,128)S(1)}, f32[8,640]{1,0:T(8,128)S(1)}, u32[]{:S(2)}, u32[]{:S(2)}) collective-permute-start(f32[8,640]{1,0:T(8,128)S(1)} %get-tuple-element.71), channel_id=1, source_target_pairs={{4,8},{8,4},{12,16},{16,12},{20,24},{24,20},{5,9},{9,5},{13,17},{1... | collective-permute-start | bytes 61448 | tf_op jit(solution)/shard_map/ppermute | solution.py:28
  41.1 6.5 %collective-permute-start.12 = (f32[16,256]{1,0:T(8,128)S(1)}, f32[16,256]{1,0:T(8,128)S(1)}, u32[]{:S(2)}, u32[]{:S(2)}) collective-permute-start(f32[16,256]{1,0:T(8,128)S(1)} %get-tuple-element.73), channel_id=1, source_target_pairs={{0,1},{1,0},{2,3},{3,2},{4,5},{5,4},{6,7},{7,6},{8,9},{9,8},{10,11... | collective-permute-start | bytes 49160 | tf_op jit(solution)/shard_map/ppermute | solution.py:28
  43.2 4.5 %collective-permute-start.13 = (f32[16,256]{1,0:T(8,128)S(1)}, f32[16,256]{1,0:T(8,128)S(1)}, u32[]{:S(2)}, u32[]{:S(2)}) collective-permute-start(f32[16,256]{1,0:T(8,128)S(1)} %get-tuple-element.74), channel_id=1, source_target_pairs={{1,2},{2,1},{5,6},{6,5},{9,10},{10,9},{13,14},{14,13},{17,18},{18,... | collective-permute-start | bytes 49160 | tf_op jit(solution)/shard_map/ppermute | solution.py:28
  45.1 2.5 %collective-permute-start.14 = (f32[8,128]{1,0:T(8,128)S(1)}, f32[8,128]{1,0:T(8,128)S(1)}, u32[]{:S(2)}, u32[]{:S(2)}) collective-permute-start(f32[8,128]{1,0:T(8,128)S(1)} %add.24.refs_5_), channel_id=1, source_target_pairs={{0,16},{4,20},{8,24},{12,28},{16,0},{20,4},{24,8},{28,12},{1,17},{... | collective-permute-start | bytes 12296 | tf_op jit(solution)/shard_map/ppermute | solution.py:32
  51.9 2.8 %collective-permute-start.15 = (f32[56,128]{1,0:T(8,128)S(1)}, f32[56,128]{1,0:T(8,128)S(1)}, u32[]{:S(2)}, u32[]{:S(2)}) collective-permute-start(f32[56,128]{1,0:T(8,128)S(1)} %get-tuple-element.78), channel_id=1, source_target_pairs={{0,3},{1,2},{2,1},{3,0},{4,7},{5,6},{6,5},{7,4},{8,11},{9,10},{10,... | collective-permute-start | bytes 86024 | tf_op jit(solution)/shard_map/ppermute | solution.py:32
  53.4 3.6 %collective-permute-start.16 = (f32[56,128]{1,0:T(8,128)S(1)}, f32[56,128]{1,0:T(8,128)S(1)}, u32[]{:S(2)}, u32[]{:S(2)}) collective-permute-start(f32[56,128]{1,0:T(8,128)S(1)} %get-tuple-element.79), channel_id=1, source_target_pairs={{0,2},{1,3},{2,0},{3,1},{4,6},{5,7},{6,4},{7,5},{8,10},{9,11},{10,... | collective-permute-start | bytes 86024 | tf_op jit(solution)/shard_map/ppermute | solution.py:32
  53.4 3.6 %collective-permute-start.17 = (f32[56,128]{1,0:T(8,128)S(1)}, f32[56,128]{1,0:T(8,128)S(1)}, u32[]{:S(2)}, u32[]{:S(2)}) collective-permute-start(f32[56,128]{1,0:T(8,128)S(1)} %get-tuple-element.80), channel_id=1, source_target_pairs={{0,1},{1,0},{2,3},{3,2},{4,5},{5,4},{6,7},{7,6},{8,9},{9,8},{10,11... | collective-permute-start | bytes 86024 | tf_op jit(solution)/shard_map/ppermute | solution.py:32
  57.0 8.0 %collective-permute-start.18 = (f32[72,128]{1,0:T(8,128)S(1)}, f32[72,128]{1,0:T(8,128)S(1)}, u32[]{:S(2)}, u32[]{:S(2)}) collective-permute-start(f32[72,128]{1,0:T(8,128)S(1)} %constant_dynamic-update-slice_fusion), channel_id=1, source_target_pairs={{0,4},{4,0},{8,12},{12,8},{16,20},{20,16},{24,28},{28,24},{1,5},{5... | collective-permute-start | bytes 110600 | tf_op jit(solution)/shard_map/ppermute | solution.py:28
  59.8 6.2 %collective-permute-start.19 = (f32[72,128]{1,0:T(8,128)S(1)}, f32[72,128]{1,0:T(8,128)S(1)}, u32[]{:S(2)}, u32[]{:S(2)}) collective-permute-start(f32[72,128]{1,0:T(8,128)S(1)} %get-tuple-element.90), channel_id=1, source_target_pairs={{4,8},{8,4},{12,16},{16,12},{20,24},{24,20},{5,9},{9,5},{13,17},{1... | collective-permute-start | bytes 110600 | tf_op jit(solution)/shard_map/ppermute | solution.py:28
  67.6 9.4 %collective-permute-start.20 = (f32[8,512]{1,0:T(8,128)S(1)}, f32[8,512]{1,0:T(8,128)S(1)}, u32[]{:S(2)}, u32[]{:S(2)}) collective-permute-start(f32[8,512]{1,0:T(8,128)S(1)} %get-tuple-element.87), channel_id=1, source_target_pairs={{0,4},{4,8},{8,12},{12,16},{16,20},{20,24},{24,28},{1,5},{5,9},{9,... | collective-permute-start | bytes 49160 | tf_op jit(solution)/shard_map/ppermute | solution.py:785
  72.7 4.4 %collective-permute-start.21 = (f32[8,128]{1,0:T(8,128)S(1)}, f32[8,128]{1,0:T(8,128)S(1)}, u32[]{:S(2)}, u32[]{:S(2)}) collective-permute-start(f32[8,128]{1,0:T(8,128)S(1)} %get-tuple-element.88), channel_id=1, source_target_pairs={{0,1},{1,2},{2,3},{4,5},{5,6},{6,7},{8,9},{9,10},{10,11},{12,13},{... | collective-permute-start | bytes 12296 | tf_op jit(solution)/shard_map/ppermute | solution.py:786

commit v3 on v2

--- a/solution.py
+++ b/solution.py
@@ -7,7 +7,6 @@
 from jax.sharding import PartitionSpec as P
 
 HJB_STEPS = 4
-ITERS = 2
 F32, BF16, I32 = jnp.float32, jnp.bfloat16, jnp.int32
 
 PAD = 16
@@ -140,40 +139,26 @@
     n_rows, n_cols = lax.axis_size("rows"), lax.axis_size("cols")
     sub = lax.broadcasted_iota(I32, (8, 128), 0)
     lane = lax.broadcasted_iota(I32, (8, 128), 1)
-    top, bottom, first, last = sub == 0, sub == 7, lane == 0, lane == 127
+    first, last = lane == 0, lane == 127
     row_first = lax.axis_index("rows") * rows
     col = jnp.where(lane < 64, cols + lane, lane - 128) + lax.axis_index("cols") * cols
     side_ok = (col >= 0) & (col < cols * n_cols)
     src, dst = ua, ub
 
-    def strip(i):
-        return [src[i : i + 8, t * 128 : (t + 1) * 128] for t in range(tiles)]
-
     for step in range(HJB_STEPS):
         if step == HJB_STEPS // 2:
             between()
-        start, stop = PAD - 8, PAD + rows + 8
-        here = strip(start)
-        fell = [pltpu.roll(x, 1, 0) for x in here]
-        rose = [pltpu.roll(x, 7, 0) for x in here]
-        fell_before = fell
-        for i in range(start, stop, 8):
-            if i + 8 < stop:
-                after = strip(i + 8)
-                rose_after = [pltpu.roll(x, 7, 0) for x in after]
-                fell_after = [pltpu.roll(x, 1, 0) for x in after]
-            else:
-                after, rose_after, fell_after = here, rose, fell
+        for i in range(PAD - 8, PAD + rows + 8, 8):
             row_ok = None
             if i < PAD or i >= PAD + rows:
                 row = sub + (row_first + (i - PAD))
                 row_ok = (row >= 0) & (row < rows * n_rows)
+            here = [src[t, i : i + 8, :] for t in range(tiles)]
             went = [pltpu.roll(x, 1, 1) for x in here]
             came = [pltpu.roll(x, 127, 1) for x in here]
             for t in range(tiles):
                 value = here[t]
-                up = jnp.where(top, fell_before[t], fell[t])
-                down = jnp.where(bottom, rose_after[t], rose[t])
+                up, down = src[t, i - 1 : i + 7, :], src[t, i + 1 : i + 9, :]
                 left = jnp.where(first, went[t - 1], went[t])
                 right = jnp.where(last, came[(t + 1) % tiles], came[t])
                 slope_x = jnp.maximum(value - jnp.minimum(up, down), 0.0)
@@ -183,10 +168,7 @@
                 ok = row_ok
                 if t == tiles - 1:
                     ok = side_ok if ok is None else ok & side_ok
-                dst[i : i + 8, t * 128 : (t + 1) * 128] = (
-                    new if ok is None else jnp.where(ok, new, 0.0)
-                )
-            here, fell_before, fell, rose = after, fell, fell_after, rose_after
+                dst[t, i : i + 8, :] = new if ok is None else jnp.where(ok, new, 0.0)
         src, dst = dst, src
     return src
 
@@ -224,8 +206,7 @@
                 halves = []
                 for j in range(2):
                     at = PAD + i + 8 * j
-                    one = u[at : at + 8, 2 * t * 128 : (2 * t + 1) * 128]
-                    two = u[at : at + 8, (2 * t + 1) * 128 : (2 * t + 2) * 128]
+                    one, two = u[2 * t, at : at + 8, :], u[2 * t + 1, at : at + 8, :]
                     halves.append(
                         jnp.where(lower, lane_pick(one, index), lane_pick(two, index))
                     )
@@ -233,11 +214,11 @@
                 tabs[parity][i : i + 16, t * 128 : (t + 1) * 128] = high
                 tabs[parity][high_rows + i : high_rows + i + 16, t * 128 : (t + 1) * 128] = low
         halo[i : i + 16, :] = jnp.broadcast_to(
-            u[PAD + i : PAD + i + 16, cols : cols + 1], (16, 128)
+            u[cols // 128, PAD + i : PAD + i + 16, 0:1], (16, 128)
         )
 
 
-def fill_slots(rows, blocks, cap, first, dest, slot_row, corner_row, counter):
+def fill_slots(blocks, cap, first, dest, slot_row, corner_row, counter):
     n_cols = lax.axis_size("cols")
     my_row, my_col = lax.axis_index("rows"), lax.axis_index("cols")
     n_rows = lax.axis_size("rows")
@@ -342,12 +323,13 @@
         east = pick(col_even, ra_ref[part, :], rb_ref[part, :])
         dst[:, 0:cols] = src[:, 0:cols]
         dst[:, cols : cols + 128] = unflipped(side_tile(west, east, width), tall)
-    ua[...] = ue_ref[...]
+    for t in range(cols // 128 + 1):
+        ua[t] = ue_ref[:, t * 128 : (t + 1) * 128]
     ub[...] = jnp.zeros(ub.shape, F32)
 
     def place_blocks():
         fetch.wait()
-        fill_slots(rows, blocks, cap, True, dest, slot_row, corner_row, counter)
+        fill_slots(blocks, cap, True, dest, slot_row, corner_row, counter)
 
     u = hjb_sweep(rows, cols, ua, ub, me_ref, place_blocks)
     tabs = (tab_even, tab_odd)
@@ -367,7 +349,7 @@
     (starts, offs, wts, ends, dest_hbm) = refs[7:12]
     outs = refs[12 : 12 + n_cols]
     value_hbm, density_ref, total_ref = refs[12 + n_cols : 15 + n_cols]
-    (ua, ub, m, tab_even, tab_odd, halo, buf, slot_row, corner_row, counter, dest, sem, value_sem) = (
+    (ua, ub, m, tab_even, tab_odd, halo, buf, slot_row, corner_row, counter, dest, sem, value_sems) = (
         refs[15 + n_cols :]
     )
     total_ref[...] = total_in[...] + more_in[...]
@@ -390,16 +372,25 @@
         d_ref[:, cols : cols + 128] + side
     )
     density_ref[...] = m[PAD : PAD + rows, 0:cols]
-    ua[...] = ue_ref[...]
+    for t in range(cols // 128 + 1):
+        ua[t] = ue_ref[:, t * 128 : (t + 1) * 128]
     ub[...] = jnp.zeros(ub.shape, F32)
 
     def place_blocks():
         fetch.wait()
-        fill_slots(rows, blocks, cap, False, dest, slot_row, corner_row, counter)
+        fill_slots(blocks, cap, False, dest, slot_row, corner_row, counter)
 
     u = hjb_sweep(rows, cols, ua, ub, m, place_blocks)
-    leave = pltpu.make_async_copy(u.at[PAD : PAD + rows, 0:cols], value_hbm, value_sem)
-    leave.start()
+    leaving = [
+        pltpu.make_async_copy(
+            u.at[t, PAD : PAD + rows, :],
+            value_hbm.at[:, t * 128 : (t + 1) * 128],
+            value_sems.at[t],
+        )
+        for t in range(cols // 128)
+    ]
+    for leave in leaving:
+        leave.start()
     tabs = (tab_even, tab_odd)
     fill_tables(rows, cols, u, tabs, halo)
     sample_moves(
@@ -408,7 +399,8 @@
     part_rows = 6 * cap + EDGE
     for k in range(n_cols):
         outs[(n_cols - k) % n_cols][...] = buf[k * part_rows : (k + 1) * part_rows, :]
-    leave.wait()
+    for leave in leaving:
+        leave.wait()
 
 
 def deposit_blocks(rows, cols, cap, chunks, moves, masses, scratch, slots):
@@ -678,10 +670,7 @@
         5,
     )(terminal_value, density_start, ra, rb, sa)
     ca, cb = swap_both(ca, cb, "cols")
-    sweep_scratch = [
-        pltpu.VMEM((tall, wide), F32),
-        pltpu.VMEM((tall, wide), F32),
-    ]
+    sweep_scratch = [pltpu.VMEM((wide // 128, tall, 128), F32)] * 2
 
     def sample_scratch(part_rows):
         return [
@@ -763,7 +752,7 @@
         sweep_scratch
         + [pltpu.VMEM((tall, wide), F32)]
         + sample_scratch(part_rows)
-        + [pltpu.SemaphoreType.DMA(())],
+        + [pltpu.SemaphoreType.DMA((cols // 128,))],
         hbm_in=(11,),
         hbm_out=(n_cols,),
     )(ue, me, deposit, ca, cb, total, more, starts, offsets, wts, ends, dest_tiles)

time: 79.2 us -> 78.3 us (0.989)
  Pallas kernels: 16.3 us -> 12.7 us
  waiting for transfers between devices: 17.9 us -> 19.8 us
  starting transfers between devices: 42.7 us -> 44.2 us
    pallas_call x10, Pallas kernels: 16.3 us -> 12.7 us  [run(): call(*[pltpu.with_memory_space_constraint(x, pltpu.HBM if i in hbm_in els...]
    ppermute x6, waiting for transfers between devices: 8.08 us -> 10.4 us  [swap_both(): lax.ppermute(second, axis, pairs_b)]
    ppermute x6, starting transfers between devices: 21.4 us -> 23.3 us  [swap_both(): lax.ppermute(second, axis, pairs_b)]
  transfers between devices with their start and end apart: 22 -> 22, of which waited for: 10 -> 12; matrix products, arithmetic and copies ran while one was open for 0% -> 0% of each run, Pallas kernels for 5% -> 3%
where the time goes in v3:
time: 78.3 us; the launch traced here: 77.6 us
  starting transfers between devices  44.2 us (56%)
  waiting for transfers between devices  19.8 us (25%)
  Pallas kernels  12.7 us (16%)
  between operations  0.87 us (1%)
    ppermute x6, starting transfers between devices, swap_both(): lax.ppermute(second, axis, pairs_b)  23.3 us
    pallas_call x10, Pallas kernels, run(): call(*[pltpu.with_memory_space_constraint(x, pltpu.HBM if i in hbm_in els...  12.7 us
    ppermute x6, waiting for transfers between devices, swap_both(): lax.ppermute(second, axis, pairs_b)  10.4 us
    ppermute x6, starting transfers between devices, swap_both(): lax.ppermute(first, axis, pairs_a)  8.11 us
    ppermute x8, waiting for transfers between devices, xor_permute(): lax.ppermute(value, axis, [(i, i ^ bit) for i in range(lax.axis_size(axis...  6.91 us
    ppermute x8, starting transfers between devices, xor_permute(): lax.ppermute(value, axis, [(i, i ^ bit) for i in range(lax.axis_size(axis...  5.84 us
    ppermute x1, starting transfers between devices, body(): below = lax.ppermute(below, 'rows', [(i, i + 1) for i in range(n_rows - 1)])  5.03 us
    ppermute x1, waiting for transfers between devices, body(): lax.ppermute(beside, 'cols', [(i, i + 1) for i in range(n_cols - 1)])  2.42 us
  transfers between devices with their start and end apart: 22, of which 12 were waited for; matrix products, arithmetic and copies ran while one was open for 0% of the time, Pallas kernels for 3%

profile of v3, /device:TPU:11, one launch (start us, length us, event | category | flops | bytes accessed | tf_op | source)
XLA Modules:
  0.0 77.6 jit_solution(8242901793291462902)
XLA Ops:
  0.6 1.2 %shard_map.86 = (f32[128,512]{1,0:T(8,128)S(1)}, f32[128,512]{1,0:T(8,128)S(1)}, f32[32,128]{1,0:T(8,128)S(1)}, s32[32,128]{1,0:T(8,128)S(1)}, f32[2,4096]{1,0:T...) custom-call(f32[128,512]{1,0:T(8,128)} %refs_0_.1, f32[128,512]{1,0:T(8,128)} %refs_1_.1, ...), custom_call_target="tpu_custom_call" | custom-call | tf_op jit(solution)/shard_map/pallas_call | solution.py:52
  1.8 0.7 collective-permute-start
  2.6 3.0 %collective-permute-start.1 = (f32[16,512]{1,0:T(8,128)S(1)}, f32[16,512]{1,0:T(8,128)S(1)}, u32[]{:S(2)}, u32[]{:S(2)}) collective-permute-start(f32[16,512]{1,0:T(8,128)S(1)} %get-tuple-element.49), channel_id=1, source_target_pairs={{4,8},{8,4},{12,16},{16,12},{20,24},{24,20},{5,9},{9,5},{13,17},{1... | collective-permute-start | bytes 98312 | tf_op jit(solution)/shard_map/ppermute | solution.py:27
  5.6 3.1 %collective-permute-done.1.b_ref = f32[16,512]{1,0:T(8,128)S(1)} collective-permute-done((f32[16,512]{1,0:T(8,128)S(1)}, f32[16,512]{1,0:T(8,128)S(1)}, u32[]{:S(2)}, u32[]{:S(2)}) %collective-permute-start.1) | collective-permute-done | bytes 32800 | tf_op jit(solution)/shard_map/ppermute | solution.py:27
  8.7 0.0 collective-permute-done.a_ref
  8.7 0.2 shard_map.87
  8.9 0.2 collective-permute-start.2
  9.1 4.3 %collective-permute-start.3 = (f32[16,256]{1,0:T(8,128)S(1)}, f32[16,256]{1,0:T(8,128)S(1)}, u32[]{:S(2)}, u32[]{:S(2)}) collective-permute-start(f32[16,256]{1,0:T(8,128)S(1)} %get-tuple-element.53), channel_id=1, source_target_pairs={{1,2},{2,1},{5,6},{6,5},{9,10},{10,9},{13,14},{14,13},{17,18},{18,... | collective-permute-start | bytes 49160 | tf_op jit(solution)/shard_map/ppermute | solution.py:27
  13.4 1.1 %collective-permute-done.3.refs_3_ = f32[16,256]{1,0:T(8,128)S(1)} collective-permute-done((f32[16,256]{1,0:T(8,128)S(1)}, f32[16,256]{1,0:T(8,128)S(1)}, u32[]{:S(2)}, u32[]{:S(2)}) %collective-permute-start.3) | collective-permute-done | bytes 16416 | tf_op jit(solution)/shard_map/ppermute | solution.py:27
  14.5 4.0 %shard_map.88 = (f32[104,128]{1,0:T(8,128)S(1)}, f32[104,128]{1,0:T(8,128)S(1)}, f32[104,128]{1,0:T(8,128)S(1)}, f32[104,128]{1,0:T(8,128)S(1)}, f32[160,640]{1,0:T(8,128)S(1)}, /*index=5*/f32[160,640]{1,0:T(8,128)S(1)}) custom-call(f32[160,640]{1,0:T(8,128)S(1)} %get-tuple-element.50.refs_0_, f32[160,640]{1,0:T(8,128)S(1)} %get-tuple-element.51.refs_1_, ...), custom_call_target="tpu_custom_call" | custom-call | tf_op jit(solution)/shard_map/pallas_call | solution.py:52
  18.6 1.7 %collective-permute-start.4 = (f32[104,128]{1,0:T(8,128)S(1)}, f32[104,128]{1,0:T(8,128)S(1)}, u32[]{:S(2)}, u32[]{:S(2)}) collective-permute-start(f32[104,128]{1,0:T(8,128)S(1)} %get-tuple-element.62), channel_id=1, source_target_pairs={{0,3},{1,2},{2,1},{3,0},{4,7},{5,6},{6,5},{7,4},{8,11},{9,10},{10,... | collective-permute-start | bytes 159752 | tf_op jit(solution)/shard_map/ppermute | solution.py:31
  20.3 0.0 collective-permute-start.5
  20.3 1.3 %collective-permute-start.6 = (f32[104,128]{1,0:T(8,128)S(1)}, f32[104,128]{1,0:T(8,128)S(1)}, u32[]{:S(2)}, u32[]{:S(2)}) collective-permute-start(f32[104,128]{1,0:T(8,128)S(1)} %get-tuple-element.64), channel_id=1, source_target_pairs={{0,1},{1,0},{2,3},{3,2},{4,5},{5,4},{6,7},{7,6},{8,9},{9,8},{10,11... | collective-permute-start | bytes 159752 | tf_op jit(solution)/shard_map/ppermute | solution.py:31
  21.6 0.2 collective-permute-done.4.refs_1_
  21.8 2.4 %collective-permute-done.5.refs_2_ = f32[104,128]{1,0:T(8,128)S(1)} collective-permute-done((f32[104,128]{1,0:T(8,128)S(1)}, f32[104,128]{1,0:T(8,128)S(1)}, u32[]{:S(2)}, u32[]{:S(2)}) %collective-permute-start.5) | collective-permute-done | bytes 53280 | tf_op jit(solution)/shard_map/ppermute | solution.py:31
  24.2 0.0 collective-permute-done.6.refs_3_
  24.2 1.9 %collective-permute-start.7 = (f32[128,128]{1,0:T(8,128)S(1)}, f32[128,128]{1,0:T(8,128)S(1)}, u32[]{:S(2)}, u32[]{:S(2)}) collective-permute-start(f32[128,128]{1,0:T(8,128)S(1)} %pad_maximum_fusion), channel_id=1, source_target_pairs={{0,4},{4,0},{8,12},{12,8},{16,20},{20,16},{24,28},{28,24},{1,5},{5... | collective-permute-start | bytes 196616 | tf_op jit(solution)/shard_map/ppermute | solution.py:27
  26.1 3.9 %collective-permute-start.8 = (f32[128,128]{1,0:T(8,128)S(1)}, f32[128,128]{1,0:T(8,128)S(1)}, u32[]{:S(2)}, u32[]{:S(2)}) collective-permute-start(f32[128,128]{1,0:T(8,128)S(1)} %pad_maximum_fusion.1), channel_id=1, source_target_pairs={{4,8},{8,4},{12,16},{16,12},{20,24},{24,20},{5,9},{9,5},{13,17},{1... | collective-permute-start | bytes 196616 | tf_op jit(solution)/shard_map/ppermute | solution.py:27
  30.1 0.1 collective-permute-start.9
  30.2 0.7 shard_map.89
  30.9 0.0 collective-permute-done.7.refs_0_
  30.9 1.8 %collective-permute-done.8.refs_1_ = f32[128,128]{1,0:T(8,128)S(1)} collective-permute-done((f32[128,128]{1,0:T(8,128)S(1)}, f32[128,128]{1,0:T(8,128)S(1)}, u32[]{:S(2)}, u32[]{:S(2)}) %collective-permute-start.8) | collective-permute-done | bytes 65568 | tf_op jit(solution)/shard_map/ppermute | solution.py:27
  32.7 0.5 shard_map.90
  33.2 0.0 collective-permute-done.9
  33.3 1.8 %collective-permute-start.10 = (f32[8,640]{1,0:T(8,128)S(1)}, f32[8,640]{1,0:T(8,128)S(1)}, u32[]{:S(2)}, u32[]{:S(2)}) collective-permute-start(f32[8,640]{1,0:T(8,128)S(1)} %get-tuple-element.70), channel_id=1, source_target_pairs={{0,4},{4,0},{8,12},{12,8},{16,20},{20,16},{24,28},{28,24},{1,5},{5... | collective-permute-start | bytes 61448 | tf_op jit(solution)/shard_map/ppermute | solution.py:27
  35.1 4.3 %collective-permute-start.11 = (f32[8,640]{1,0:T(8,128)S(1)}, f32[8,640]{1,0:T(8,128)S(1)}, u32[]{:S(2)}, u32[]{:S(2)}) collective-permute-start(f32[8,640]{1,0:T(8,128)S(1)} %get-tuple-element.71), channel_id=1, source_target_pairs={{4,8},{8,4},{12,16},{16,12},{20,24},{24,20},{5,9},{9,5},{13,17},{1... | collective-permute-start | bytes 61448 | tf_op jit(solution)/shard_map/ppermute | solution.py:27
  39.4 1.8 %collective-permute-done.11.b_ref = f32[8,640]{1,0:T(8,128)S(1)} collective-permute-done((f32[8,640]{1,0:T(8,128)S(1)}, f32[8,640]{1,0:T(8,128)S(1)}, u32[]{:S(2)}, u32[]{:S(2)}) %collective-permute-start.11) | collective-permute-done | bytes 20512 | tf_op jit(solution)/shard_map/ppermute | solution.py:27
  41.2 0.1 shard_map.91
  41.3 0.9 %collective-permute-start.12 = (f32[16,256]{1,0:T(8,128)S(1)}, f32[16,256]{1,0:T(8,128)S(1)}, u32[]{:S(2)}, u32[]{:S(2)}) collective-permute-start(f32[16,256]{1,0:T(8,128)S(1)} %get-tuple-element.73), channel_id=1, source_target_pairs={{0,1},{1,0},{2,3},{3,2},{4,5},{5,4},{6,7},{7,6},{8,9},{9,8},{10,11... | collective-permute-start | bytes 49160 | tf_op jit(solution)/shard_map/ppermute | solution.py:27
  42.3 4.9 %collective-permute-start.13 = (f32[16,256]{1,0:T(8,128)S(1)}, f32[16,256]{1,0:T(8,128)S(1)}, u32[]{:S(2)}, u32[]{:S(2)}) collective-permute-start(f32[16,256]{1,0:T(8,128)S(1)} %get-tuple-element.74), channel_id=1, source_target_pairs={{1,2},{2,1},{5,6},{6,5},{9,10},{10,9},{13,14},{14,13},{17,18},{18,... | collective-permute-start | bytes 49160 | tf_op jit(solution)/shard_map/ppermute | solution.py:27
  47.2 0.1 collective-permute-start.14
  47.3 2.4 %collective-permute-done.14.refs_6_ = f32[8,128]{1,0:T(8,128)S(1)} collective-permute-done((f32[8,128]{1,0:T(8,128)S(1)}, f32[8,128]{1,0:T(8,128)S(1)}, u32[]{:S(2)}, u32[]{:S(2)}) %collective-permute-start.14) | collective-permute-done | bytes 4128 | tf_op jit(solution)/shard_map/ppermute | solution.py:31
  49.8 3.8 %shard_map.92 = (f32[56,128]{1,0:T(8,128)S(1)}, f32[56,128]{1,0:T(8,128)S(1)}, f32[56,128]{1,0:T(8,128)S(1)}, f32[56,128]{1,0:T(8,128)S(1)}, f32[128,512]{1,0:T(...) custom-call(f32[160,640]{1,0:T(8,128)S(1)} %get-tuple-element.59.refs_0_, ...), custom_call_target="tpu_custom_call" | custom-call | tf_op jit(solution)/shard_map/pallas_call | solution.py:52
  53.6 0.1 collective-permute-start.15
  53.7 0.1 collective-permute-start.16
  53.7 2.6 %collective-permute-start.17 = (f32[56,128]{1,0:T(8,128)S(1)}, f32[56,128]{1,0:T(8,128)S(1)}, u32[]{:S(2)}, u32[]{:S(2)}) collective-permute-start(f32[56,128]{1,0:T(8,128)S(1)} %get-tuple-element.80), channel_id=1, source_target_pairs={{0,1},{1,0},{2,3},{3,2},{4,5},{5,4},{6,7},{7,6},{8,9},{9,8},{10,11... | collective-permute-start | bytes 86024 | tf_op jit(solution)/shard_map/ppermute | solution.py:31
  56.3 0.1 collective-permute-done.15.refs_1_
  56.4 1.0 %collective-permute-done.16.refs_2_ = f32[56,128]{1,0:T(8,128)S(1)} collective-permute-done((f32[56,128]{1,0:T(8,128)S(1)}, f32[56,128]{1,0:T(8,128)S(1)}, u32[]{:S(2)}, u32[]{:S(2)}) %collective-permute-start.16) | collective-permute-done | bytes 28704 | tf_op jit(solution)/shard_map/ppermute | solution.py:31
  57.3 0.8 %collective-permute-done.17.refs_3_ = f32[56,128]{1,0:T(8,128)S(1)} collective-permute-done((f32[56,128]{1,0:T(8,128)S(1)}, f32[56,128]{1,0:T(8,128)S(1)}, u32[]{:S(2)}, u32[]{:S(2)}) %collective-permute-start.17) | collective-permute-done | bytes 28704 | tf_op jit(solution)/shard_map/ppermute | solution.py:31
  58.2 2.5 %collective-permute-start.18 = (f32[72,128]{1,0:T(8,128)S(1)}, f32[72,128]{1,0:T(8,128)S(1)}, u32[]{:S(2)}, u32[]{:S(2)}) collective-permute-start(f32[72,128]{1,0:T(8,128)S(1)} %constant_dynamic-update-slice_fusion), channel_id=1, source_target_pairs={{0,4},{4,0},{8,12},{12,8},{16,20},{20,16},{24,28},{28,24},{1,5},{5... | collective-permute-start | bytes 110600 | tf_op jit(solution)/shard_map/ppermute | solution.py:27
  60.7 2.8 %collective-permute-start.19 = (f32[72,128]{1,0:T(8,128)S(1)}, f32[72,128]{1,0:T(8,128)S(1)}, u32[]{:S(2)}, u32[]{:S(2)}) collective-permute-start(f32[72,128]{1,0:T(8,128)S(1)} %get-tuple-element.90), channel_id=1, source_target_pairs={{4,8},{8,4},{12,16},{16,12},{20,24},{24,20},{5,9},{9,5},{13,17},{1... | collective-permute-start | bytes 110600 | tf_op jit(solution)/shard_map/ppermute | solution.py:27
  63.5 0.7 shard_map.93
  64.2 2.6 %collective-permute-done.19.refs_1_ = f32[72,128]{1,0:T(8,128)S(1)} collective-permute-done((f32[72,128]{1,0:T(8,128)S(1)}, f32[72,128]{1,0:T(8,128)S(1)}, u32[]{:S(2)}, u32[]{:S(2)}) %collective-permute-start.19) | collective-permute-done | bytes 36896 | tf_op jit(solution)/shard_map/ppermute | solution.py:27
  66.8 0.6 shard_map.94
  67.4 5.0 %collective-permute-start.20 = (f32[8,512]{1,0:T(8,128)S(1)}, f32[8,512]{1,0:T(8,128)S(1)}, u32[]{:S(2)}, u32[]{:S(2)}) collective-permute-start(f32[8,512]{1,0:T(8,128)S(1)} %get-tuple-element.87), channel_id=1, source_target_pairs={{0,4},{4,8},{8,12},{12,16},{16,20},{20,24},{24,28},{1,5},{5,9},{9,... | collective-permute-start | bytes 49160 | tf_op jit(solution)/shard_map/ppermute | solution.py:774
  72.4 1.9 %collective-permute-start.21 = (f32[8,128]{1,0:T(8,128)S(1)}, f32[8,128]{1,0:T(8,128)S(1)}, u32[]{:S(2)}, u32[]{:S(2)}) collective-permute-start(f32[8,128]{1,0:T(8,128)S(1)} %get-tuple-element.88), channel_id=1, source_target_pairs={{0,1},{1,2},{2,3},{4,5},{5,6},{6,7},{8,9},{9,10},{10,11},{12,13},{... | collective-permute-start | bytes 12296 | tf_op jit(solution)/shard_map/ppermute | solution.py:775
  74.4 2.4 %collective-permute-done.21.col_in = f32[8,128]{1,0:T(8,128)S(1)} collective-permute-done((f32[8,128]{1,0:T(8,128)S(1)}, f32[8,128]{1,0:T(8,128)S(1)}, u32[]{:S(2)}, u32[]{:S(2)}) %collective-permute-start.21) | collective-permute-done | bytes 4128 | tf_op jit(solution)/shard_map/ppermute | solution.py:775
  76.8 0.8 %shard_map.95 = f32[128,512]{1,0:T(8,128)} custom-call(f32[136,640]{1,0:T(8,128)S(1)} %get-tuple-element.85.g_ref, f32[128,512]{1,0:T(8,128)S(1)} %get-tuple-element.86.m_ref, f32[8,512]{1,0:T(8,128)S(1)} %collective-permute-done.20.row_in, f32[8,128]{1,0:T(8,128)S(1)} %collective-permute-done.21.col_in, f32[8,128]{1,0:T(8,128)S(1)} %get-tuple-element.89.total_ref), custom_call_target="tpu_custom_call" | custom-call | tf_op jit(solution)/shard_map/pallas_call | solution.py:52
  (20 shorter events, 0.1 us)
Async XLA Ops:
  1.8 6.9 %collective-permute-start = (f32[24,512]{1,0:T(8,128)S(1)}, f32[24,512]{1,0:T(8,128)S(1)}, u32[]{:S(2)}, u32[]{:S(2)}) collective-permute-start(f32[24,512]{1,0:T(8,128)S(1)} %get-tuple-element.48.s_ref), channel_id=1, source_target_pairs={{0,4},{4,0},{8,12},{12,8},{16,20},{20,16},{24,28},{28,24},{1,5},{5... | collective-permute-start | bytes 147464 | tf_op jit(solution)/shard_map/ppermute | solution.py:27
  2.6 6.1 %collective-permute-start.1 = (f32[16,512]{1,0:T(8,128)S(1)}, f32[16,512]{1,0:T(8,128)S(1)}, u32[]{:S(2)}, u32[]{:S(2)}) collective-permute-start(f32[16,512]{1,0:T(8,128)S(1)} %get-tuple-element.49), channel_id=1, source_target_pairs={{4,8},{8,4},{12,16},{16,12},{20,24},{24,20},{5,9},{9,5},{13,17},{1... | collective-permute-start | bytes 98312 | tf_op jit(solution)/shard_map/ppermute | solution.py:27
  8.9 4.6 %collective-permute-start.2 = (f32[16,256]{1,0:T(8,128)S(1)}, f32[16,256]{1,0:T(8,128)S(1)}, u32[]{:S(2)}, u32[]{:S(2)}) collective-permute-start(f32[16,256]{1,0:T(8,128)S(1)} %get-tuple-element.52), channel_id=1, source_target_pairs={{0,1},{1,0},{2,3},{3,2},{4,5},{5,4},{6,7},{7,6},{8,9},{9,8},{10,11... | collective-permute-start | bytes 49160 | tf_op jit(solution)/shard_map/ppermute | solution.py:27
  9.1 5.4 %collective-permute-start.3 = (f32[16,256]{1,0:T(8,128)S(1)}, f32[16,256]{1,0:T(8,128)S(1)}, u32[]{:S(2)}, u32[]{:S(2)}) collective-permute-start(f32[16,256]{1,0:T(8,128)S(1)} %get-tuple-element.53), channel_id=1, source_target_pairs={{1,2},{2,1},{5,6},{6,5},{9,10},{10,9},{13,14},{14,13},{17,18},{18,... | collective-permute-start | bytes 49160 | tf_op jit(solution)/shard_map/ppermute | solution.py:27
  18.6 3.2 %collective-permute-start.4 = (f32[104,128]{1,0:T(8,128)S(1)}, f32[104,128]{1,0:T(8,128)S(1)}, u32[]{:S(2)}, u32[]{:S(2)}) collective-permute-start(f32[104,128]{1,0:T(8,128)S(1)} %get-tuple-element.62), channel_id=1, source_target_pairs={{0,3},{1,2},{2,1},{3,0},{4,7},{5,6},{6,5},{7,4},{8,11},{9,10},{10,... | collective-permute-start | bytes 159752 | tf_op jit(solution)/shard_map/ppermute | solution.py:31
  20.3 3.9 %collective-permute-start.5 = (f32[104,128]{1,0:T(8,128)S(1)}, f32[104,128]{1,0:T(8,128)S(1)}, u32[]{:S(2)}, u32[]{:S(2)}) collective-permute-start(f32[104,128]{1,0:T(8,128)S(1)} %get-tuple-element.63), channel_id=1, source_target_pairs={{0,2},{1,3},{2,0},{3,1},{4,6},{5,7},{6,4},{7,5},{8,10},{9,11},{10,... | collective-permute-start | bytes 159752 | tf_op jit(solution)/shard_map/ppermute | solution.py:31
  20.3 3.9 %collective-permute-start.6 = (f32[104,128]{1,0:T(8,128)S(1)}, f32[104,128]{1,0:T(8,128)S(1)}, u32[]{:S(2)}, u32[]{:S(2)}) collective-permute-start(f32[104,128]{1,0:T(8,128)S(1)} %get-tuple-element.64), channel_id=1, source_target_pairs={{0,1},{1,0},{2,3},{3,2},{4,5},{5,4},{6,7},{7,6},{8,9},{9,8},{10,11... | collective-permute-start | bytes 159752 | tf_op jit(solution)/shard_map/ppermute | solution.py:31
  24.2 6.7 %collective-permute-start.7 = (f32[128,128]{1,0:T(8,128)S(1)}, f32[128,128]{1,0:T(8,128)S(1)}, u32[]{:S(2)}, u32[]{:S(2)}) collective-permute-start(f32[128,128]{1,0:T(8,128)S(1)} %pad_maximum_fusion), channel_id=1, source_target_pairs={{0,4},{4,0},{8,12},{12,8},{16,20},{20,16},{24,28},{28,24},{1,5},{5... | collective-permute-start | bytes 196616 | tf_op jit(solution)/shard_map/ppermute | solution.py:27
  26.1 6.6 %collective-permute-start.8 = (f32[128,128]{1,0:T(8,128)S(1)}, f32[128,128]{1,0:T(8,128)S(1)}, u32[]{:S(2)}, u32[]{:S(2)}) collective-permute-start(f32[128,128]{1,0:T(8,128)S(1)} %pad_maximum_fusion.1), channel_id=1, source_target_pairs={{4,8},{8,4},{12,16},{16,12},{20,24},{24,20},{5,9},{9,5},{13,17},{1... | collective-permute-start | bytes 196616 | tf_op jit(solution)/shard_map/ppermute | solution.py:27
  30.1 3.2 %collective-permute-start.9 = (f32[8,128]{1,0:T(8,128)S(1)}, f32[8,128]{1,0:T(8,128)S(1)}, u32[]{:S(2)}, u32[]{:S(2)}) collective-permute-start(f32[8,128]{1,0:T(8,128)S(1)} %slice_add_fusion.3), channel_id=1, source_target_pairs={{0,8},{4,12},{8,0},{12,4},{16,24},{20,28},{24,16},{28,20},{1,9},{5... | collective-permute-start | bytes 12296 | tf_op jit(solution)/shard_map/ppermute | solution.py:31
  33.3 6.1 %collective-permute-start.10 = (f32[8,640]{1,0:T(8,128)S(1)}, f32[8,640]{1,0:T(8,128)S(1)}, u32[]{:S(2)}, u32[]{:S(2)}) collective-permute-start(f32[8,640]{1,0:T(8,128)S(1)} %get-tuple-element.70), channel_id=1, source_target_pairs={{0,4},{4,0},{8,12},{12,8},{16,20},{20,16},{24,28},{28,24},{1,5},{5... | collective-permute-start | bytes 61448 | tf_op jit(solution)/shard_map/ppermute | solution.py:27
  35.1 6.1 %collective-permute-start.11 = (f32[8,640]{1,0:T(8,128)S(1)}, f32[8,640]{1,0:T(8,128)S(1)}, u32[]{:S(2)}, u32[]{:S(2)}) collective-permute-start(f32[8,640]{1,0:T(8,128)S(1)} %get-tuple-element.71), channel_id=1, source_target_pairs={{4,8},{8,4},{12,16},{16,12},{20,24},{24,20},{5,9},{9,5},{13,17},{1... | collective-permute-start | bytes 61448 | tf_op jit(solution)/shard_map/ppermute | solution.py:27
  41.3 8.4 %collective-permute-start.12 = (f32[16,256]{1,0:T(8,128)S(1)}, f32[16,256]{1,0:T(8,128)S(1)}, u32[]{:S(2)}, u32[]{:S(2)}) collective-permute-start(f32[16,256]{1,0:T(8,128)S(1)} %get-tuple-element.73), channel_id=1, source_target_pairs={{0,1},{1,0},{2,3},{3,2},{4,5},{5,4},{6,7},{7,6},{8,9},{9,8},{10,11... | collective-permute-start | bytes 49160 | tf_op jit(solution)/shard_map/ppermute | solution.py:27
  42.3 7.5 %collective-permute-start.13 = (f32[16,256]{1,0:T(8,128)S(1)}, f32[16,256]{1,0:T(8,128)S(1)}, u32[]{:S(2)}, u32[]{:S(2)}) collective-permute-start(f32[16,256]{1,0:T(8,128)S(1)} %get-tuple-element.74), channel_id=1, source_target_pairs={{1,2},{2,1},{5,6},{6,5},{9,10},{10,9},{13,14},{14,13},{17,18},{18,... | collective-permute-start | bytes 49160 | tf_op jit(solution)/shard_map/ppermute | solution.py:27
  47.2 2.5 %collective-permute-start.14 = (f32[8,128]{1,0:T(8,128)S(1)}, f32[8,128]{1,0:T(8,128)S(1)}, u32[]{:S(2)}, u32[]{:S(2)}) collective-permute-start(f32[8,128]{1,0:T(8,128)S(1)} %add.24.refs_5_), channel_id=1, source_target_pairs={{0,16},{4,20},{8,24},{12,28},{16,0},{20,4},{24,8},{28,12},{1,17},{... | collective-permute-start | bytes 12296 | tf_op jit(solution)/shard_map/ppermute | solution.py:31
  53.6 2.8 %collective-permute-start.15 = (f32[56,128]{1,0:T(8,128)S(1)}, f32[56,128]{1,0:T(8,128)S(1)}, u32[]{:S(2)}, u32[]{:S(2)}) collective-permute-start(f32[56,128]{1,0:T(8,128)S(1)} %get-tuple-element.78), channel_id=1, source_target_pairs={{0,3},{1,2},{2,1},{3,0},{4,7},{5,6},{6,5},{7,4},{8,11},{9,10},{10,... | collective-permute-start | bytes 86024 | tf_op jit(solution)/shard_map/ppermute | solution.py:31
  53.7 3.7 %collective-permute-start.16 = (f32[56,128]{1,0:T(8,128)S(1)}, f32[56,128]{1,0:T(8,128)S(1)}, u32[]{:S(2)}, u32[]{:S(2)}) collective-permute-start(f32[56,128]{1,0:T(8,128)S(1)} %get-tuple-element.79), channel_id=1, source_target_pairs={{0,2},{1,3},{2,0},{3,1},{4,6},{5,7},{6,4},{7,5},{8,10},{9,11},{10,... | collective-permute-start | bytes 86024 | tf_op jit(solution)/shard_map/ppermute | solution.py:31
  53.7 4.4 %collective-permute-start.17 = (f32[56,128]{1,0:T(8,128)S(1)}, f32[56,128]{1,0:T(8,128)S(1)}, u32[]{:S(2)}, u32[]{:S(2)}) collective-permute-start(f32[56,128]{1,0:T(8,128)S(1)} %get-tuple-element.80), channel_id=1, source_target_pairs={{0,1},{1,0},{2,3},{3,2},{4,5},{5,4},{6,7},{7,6},{8,9},{9,8},{10,11... | collective-permute-start | bytes 86024 | tf_op jit(solution)/shard_map/ppermute | solution.py:31
  58.2 6.1 %collective-permute-start.18 = (f32[72,128]{1,0:T(8,128)S(1)}, f32[72,128]{1,0:T(8,128)S(1)}, u32[]{:S(2)}, u32[]{:S(2)}) collective-permute-start(f32[72,128]{1,0:T(8,128)S(1)} %constant_dynamic-update-slice_fusion), channel_id=1, source_target_pairs={{0,4},{4,0},{8,12},{12,8},{16,20},{20,16},{24,28},{28,24},{1,5},{5... | collective-permute-start | bytes 110600 | tf_op jit(solution)/shard_map/ppermute | solution.py:27
  60.7 6.2 %collective-permute-start.19 = (f32[72,128]{1,0:T(8,128)S(1)}, f32[72,128]{1,0:T(8,128)S(1)}, u32[]{:S(2)}, u32[]{:S(2)}) collective-permute-start(f32[72,128]{1,0:T(8,128)S(1)} %get-tuple-element.90), channel_id=1, source_target_pairs={{4,8},{8,4},{12,16},{16,12},{20,24},{24,20},{5,9},{9,5},{13,17},{1... | collective-permute-start | bytes 110600 | tf_op jit(solution)/shard_map/ppermute | solution.py:27
  67.4 9.4 %collective-permute-start.20 = (f32[8,512]{1,0:T(8,128)S(1)}, f32[8,512]{1,0:T(8,128)S(1)}, u32[]{:S(2)}, u32[]{:S(2)}) collective-permute-start(f32[8,512]{1,0:T(8,128)S(1)} %get-tuple-element.87), channel_id=1, source_target_pairs={{0,4},{4,8},{8,12},{12,16},{16,20},{20,24},{24,28},{1,5},{5,9},{9,... | collective-permute-start | bytes 49160 | tf_op jit(solution)/shard_map/ppermute | solution.py:774
  72.4 4.4 %collective-permute-start.21 = (f32[8,128]{1,0:T(8,128)S(1)}, f32[8,128]{1,0:T(8,128)S(1)}, u32[]{:S(2)}, u32[]{:S(2)}) collective-permute-start(f32[8,128]{1,0:T(8,128)S(1)} %get-tuple-element.88), channel_id=1, source_target_pairs={{0,1},{1,2},{2,3},{4,5},{5,6},{6,7},{8,9},{9,10},{10,11},{12,13},{... | collective-permute-start | bytes 12296 | tf_op jit(solution)/shard_map/ppermute | solution.py:775

commit v4 on v3

--- a/solution.py
+++ b/solution.py
@@ -12,7 +12,6 @@
 PAD = 16
 EDGE = 8
 GROUP = 4
-UNROLL = 4
 VMEM_LIMIT = 24 * 1024 * 1024
 
 
@@ -302,7 +301,7 @@
                 buf[pl.ds(base + q * cap, 1), :] = value[:, half * 128 : (half + 1) * 128]
         return carry
 
-    lax.fori_loop(0, blocks // 2, step, 0, unroll=UNROLL)
+    lax.fori_loop(0, blocks // 2, step, 0, unroll=True if first else 4)
 
 
 def first_kernel(
@@ -479,7 +478,12 @@
             build((2 * g + part) * GROUP)
         return carry
 
-    lax.fori_loop(0, (base + 2 * GROUP - 1) // (2 * GROUP), step, 0)
+    def double_step(g, carry):
+        return step(2 * g + 1, step(2 * g, carry))
+
+    steps = (base + 2 * GROUP - 1) // (2 * GROUP)
+    lax.fori_loop(0, steps // 2, double_step, 0)
+    lax.fori_loop(steps - steps % 2, steps, step, 0)
 
 
 def finish_grid(rows, cols, acc, beside, grid):

time: 78.3 us -> 77 us (0.983)
  starting transfers between devices: 44.2 us -> 42.7 us
    ppermute x6, starting transfers between devices: 8.11 us -> 7.11 us  [swap_both(): lax.ppermute(first, axis, pairs_a)]
where the time goes in v4:
time: 77 us; the launch traced here: 76.3 us
  starting transfers between devices  42.7 us (55%)
  waiting for transfers between devices  20.3 us (26%)
  Pallas kernels  12.4 us (16%)
  between operations  0.87 us (1%)
    ppermute x6, starting transfers between devices, swap_both(): lax.ppermute(second, axis, pairs_b)  23.3 us
    pallas_call x10, Pallas kernels, run(): call(*[pltpu.with_memory_space_constraint(x, pltpu.HBM if i in hbm_in els...  12.4 us
    ppermute x6, waiting for transfers between devices, swap_both(): lax.ppermute(second, axis, pairs_b)  10.9 us
    ppermute x6, starting transfers between devices, swap_both(): lax.ppermute(first, axis, pairs_a)  7.11 us
    ppermute x8, waiting for transfers between devices, xor_permute(): lax.ppermute(value, axis, [(i, i ^ bit) for i in range(lax.axis_size(axis...  6.91 us
    ppermute x8, starting transfers between devices, xor_permute(): lax.ppermute(value, axis, [(i, i ^ bit) for i in range(lax.axis_size(axis...  5.84 us
    ppermute x1, starting transfers between devices, body(): below = lax.ppermute(below, 'rows', [(i, i + 1) for i in range(n_rows - 1)])  4.51 us
    ppermute x1, waiting for transfers between devices, body(): lax.ppermute(beside, 'cols', [(i, i + 1) for i in range(n_cols - 1)])  2.42 us
  transfers between devices with their start and end apart: 22, of which 12 were waited for; matrix products, arithmetic and copies ran while one was open for 0% of the time, Pallas kernels for 3%

profile of v4, /device:TPU:11, one launch (start us, length us, event | category | flops | bytes accessed | tf_op | source)
XLA Modules:
  0.0 76.3 jit_solution(15742264626283553515)
XLA Ops:
  0.6 1.2 %shard_map.86 = (f32[128,512]{1,0:T(8,128)S(1)}, f32[128,512]{1,0:T(8,128)S(1)}, f32[32,128]{1,0:T(8,128)S(1)}, s32[32,128]{1,0:T(8,128)S(1)}, f32[2,4096]{1,0:T...) custom-call(f32[128,512]{1,0:T(8,128)} %refs_0_.1, f32[128,512]{1,0:T(8,128)} %refs_1_.1, ...), custom_call_target="tpu_custom_call" | custom-call | tf_op jit(solution)/shard_map/pallas_call | solution.py:51
  1.8 0.7 collective-permute-start
  2.6 3.0 %collective-permute-start.1 = (f32[16,512]{1,0:T(8,128)S(1)}, f32[16,512]{1,0:T(8,128)S(1)}, u32[]{:S(2)}, u32[]{:S(2)}) collective-permute-start(f32[16,512]{1,0:T(8,128)S(1)} %get-tuple-element.49), channel_id=1, source_target_pairs={{4,8},{8,4},{12,16},{16,12},{20,24},{24,20},{5,9},{9,5},{13,17},{1... | collective-permute-start | bytes 98312 | tf_op jit(solution)/shard_map/ppermute | solution.py:26
  5.6 3.1 %collective-permute-done.1.b_ref = f32[16,512]{1,0:T(8,128)S(1)} collective-permute-done((f32[16,512]{1,0:T(8,128)S(1)}, f32[16,512]{1,0:T(8,128)S(1)}, u32[]{:S(2)}, u32[]{:S(2)}) %collective-permute-start.1) | collective-permute-done | bytes 32800 | tf_op jit(solution)/shard_map/ppermute | solution.py:26
  8.7 0.0 collective-permute-done.a_ref
  8.7 0.2 shard_map.87
  8.9 0.2 collective-permute-start.2
  9.1 4.3 %collective-permute-start.3 = (f32[16,256]{1,0:T(8,128)S(1)}, f32[16,256]{1,0:T(8,128)S(1)}, u32[]{:S(2)}, u32[]{:S(2)}) collective-permute-start(f32[16,256]{1,0:T(8,128)S(1)} %get-tuple-element.53), channel_id=1, source_target_pairs={{1,2},{2,1},{5,6},{6,5},{9,10},{10,9},{13,14},{14,13},{17,18},{18,... | collective-permute-start | bytes 49160 | tf_op jit(solution)/shard_map/ppermute | solution.py:26
  13.4 1.1 %collective-permute-done.3.refs_3_ = f32[16,256]{1,0:T(8,128)S(1)} collective-permute-done((f32[16,256]{1,0:T(8,128)S(1)}, f32[16,256]{1,0:T(8,128)S(1)}, u32[]{:S(2)}, u32[]{:S(2)}) %collective-permute-start.3) | collective-permute-done | bytes 16416 | tf_op jit(solution)/shard_map/ppermute | solution.py:26
  14.5 3.7 %shard_map.88 = (f32[104,128]{1,0:T(8,128)S(1)}, f32[104,128]{1,0:T(8,128)S(1)}, f32[104,128]{1,0:T(8,128)S(1)}, f32[104,128]{1,0:T(8,128)S(1)}, f32[160,640]{1,0:T(8,128)S(1)}, /*index=5*/f32[160,640]{1,0:T(8,128)S(1)}) custom-call(f32[160,640]{1,0:T(8,128)S(1)} %get-tuple-element.50.refs_0_, f32[160,640]{1,0:T(8,128)S(1)} %get-tuple-element.51.refs_1_, ...), custom_call_target="tpu_custom_call" | custom-call | tf_op jit(solution)/shard_map/pallas_call | solution.py:51
  18.3 1.7 %collective-permute-start.4 = (f32[104,128]{1,0:T(8,128)S(1)}, f32[104,128]{1,0:T(8,128)S(1)}, u32[]{:S(2)}, u32[]{:S(2)}) collective-permute-start(f32[104,128]{1,0:T(8,128)S(1)} %get-tuple-element.62), channel_id=1, source_target_pairs={{0,3},{1,2},{2,1},{3,0},{4,7},{5,6},{6,5},{7,4},{8,11},{9,10},{10,... | collective-permute-start | bytes 159752 | tf_op jit(solution)/shard_map/ppermute | solution.py:30
  20.0 0.0 collective-permute-start.5
  20.0 1.3 %collective-permute-start.6 = (f32[104,128]{1,0:T(8,128)S(1)}, f32[104,128]{1,0:T(8,128)S(1)}, u32[]{:S(2)}, u32[]{:S(2)}) collective-permute-start(f32[104,128]{1,0:T(8,128)S(1)} %get-tuple-element.64), channel_id=1, source_target_pairs={{0,1},{1,0},{2,3},{3,2},{4,5},{5,4},{6,7},{7,6},{8,9},{9,8},{10,11... | collective-permute-start | bytes 159752 | tf_op jit(solution)/shard_map/ppermute | solution.py:30
  21.3 0.2 collective-permute-done.4.refs_1_
  21.5 2.4 %collective-permute-done.5.refs_2_ = f32[104,128]{1,0:T(8,128)S(1)} collective-permute-done((f32[104,128]{1,0:T(8,128)S(1)}, f32[104,128]{1,0:T(8,128)S(1)}, u32[]{:S(2)}, u32[]{:S(2)}) %collective-permute-start.5) | collective-permute-done | bytes 53280 | tf_op jit(solution)/shard_map/ppermute | solution.py:30
  23.9 0.0 collective-permute-done.6.refs_3_
  23.9 1.9 %collective-permute-start.7 = (f32[128,128]{1,0:T(8,128)S(1)}, f32[128,128]{1,0:T(8,128)S(1)}, u32[]{:S(2)}, u32[]{:S(2)}) collective-permute-start(f32[128,128]{1,0:T(8,128)S(1)} %pad_maximum_fusion), channel_id=1, source_target_pairs={{0,4},{4,0},{8,12},{12,8},{16,20},{20,16},{24,28},{28,24},{1,5},{5... | collective-permute-start | bytes 196616 | tf_op jit(solution)/shard_map/ppermute | solution.py:26
  25.8 3.9 %collective-permute-start.8 = (f32[128,128]{1,0:T(8,128)S(1)}, f32[128,128]{1,0:T(8,128)S(1)}, u32[]{:S(2)}, u32[]{:S(2)}) collective-permute-start(f32[128,128]{1,0:T(8,128)S(1)} %pad_maximum_fusion.1), channel_id=1, source_target_pairs={{4,8},{8,4},{12,16},{16,12},{20,24},{24,20},{5,9},{9,5},{13,17},{1... | collective-permute-start | bytes 196616 | tf_op jit(solution)/shard_map/ppermute | solution.py:26
  29.8 0.1 collective-permute-start.9
  29.9 0.7 shard_map.89
  30.6 0.0 collective-permute-done.7.refs_0_
  30.6 2.4 %collective-permute-done.8.refs_1_ = f32[128,128]{1,0:T(8,128)S(1)} collective-permute-done((f32[128,128]{1,0:T(8,128)S(1)}, f32[128,128]{1,0:T(8,128)S(1)}, u32[]{:S(2)}, u32[]{:S(2)}) %collective-permute-start.8) | collective-permute-done | bytes 65568 | tf_op jit(solution)/shard_map/ppermute | solution.py:26
  33.0 0.5 shard_map.90
  33.5 0.8 %collective-permute-start.10 = (f32[8,640]{1,0:T(8,128)S(1)}, f32[8,640]{1,0:T(8,128)S(1)}, u32[]{:S(2)}, u32[]{:S(2)}) collective-permute-start(f32[8,640]{1,0:T(8,128)S(1)} %get-tuple-element.70), channel_id=1, source_target_pairs={{0,4},{4,0},{8,12},{12,8},{16,20},{20,16},{24,28},{28,24},{1,5},{5... | collective-permute-start | bytes 61448 | tf_op jit(solution)/shard_map/ppermute | solution.py:26
  34.3 4.3 %collective-permute-start.11 = (f32[8,640]{1,0:T(8,128)S(1)}, f32[8,640]{1,0:T(8,128)S(1)}, u32[]{:S(2)}, u32[]{:S(2)}) collective-permute-start(f32[8,640]{1,0:T(8,128)S(1)} %get-tuple-element.71), channel_id=1, source_target_pairs={{4,8},{8,4},{12,16},{16,12},{20,24},{24,20},{5,9},{9,5},{13,17},{1... | collective-permute-start | bytes 61448 | tf_op jit(solution)/shard_map/ppermute | solution.py:26
  38.6 0.0 collective-permute-done.10.a_ref
  38.6 1.7 %collective-permute-done.11.b_ref = f32[8,640]{1,0:T(8,128)S(1)} collective-permute-done((f32[8,640]{1,0:T(8,128)S(1)}, f32[8,640]{1,0:T(8,128)S(1)}, u32[]{:S(2)}, u32[]{:S(2)}) %collective-permute-start.11) | collective-permute-done | bytes 20512 | tf_op jit(solution)/shard_map/ppermute | solution.py:26
  40.3 0.1 shard_map.91
  40.5 0.9 %collective-permute-start.12 = (f32[16,256]{1,0:T(8,128)S(1)}, f32[16,256]{1,0:T(8,128)S(1)}, u32[]{:S(2)}, u32[]{:S(2)}) collective-permute-start(f32[16,256]{1,0:T(8,128)S(1)} %get-tuple-element.73), channel_id=1, source_target_pairs={{0,1},{1,0},{2,3},{3,2},{4,5},{5,4},{6,7},{7,6},{8,9},{9,8},{10,11... | collective-permute-start | bytes 49160 | tf_op jit(solution)/shard_map/ppermute | solution.py:26
  41.4 5.0 %collective-permute-start.13 = (f32[16,256]{1,0:T(8,128)S(1)}, f32[16,256]{1,0:T(8,128)S(1)}, u32[]{:S(2)}, u32[]{:S(2)}) collective-permute-start(f32[16,256]{1,0:T(8,128)S(1)} %get-tuple-element.74), channel_id=1, source_target_pairs={{1,2},{2,1},{5,6},{6,5},{9,10},{10,9},{13,14},{14,13},{17,18},{18,... | collective-permute-start | bytes 49160 | tf_op jit(solution)/shard_map/ppermute | solution.py:26
  46.5 0.1 collective-permute-start.14
  46.5 2.4 %collective-permute-done.14.refs_6_ = f32[8,128]{1,0:T(8,128)S(1)} collective-permute-done((f32[8,128]{1,0:T(8,128)S(1)}, f32[8,128]{1,0:T(8,128)S(1)}, u32[]{:S(2)}, u32[]{:S(2)}) %collective-permute-start.14) | collective-permute-done | bytes 4128 | tf_op jit(solution)/shard_map/ppermute | solution.py:30
  49.0 3.8 %shard_map.92 = (f32[56,128]{1,0:T(8,128)S(1)}, f32[56,128]{1,0:T(8,128)S(1)}, f32[56,128]{1,0:T(8,128)S(1)}, f32[56,128]{1,0:T(8,128)S(1)}, f32[128,512]{1,0:T(...) custom-call(f32[160,640]{1,0:T(8,128)S(1)} %get-tuple-element.59.refs_0_, ...), custom_call_target="tpu_custom_call" | custom-call | tf_op jit(solution)/shard_map/pallas_call | solution.py:51
  52.8 0.1 collective-permute-start.15
  52.9 0.1 collective-permute-start.16
  52.9 2.6 %collective-permute-start.17 = (f32[56,128]{1,0:T(8,128)S(1)}, f32[56,128]{1,0:T(8,128)S(1)}, u32[]{:S(2)}, u32[]{:S(2)}) collective-permute-start(f32[56,128]{1,0:T(8,128)S(1)} %get-tuple-element.80), channel_id=1, source_target_pairs={{0,1},{1,0},{2,3},{3,2},{4,5},{5,4},{6,7},{7,6},{8,9},{9,8},{10,11... | collective-permute-start | bytes 86024 | tf_op jit(solution)/shard_map/ppermute | solution.py:30
  55.5 0.1 collective-permute-done.15.refs_1_
  55.6 1.0 %collective-permute-done.16.refs_2_ = f32[56,128]{1,0:T(8,128)S(1)} collective-permute-done((f32[56,128]{1,0:T(8,128)S(1)}, f32[56,128]{1,0:T(8,128)S(1)}, u32[]{:S(2)}, u32[]{:S(2)}) %collective-permute-start.16) | collective-permute-done | bytes 28704 | tf_op jit(solution)/shard_map/ppermute | solution.py:30
  56.6 0.8 %collective-permute-done.17.refs_3_ = f32[56,128]{1,0:T(8,128)S(1)} collective-permute-done((f32[56,128]{1,0:T(8,128)S(1)}, f32[56,128]{1,0:T(8,128)S(1)}, u32[]{:S(2)}, u32[]{:S(2)}) %collective-permute-start.17) | collective-permute-done | bytes 28704 | tf_op jit(solution)/shard_map/ppermute | solution.py:30
  57.4 2.5 %collective-permute-start.18 = (f32[72,128]{1,0:T(8,128)S(1)}, f32[72,128]{1,0:T(8,128)S(1)}, u32[]{:S(2)}, u32[]{:S(2)}) collective-permute-start(f32[72,128]{1,0:T(8,128)S(1)} %constant_dynamic-update-slice_fusion), channel_id=1, source_target_pairs={{0,4},{4,0},{8,12},{12,8},{16,20},{20,16},{24,28},{28,24},{1,5},{5... | collective-permute-start | bytes 110600 | tf_op jit(solution)/shard_map/ppermute | solution.py:26
  59.9 2.7 %collective-permute-start.19 = (f32[72,128]{1,0:T(8,128)S(1)}, f32[72,128]{1,0:T(8,128)S(1)}, u32[]{:S(2)}, u32[]{:S(2)}) collective-permute-start(f32[72,128]{1,0:T(8,128)S(1)} %get-tuple-element.90), channel_id=1, source_target_pairs={{4,8},{8,4},{12,16},{16,12},{20,24},{24,20},{5,9},{9,5},{13,17},{1... | collective-permute-start | bytes 110600 | tf_op jit(solution)/shard_map/ppermute | solution.py:26
  62.6 0.7 shard_map.93
  63.4 2.7 %collective-permute-done.19.refs_1_ = f32[72,128]{1,0:T(8,128)S(1)} collective-permute-done((f32[72,128]{1,0:T(8,128)S(1)}, f32[72,128]{1,0:T(8,128)S(1)}, u32[]{:S(2)}, u32[]{:S(2)}) %collective-permute-start.19) | collective-permute-done | bytes 36896 | tf_op jit(solution)/shard_map/ppermute | solution.py:26
  66.0 0.6 shard_map.94
  66.6 4.5 %collective-permute-start.20 = (f32[8,512]{1,0:T(8,128)S(1)}, f32[8,512]{1,0:T(8,128)S(1)}, u32[]{:S(2)}, u32[]{:S(2)}) collective-permute-start(f32[8,512]{1,0:T(8,128)S(1)} %get-tuple-element.87), channel_id=1, source_target_pairs={{0,4},{4,8},{8,12},{12,16},{16,20},{20,24},{24,28},{1,5},{5,9},{9,... | collective-permute-start | bytes 49160 | tf_op jit(solution)/shard_map/ppermute | solution.py:778
  71.1 1.9 %collective-permute-start.21 = (f32[8,128]{1,0:T(8,128)S(1)}, f32[8,128]{1,0:T(8,128)S(1)}, u32[]{:S(2)}, u32[]{:S(2)}) collective-permute-start(f32[8,128]{1,0:T(8,128)S(1)} %get-tuple-element.88), channel_id=1, source_target_pairs={{0,1},{1,2},{2,3},{4,5},{5,6},{6,7},{8,9},{9,10},{10,11},{12,13},{... | collective-permute-start | bytes 12296 | tf_op jit(solution)/shard_map/ppermute | solution.py:779
  73.1 2.4 %collective-permute-done.21.col_in = f32[8,128]{1,0:T(8,128)S(1)} collective-permute-done((f32[8,128]{1,0:T(8,128)S(1)}, f32[8,128]{1,0:T(8,128)S(1)}, u32[]{:S(2)}, u32[]{:S(2)}) %collective-permute-start.21) | collective-permute-done | bytes 4128 | tf_op jit(solution)/shard_map/ppermute | solution.py:779
  75.5 0.8 %shard_map.95 = f32[128,512]{1,0:T(8,128)} custom-call(f32[136,640]{1,0:T(8,128)S(1)} %get-tuple-element.85.g_ref, f32[128,512]{1,0:T(8,128)S(1)} %get-tuple-element.86.m_ref, f32[8,512]{1,0:T(8,128)S(1)} %collective-permute-done.20.row_in, f32[8,128]{1,0:T(8,128)S(1)} %collective-permute-done.21.col_in, f32[8,128]{1,0:T(8,128)S(1)} %get-tuple-element.89.total_ref), custom_call_target="tpu_custom_call" | custom-call | tf_op jit(solution)/shard_map/pallas_call | solution.py:51
  (20 shorter events, 0.1 us)
Async XLA Ops:
  1.8 6.9 %collective-permute-start = (f32[24,512]{1,0:T(8,128)S(1)}, f32[24,512]{1,0:T(8,128)S(1)}, u32[]{:S(2)}, u32[]{:S(2)}) collective-permute-start(f32[24,512]{1,0:T(8,128)S(1)} %get-tuple-element.48.s_ref), channel_id=1, source_target_pairs={{0,4},{4,0},{8,12},{12,8},{16,20},{20,16},{24,28},{28,24},{1,5},{5... | collective-permute-start | bytes 147464 | tf_op jit(solution)/shard_map/ppermute | solution.py:26
  2.6 6.1 %collective-permute-start.1 = (f32[16,512]{1,0:T(8,128)S(1)}, f32[16,512]{1,0:T(8,128)S(1)}, u32[]{:S(2)}, u32[]{:S(2)}) collective-permute-start(f32[16,512]{1,0:T(8,128)S(1)} %get-tuple-element.49), channel_id=1, source_target_pairs={{4,8},{8,4},{12,16},{16,12},{20,24},{24,20},{5,9},{9,5},{13,17},{1... | collective-permute-start | bytes 98312 | tf_op jit(solution)/shard_map/ppermute | solution.py:26
  8.9 4.6 %collective-permute-start.2 = (f32[16,256]{1,0:T(8,128)S(1)}, f32[16,256]{1,0:T(8,128)S(1)}, u32[]{:S(2)}, u32[]{:S(2)}) collective-permute-start(f32[16,256]{1,0:T(8,128)S(1)} %get-tuple-element.52), channel_id=1, source_target_pairs={{0,1},{1,0},{2,3},{3,2},{4,5},{5,4},{6,7},{7,6},{8,9},{9,8},{10,11... | collective-permute-start | bytes 49160 | tf_op jit(solution)/shard_map/ppermute | solution.py:26
  9.1 5.4 %collective-permute-start.3 = (f32[16,256]{1,0:T(8,128)S(1)}, f32[16,256]{1,0:T(8,128)S(1)}, u32[]{:S(2)}, u32[]{:S(2)}) collective-permute-start(f32[16,256]{1,0:T(8,128)S(1)} %get-tuple-element.53), channel_id=1, source_target_pairs={{1,2},{2,1},{5,6},{6,5},{9,10},{10,9},{13,14},{14,13},{17,18},{18,... | collective-permute-start | bytes 49160 | tf_op jit(solution)/shard_map/ppermute | solution.py:26
  18.3 3.2 %collective-permute-start.4 = (f32[104,128]{1,0:T(8,128)S(1)}, f32[104,128]{1,0:T(8,128)S(1)}, u32[]{:S(2)}, u32[]{:S(2)}) collective-permute-start(f32[104,128]{1,0:T(8,128)S(1)} %get-tuple-element.62), channel_id=1, source_target_pairs={{0,3},{1,2},{2,1},{3,0},{4,7},{5,6},{6,5},{7,4},{8,11},{9,10},{10,... | collective-permute-start | bytes 159752 | tf_op jit(solution)/shard_map/ppermute | solution.py:30
  20.0 3.9 %collective-permute-start.5 = (f32[104,128]{1,0:T(8,128)S(1)}, f32[104,128]{1,0:T(8,128)S(1)}, u32[]{:S(2)}, u32[]{:S(2)}) collective-permute-start(f32[104,128]{1,0:T(8,128)S(1)} %get-tuple-element.63), channel_id=1, source_target_pairs={{0,2},{1,3},{2,0},{3,1},{4,6},{5,7},{6,4},{7,5},{8,10},{9,11},{10,... | collective-permute-start | bytes 159752 | tf_op jit(solution)/shard_map/ppermute | solution.py:30
  20.0 3.9 %collective-permute-start.6 = (f32[104,128]{1,0:T(8,128)S(1)}, f32[104,128]{1,0:T(8,128)S(1)}, u32[]{:S(2)}, u32[]{:S(2)}) collective-permute-start(f32[104,128]{1,0:T(8,128)S(1)} %get-tuple-element.64), channel_id=1, source_target_pairs={{0,1},{1,0},{2,3},{3,2},{4,5},{5,4},{6,7},{7,6},{8,9},{9,8},{10,11... | collective-permute-start | bytes 159752 | tf_op jit(solution)/shard_map/ppermute | solution.py:30
  23.9 6.7 %collective-permute-start.7 = (f32[128,128]{1,0:T(8,128)S(1)}, f32[128,128]{1,0:T(8,128)S(1)}, u32[]{:S(2)}, u32[]{:S(2)}) collective-permute-start(f32[128,128]{1,0:T(8,128)S(1)} %pad_maximum_fusion), channel_id=1, source_target_pairs={{0,4},{4,0},{8,12},{12,8},{16,20},{20,16},{24,28},{28,24},{1,5},{5... | collective-permute-start | bytes 196616 | tf_op jit(solution)/shard_map/ppermute | solution.py:26
  25.8 7.1 %collective-permute-start.8 = (f32[128,128]{1,0:T(8,128)S(1)}, f32[128,128]{1,0:T(8,128)S(1)}, u32[]{:S(2)}, u32[]{:S(2)}) collective-permute-start(f32[128,128]{1,0:T(8,128)S(1)} %pad_maximum_fusion.1), channel_id=1, source_target_pairs={{4,8},{8,4},{12,16},{16,12},{20,24},{24,20},{5,9},{9,5},{13,17},{1... | collective-permute-start | bytes 196616 | tf_op jit(solution)/shard_map/ppermute | solution.py:26
  29.8 3.7 %collective-permute-start.9 = (f32[8,128]{1,0:T(8,128)S(1)}, f32[8,128]{1,0:T(8,128)S(1)}, u32[]{:S(2)}, u32[]{:S(2)}) collective-permute-start(f32[8,128]{1,0:T(8,128)S(1)} %slice_add_fusion.3), channel_id=1, source_target_pairs={{0,8},{4,12},{8,0},{12,4},{16,24},{20,28},{24,16},{28,20},{1,9},{5... | collective-permute-start | bytes 12296 | tf_op jit(solution)/shard_map/ppermute | solution.py:30
  33.5 5.1 %collective-permute-start.10 = (f32[8,640]{1,0:T(8,128)S(1)}, f32[8,640]{1,0:T(8,128)S(1)}, u32[]{:S(2)}, u32[]{:S(2)}) collective-permute-start(f32[8,640]{1,0:T(8,128)S(1)} %get-tuple-element.70), channel_id=1, source_target_pairs={{0,4},{4,0},{8,12},{12,8},{16,20},{20,16},{24,28},{28,24},{1,5},{5... | collective-permute-start | bytes 61448 | tf_op jit(solution)/shard_map/ppermute | solution.py:26
  34.3 6.0 %collective-permute-start.11 = (f32[8,640]{1,0:T(8,128)S(1)}, f32[8,640]{1,0:T(8,128)S(1)}, u32[]{:S(2)}, u32[]{:S(2)}) collective-permute-start(f32[8,640]{1,0:T(8,128)S(1)} %get-tuple-element.71), channel_id=1, source_target_pairs={{4,8},{8,4},{12,16},{16,12},{20,24},{24,20},{5,9},{9,5},{13,17},{1... | collective-permute-start | bytes 61448 | tf_op jit(solution)/shard_map/ppermute | solution.py:26
  40.5 8.5 %collective-permute-start.12 = (f32[16,256]{1,0:T(8,128)S(1)}, f32[16,256]{1,0:T(8,128)S(1)}, u32[]{:S(2)}, u32[]{:S(2)}) collective-permute-start(f32[16,256]{1,0:T(8,128)S(1)} %get-tuple-element.73), channel_id=1, source_target_pairs={{0,1},{1,0},{2,3},{3,2},{4,5},{5,4},{6,7},{7,6},{8,9},{9,8},{10,11... | collective-permute-start | bytes 49160 | tf_op jit(solution)/shard_map/ppermute | solution.py:26
  41.4 7.6 %collective-permute-start.13 = (f32[16,256]{1,0:T(8,128)S(1)}, f32[16,256]{1,0:T(8,128)S(1)}, u32[]{:S(2)}, u32[]{:S(2)}) collective-permute-start(f32[16,256]{1,0:T(8,128)S(1)} %get-tuple-element.74), channel_id=1, source_target_pairs={{1,2},{2,1},{5,6},{6,5},{9,10},{10,9},{13,14},{14,13},{17,18},{18,... | collective-permute-start | bytes 49160 | tf_op jit(solution)/shard_map/ppermute | solution.py:26
  46.5 2.5 %collective-permute-start.14 = (f32[8,128]{1,0:T(8,128)S(1)}, f32[8,128]{1,0:T(8,128)S(1)}, u32[]{:S(2)}, u32[]{:S(2)}) collective-permute-start(f32[8,128]{1,0:T(8,128)S(1)} %add.24.refs_5_), channel_id=1, source_target_pairs={{0,16},{4,20},{8,24},{12,28},{16,0},{20,4},{24,8},{28,12},{1,17},{... | collective-permute-start | bytes 12296 | tf_op jit(solution)/shard_map/ppermute | solution.py:30
  52.8 2.8 %collective-permute-start.15 = (f32[56,128]{1,0:T(8,128)S(1)}, f32[56,128]{1,0:T(8,128)S(1)}, u32[]{:S(2)}, u32[]{:S(2)}) collective-permute-start(f32[56,128]{1,0:T(8,128)S(1)} %get-tuple-element.78), channel_id=1, source_target_pairs={{0,3},{1,2},{2,1},{3,0},{4,7},{5,6},{6,5},{7,4},{8,11},{9,10},{10,... | collective-permute-start | bytes 86024 | tf_op jit(solution)/shard_map/ppermute | solution.py:30
  52.9 3.7 %collective-permute-start.16 = (f32[56,128]{1,0:T(8,128)S(1)}, f32[56,128]{1,0:T(8,128)S(1)}, u32[]{:S(2)}, u32[]{:S(2)}) collective-permute-start(f32[56,128]{1,0:T(8,128)S(1)} %get-tuple-element.79), channel_id=1, source_target_pairs={{0,2},{1,3},{2,0},{3,1},{4,6},{5,7},{6,4},{7,5},{8,10},{9,11},{10,... | collective-permute-start | bytes 86024 | tf_op jit(solution)/shard_map/ppermute | solution.py:30
  52.9 4.4 %collective-permute-start.17 = (f32[56,128]{1,0:T(8,128)S(1)}, f32[56,128]{1,0:T(8,128)S(1)}, u32[]{:S(2)}, u32[]{:S(2)}) collective-permute-start(f32[56,128]{1,0:T(8,128)S(1)} %get-tuple-element.80), channel_id=1, source_target_pairs={{0,1},{1,0},{2,3},{3,2},{4,5},{5,4},{6,7},{7,6},{8,9},{9,8},{10,11... | collective-permute-start | bytes 86024 | tf_op jit(solution)/shard_map/ppermute | solution.py:30
  57.4 6.0 %collective-permute-start.18 = (f32[72,128]{1,0:T(8,128)S(1)}, f32[72,128]{1,0:T(8,128)S(1)}, u32[]{:S(2)}, u32[]{:S(2)}) collective-permute-start(f32[72,128]{1,0:T(8,128)S(1)} %constant_dynamic-update-slice_fusion), channel_id=1, source_target_pairs={{0,4},{4,0},{8,12},{12,8},{16,20},{20,16},{24,28},{28,24},{1,5},{5... | collective-permute-start | bytes 110600 | tf_op jit(solution)/shard_map/ppermute | solution.py:26
  59.9 6.2 %collective-permute-start.19 = (f32[72,128]{1,0:T(8,128)S(1)}, f32[72,128]{1,0:T(8,128)S(1)}, u32[]{:S(2)}, u32[]{:S(2)}) collective-permute-start(f32[72,128]{1,0:T(8,128)S(1)} %get-tuple-element.90), channel_id=1, source_target_pairs={{4,8},{8,4},{12,16},{16,12},{20,24},{24,20},{5,9},{9,5},{13,17},{1... | collective-permute-start | bytes 110600 | tf_op jit(solution)/shard_map/ppermute | solution.py:26
  66.6 8.9 %collective-permute-start.20 = (f32[8,512]{1,0:T(8,128)S(1)}, f32[8,512]{1,0:T(8,128)S(1)}, u32[]{:S(2)}, u32[]{:S(2)}) collective-permute-start(f32[8,512]{1,0:T(8,128)S(1)} %get-tuple-element.87), channel_id=1, source_target_pairs={{0,4},{4,8},{8,12},{12,16},{16,20},{20,24},{24,28},{1,5},{5,9},{9,... | collective-permute-start | bytes 49160 | tf_op jit(solution)/shard_map/ppermute | solution.py:778
  71.1 4.4 %collective-permute-start.21 = (f32[8,128]{1,0:T(8,128)S(1)}, f32[8,128]{1,0:T(8,128)S(1)}, u32[]{:S(2)}, u32[]{:S(2)}) collective-permute-start(f32[8,128]{1,0:T(8,128)S(1)} %get-tuple-element.88), channel_id=1, source_target_pairs={{0,1},{1,2},{2,3},{4,5},{5,6},{6,7},{8,9},{9,10},{10,11},{12,13},{... | collective-permute-start | bytes 12296 | tf_op jit(solution)/shard_map/ppermute | solution.py:779
